TPU v7x, 128 devices: a whole 4x4x4 slice. The times are simulated.
128 devices in a mesh: dom: 2 (over core), gx: 8 (over z, y_hi), yz: 8 (over y_lo, x).
Axes of the slice: x: 4, y: 4 (y_hi: 2, y_lo: 2; y = y_hi * 2 + y_lo), z: 4, core: 2. Of those that a mesh axis runs over, the one named last changes fastest.
Arguments:
- field_state: float32 [2, 8, 128, 128, 128], P('dom', None, 'gx', 'yz'), as said below
- shell_owner: int32 [8, 8, 8], P('gx'), may hold values from 0 to 7, as said below
- block_sources: int32 [8, 8, 4, 4], P('gx', 'yz'), may hold values from -1 to 15, as said below
- block_targets: int32 [8, 8, 4], P('gx', 'yz'), may hold values from -1 to 63, as said below
- interp_weights: bfloat16 [8, 8, 4, 4, 512, 512], P('gx', 'yz'), as said below
Outputs:
- new_state: float32 [2, 8, 128, 128, 128], P('dom', None, 'gx', 'yz')
Inputs may be any that keep to these rules, and one draw needn't show every extreme that they name: `shell_owner`: entry [g, t, b] is the yz index of the heliosphere device, at the same gx index g, that owns shell block b of the corona device (g, t). No corona device gives more than 2 of its blocks to one owner, and in every gx index some owner receives exactly 2 blocks from each corona device of that gx index. `block_sources`: the live entries of device (g, y) come first in slot order and are the positions 0 to R - 1 of its owned list, each exactly once, R being the number of shell blocks it owns; the rest are -1. `block_targets`: live slots of one device name distinct local blocks; a slot is -1 exactly when all its sources are -1. `field_state`: each cell holds conserved variables of a state with positive density and pressure. `interp_weights`: for every target cell the entries over all 4 source blocks and their cells sum to less than one.
All inputs are finite; a program needn't handle non-finite values.
Results may differ from a plain program's by a relative error of at most 0.002.
Values may be sent and summed in bfloat16 or wider, within the bound.
A program may use at most 64 MiB of HBM per device.

v0:
```python
import jax
import jax.numpy as jnp
from jax import lax
from jax.sharding import PartitionSpec as P

BLK = 8
SR = 2
CAP = 2


HEAT_RATIO = 5.0 / 3.0
CORONA_RATIO = 0.04
HELIO_RATIO = 0.03


def shifted(block, axis, distance):
    devices = range(lax.axis_size(axis))
    route = [(i - distance, i) for i in devices if i - distance in devices]
    return lax.ppermute(block, axis, route)


def extended(cells, sides, width):
    for axis, dim in sides:
        count = lax.axis_size(axis)
        head = lax.slice_in_dim(cells, 0, width, axis=dim)
        tail = lax.slice_in_dim(cells, cells.shape[dim] - width, cells.shape[dim], axis=dim)
        cells = jnp.concatenate(
            [
                lax.ppermute(tail, axis, [(i, (i + 1) % count) for i in range(count)]),
                cells,
                lax.ppermute(head, axis, [((i + 1) % count, i) for i in range(count)]),
            ],
            axis=dim,
        )
    return cells


def direction_flux(grid_cells, direction):
    density = grid_cells[0]
    momentum = grid_cells[1:4]
    magnetic = grid_cells[4:7]
    energy = grid_cells[7]
    velocity = momentum / density
    field_sq = jnp.sum(magnetic * magnetic, axis=0)
    pressure = (HEAT_RATIO - 1.0) * (
        energy - 0.5 * jnp.sum(momentum * velocity, axis=0) - 0.5 * field_sq
    )
    total_pressure = pressure + 0.5 * field_sq
    normal_speed = velocity[direction]
    normal_field = magnetic[direction]
    velocity_dot = jnp.sum(velocity * magnetic, axis=0)
    flux_list = [momentum[direction]]
    for other in range(3):
        term = momentum[other] * normal_speed - magnetic[other] * normal_field
        if other == direction:
            term = term + total_pressure
        flux_list.append(term)
    for other in range(3):
        flux_list.append(normal_speed * magnetic[other] - normal_field * velocity[other])
    flux_list.append((energy + total_pressure) * normal_speed - normal_field * velocity_dot)
    wave_speed = jnp.abs(normal_speed) + jnp.sqrt((HEAT_RATIO * pressure + field_sq) / density)
    return (jnp.stack(flux_list), wave_speed)


def interface_change(padded_line, direction):
    phys_flux, wave_speed = direction_flux(padded_line, direction)
    array_dim = direction + 1
    cell_count = padded_line.shape[array_dim]
    low_cells = lax.slice_in_dim(padded_line, 0, cell_count - 1, axis=array_dim)
    high_cells = lax.slice_in_dim(padded_line, 1, cell_count, axis=array_dim)
    low_flux = lax.slice_in_dim(phys_flux, 0, cell_count - 1, axis=array_dim)
    high_flux = lax.slice_in_dim(phys_flux, 1, cell_count, axis=array_dim)
    low_speed = lax.slice_in_dim(wave_speed, 0, cell_count - 1, axis=direction)
    high_speed = lax.slice_in_dim(wave_speed, 1, cell_count, axis=direction)
    fastest = jnp.maximum(low_speed, high_speed)
    face_flux = 0.5 * (low_flux + high_flux) - 0.5 * fastest[None] * (high_cells - low_cells)
    upper_face = lax.slice_in_dim(face_flux, 1, cell_count - 1, axis=array_dim)
    lower_face = lax.slice_in_dim(face_flux, 0, cell_count - 2, axis=array_dim)
    return upper_face - lower_face


def advance(line_set, inner_cells, step_ratio):
    change = interface_change(line_set[0], 0) + interface_change(line_set[1], 1)
    change = change + interface_change(line_set[2], 2)
    return inner_cells - step_ratio * change


def edge_copy(padded_line, direction, fix_low, fix_high):
    array_dim = direction + 1
    cell_count = padded_line.shape[array_dim]
    first_layer = lax.slice_in_dim(padded_line, 0, 1, axis=array_dim)
    second_layer = lax.slice_in_dim(padded_line, 1, 2, axis=array_dim)
    before_last = lax.slice_in_dim(padded_line, cell_count - 2, cell_count - 1, axis=array_dim)
    last_layer = lax.slice_in_dim(padded_line, cell_count - 1, cell_count, axis=array_dim)
    middle = lax.slice_in_dim(padded_line, 1, cell_count - 1, axis=array_dim)
    first_layer = jnp.where(fix_low, second_layer, first_layer)
    last_layer = jnp.where(fix_high, before_last, last_layer)
    return jnp.concatenate([first_layer, middle, last_layer], axis=array_dim)


def local(field_state, shell_owner, block_sources, block_targets, interp_weights):
    grid_cells = field_state[0]
    ncomp, len_x, len_y, len_z = grid_cells.shape
    domain = lax.axis_index("dom")
    column = lax.axis_index("gx")
    yz_index = lax.axis_index("yz")
    gx_count = lax.axis_size("gx")
    yz_count = lax.axis_size("yz")
    per_y = len_y // BLK
    per_z = len_z // BLK
    volume = BLK * BLK * BLK
    shell_cells = grid_cells[:, :, :, len_z - SR * BLK :]
    shell_cells = shell_cells.reshape(ncomp, len_x // BLK, BLK, per_y, BLK, SR, BLK)
    shell_cells = (
        shell_cells.transpose(1, 3, 5, 0, 2, 4, 6).reshape(-1, ncomp * volume).astype(jnp.bfloat16)
    )
    count_here = shell_cells.shape[0]
    owners = shell_owner[0].reshape(-1)
    own_owner = lax.dynamic_slice_in_dim(owners, yz_index * count_here, count_here)
    own_spot = yz_index * count_here + jnp.arange(count_here, dtype=jnp.int32)
    all_spots = jnp.arange(owners.shape[0], dtype=jnp.int32)
    same_owner = owners[None, :] == own_owner[:, None]
    rank_all = jnp.sum(
        (same_owner & (all_spots[None, :] < own_spot[:, None])).astype(jnp.int32), axis=1
    )
    index_here = jnp.arange(count_here, dtype=jnp.int32)
    local_same = own_owner[None, :] == own_owner[:, None]
    rank_local = jnp.sum(
        (local_same & (index_here[None, :] < index_here[:, None])).astype(jnp.int32), axis=1
    )
    slot_of = own_owner * CAP + rank_local
    slot_count = yz_count * CAP
    select = jnp.arange(slot_count, dtype=jnp.int32)[:, None] == slot_of[None, :]
    send_cells = jnp.dot(
        select.astype(jnp.bfloat16), shell_cells, preferred_element_type=jnp.float32
    )
    send_cells = send_cells.astype(jnp.bfloat16).reshape(yz_count, CAP, ncomp * volume)
    send_tags = jnp.sum(jnp.where(select, rank_all[None, :], 0), axis=1)
    send_tags = jnp.where(jnp.any(select, axis=1), send_tags, -1).reshape(yz_count, CAP)
    moved_pair = shifted((send_cells, send_tags), "dom", 1)
    got_cells, got_tags = (
        lax.all_to_all(moved_pair[0], "yz", split_axis=0, concat_axis=0, tiled=True),
        lax.all_to_all(moved_pair[1], "yz", split_axis=0, concat_axis=0, tiled=True),
    )
    got_cells = got_cells.reshape(slot_count, ncomp * volume)
    got_tags = got_tags.reshape(slot_count)
    wanted = block_sources[0, 0].reshape(-1)
    match_table = (wanted[:, None] == got_tags[None, :]) & (wanted[:, None] >= 0)
    picked = jnp.dot(
        match_table.astype(jnp.bfloat16), got_cells, preferred_element_type=jnp.float32
    )
    slots_here = block_targets.shape[2]
    picked = picked.astype(jnp.bfloat16).reshape(slots_here, -1, ncomp, volume)
    interp_blocks = jnp.einsum(
        "jkcs,jkst->jct", picked, interp_weights[0, 0], preferred_element_type=jnp.float32
    )

    def place_block(slot_number, grid_now):
        target_block = block_targets[0, 0, slot_number]
        live_slot = (target_block >= 0) & (domain == 1)
        block_spot = jnp.maximum(target_block, 0)
        block_x = block_spot // (per_y * per_z)
        block_y = block_spot // per_z % per_y
        block_z = block_spot % per_z
        corner_start = (jnp.int32(0), block_x * BLK, block_y * BLK, block_z * BLK)
        old_block = lax.dynamic_slice(grid_now, corner_start, (ncomp, BLK, BLK, BLK))
        new_block = lax.dynamic_index_in_dim(interp_blocks, slot_number, 0, keepdims=False)
        new_block = new_block.reshape(ncomp, BLK, BLK, BLK)
        return lax.dynamic_update_slice(
            grid_now, jnp.where(live_slot, new_block, old_block), corner_start
        )

    grid_cells = lax.fori_loop(0, slots_here, place_block, grid_cells)
    helio_side = domain == 1
    low_x = helio_side & (column == 0)
    high_x = helio_side & (column == gx_count - 1)
    low_y = yz_index == 0
    high_y = yz_index == yz_count - 1
    padded = extended(grid_cells, (("gx", 1), ("yz", 2)), 1)
    line_x = padded[:, :, 1:-1, :]
    line_y = padded[:, 1:-1, :, :]
    line_x = edge_copy(line_x, 0, low_x, high_x)
    line_y = edge_copy(line_y, 1, low_y, high_y)
    line_z = jnp.pad(grid_cells, ((0, 0), (0, 0), (0, 0), (1, 1)), mode="edge")
    step_ratio = jnp.where(domain == 0, CORONA_RATIO, HELIO_RATIO).astype(jnp.float32)
    updated = advance((line_x, line_y, line_z), grid_cells, step_ratio)
    return updated[None]


def solution(mesh):
    placed = (
        P("dom", None, "gx", "yz", None),
        P("gx", None, None),
        P("gx", "yz", None, None),
        P("gx", "yz", None),
        P("gx", "yz", None, None, None, None),
    )
    return jax.shard_map(
        local,
        mesh=mesh,
        in_specs=placed,
        out_specs=P("dom", None, "gx", "yz", None),
        check_vma=False,
    )
```

profile of v0, /device:TPU:54, one launch (start us, length us, event | category | flops | bytes accessed | tf_op | source)
XLA Modules:
  0.0 151.3 jit_solution(3214558605555499464)
XLA Ops:
  0.0 1.2 copy.54
  1.2 0.2 slice.623
  1.4 0.4 convert_element_type.26
  1.9 0.2 copy.22
  2.1 1.5 convert_element_type.28
  3.8 0.2 convert_reduce_fusion.1
  4.0 0.3 convolution_convert_fusion.1
  4.4 2.4 %collective-permute-start.1 = (bf16[8,2,4096]{2,1,0:T(2,128)(2,1)S(1)}, bf16[8,2,4096]{2,1,0:T(2,128)(2,1)}, u32[]{:S(2)}, u32[]{:S(2)}) collective-permute-start(bf16[8,2,4096]{2,1,0:T(2,128)(2,1)S(1)} %reshape.140), channel_id=1, source_target_pairs={{0,64},{1,65},{2,66},{3,67},{4,68},{5,69},{6,70},{7,71},{8,72},{9,... | collective-permute-start | bytes 393224 | tf_op jit(solution)/shard_map/ppermute | solution.py:19
  6.9 0.2 convert_reduce_fusion
  7.3 1.9 %collective-permute-start = (s32[8,2]{1,0:T(8,128)S(1)}, s32[8,2]{1,0:T(8,128)}, u32[]{:S(2)}, u32[]{:S(2)}) collective-permute-start(s32[8,2]{1,0:T(8,128)S(1)} %select_n.183), channel_id=1, source_target_pairs={{0,64},{1,65},{2,66},{3,67},{4,68},{5,69},{6,70},{7,71},{8,72},{9,... | collective-permute-start | bytes 200 | tf_op jit(solution)/shard_map/ppermute | solution.py:19
  9.2 0.3 collective-permute-done
  9.5 5.5 %all-to-all-start = ((s32[8,1,2]{2,1,0:T(1,128)}), s32[8,1,2]{2,1,0:T(1,128)S(1)}, u32[]{:S(2)}, u32[]{:S(2)}) async-start(s32[8,1,2]{2,1,0:T(1,128)} %bitcast.31), calls=%async_computation | async-start | bytes 8192 | tf_op jit(solution)/shard_map/all_to_all | solution.py:143
  15.0 4.1 %all-to-all-done = s32[8,1,2]{2,1,0:T(1,128)S(1)} async-done(((s32[8,1,2]{2,1,0:T(1,128)}), s32[8,1,2]{2,1,0:T(1,128)S(1)}, u32[]{:S(2)}, u32[]{:S(2)}) %all-to-all-start) | async-done | bytes 96 | tf_op jit(solution)/shard_map/all_to_all | solution.py:143
  19.1 5.3 %all-to-all-start.1 = ((bf16[8,2,4096]{2,1,0:T(2,128)(2,1)}), bf16[8,2,4096]{2,1,0:T(2,128)(2,1)S(1)}, u32[]{:S(2)}, u32[]{:S(2)}) async-start(bf16[8,2,4096]{2,1,0:T(2,128)(2,1)} %collective-permute-done.1), calls=%async_computation.1 | async-start | bytes 262144 | tf_op jit(solution)/shard_map/all_to_all | solution.py:142
  24.5 0.5 broadcast.135
  25.0 0.6 reduce.3
  25.6 3.5 %all-to-all-done.1 = bf16[8,2,4096]{2,1,0:T(2,128)(2,1)S(1)} async-done(((bf16[8,2,4096]{2,1,0:T(2,128)(2,1)}), bf16[8,2,4096]{2,1,0:T(2,128)(2,1)S(1)}, u32[]{:S(2)}, u32[]{:S(2)}) %all-to-all-start.1) | async-done | bytes 131104 | tf_op jit(solution)/shard_map/all_to_all | solution.py:142
  29.2 0.2 convolution_convert_fusion
  29.4 4.6 %fusion.8 = f32[4,8,512]{2,1,0:T(8,128)S(1)} fusion(bf16[4,4,8,512]{3,2,1,0:T(8,128)(2,1)S(1)} %bitcast.183, bf16[1,1,4,4,512,512]{5,4,3,2,1,0:T(8,128)(2,1)} %param.11), kind=kOutput, calls=%fused_computation.20 | convolution fusion | flops 67108864 | bytes 8585216 | tf_op jit(solution)/shard_map/jkcs,jkst->jct/dot_general | solution.py:154
  34.0 59.0 %while.16 = (s32[]{:T(128)}, f32[8,16,16,128]{3,2,1,0:T(8,128)S(1)}, s32[1,1,4]{2,1,0:T(1,128)S(1)}, pred[]{:T(512)}, f32[4,8,512]{2,1,0:T(8,128)S(1)}, /*index=...) while((s32[]{:T(128)}, ...), condition=%wide.region_5.6_spmd, body=%wide.region_4.5_spmd.sunk | while | flops 4142 | bytes 148101 | solution.py:173
  34.0 0.2 reshape.154
  34.2 0.7 fusion.90
  38.6 18.8 %dynamic_update_slice.12 = f32[8,16,16,128]{3,2,1,0:T(8,128)S(1)} dynamic-update-slice(f32[8,16,16,128]{3,2,1,0:T(8,128)S(1)} %get-tuple-element.271, f32[8,8,8,8]{3,2,1,0:T(8,128)S(1)} %dynamic-slice_select_fusion.2, s32[]{:T(128)} %constant.207.clone.1..sunk, s32[]{:T(128)S(6)} %select_n.217, s32[]{:T(128)S(6)} %select_n.220, s32[]{:T(128)S(6)} %select_n.222) | dynamic-update-slice | bytes 32772 | tf_op jit(solution)/shard_map/while/body/eval_jaxpr/dynamic_update_slice | solution.py:169
  57.5 0.7 fusion.90
  61.9 18.8 %dynamic_update_slice.12 = f32[8,16,16,128]{3,2,1,0:T(8,128)S(1)} dynamic-update-slice(f32[8,16,16,128]{3,2,1,0:T(8,128)S(1)} %get-tuple-element.271, f32[8,8,8,8]{3,2,1,0:T(8,128)S(1)} %dynamic-slice_select_fusion.2, s32[]{:T(128)} %constant.207.clone.1..sunk, s32[]{:T(128)S(6)} %select_n.217, s32[]{:T(128)S(6)} %select_n.220, s32[]{:T(128)S(6)} %select_n.222) | dynamic-update-slice | bytes 32772 | tf_op jit(solution)/shard_map/while/body/eval_jaxpr/dynamic_update_slice | solution.py:169
  80.9 0.7 fusion.90
  85.3 1.6 %dynamic_update_slice.12 = f32[8,16,16,128]{3,2,1,0:T(8,128)S(1)} dynamic-update-slice(f32[8,16,16,128]{3,2,1,0:T(8,128)S(1)} %get-tuple-element.271, f32[8,8,8,8]{3,2,1,0:T(8,128)S(1)} %dynamic-slice_select_fusion.2, s32[]{:T(128)} %constant.207.clone.1..sunk, s32[]{:T(128)S(6)} %select_n.217, s32[]{:T(128)S(6)} %select_n.220, s32[]{:T(128)S(6)} %select_n.222) | dynamic-update-slice | bytes 32772 | tf_op jit(solution)/shard_map/while/body/eval_jaxpr/dynamic_update_slice | solution.py:169
  87.1 0.7 fusion.90
  91.4 1.6 %dynamic_update_slice.12 = f32[8,16,16,128]{3,2,1,0:T(8,128)S(1)} dynamic-update-slice(f32[8,16,16,128]{3,2,1,0:T(8,128)S(1)} %get-tuple-element.271, f32[8,8,8,8]{3,2,1,0:T(8,128)S(1)} %dynamic-slice_select_fusion.2, s32[]{:T(128)} %constant.207.clone.1..sunk, s32[]{:T(128)S(6)} %select_n.217, s32[]{:T(128)S(6)} %select_n.220, s32[]{:T(128)S(6)} %select_n.222) | dynamic-update-slice | bytes 32772 | tf_op jit(solution)/shard_map/while/body/eval_jaxpr/dynamic_update_slice | solution.py:169
  93.0 0.3 fusion.85
  93.4 0.9 pad_maximum_fusion
  94.4 0.3 multiply_reduce_fusion
  95.0 0.2 add_dynamic-update-slice_fusion
  95.6 2.1 %collective-permute-start.2 = (f32[8,1,16,128]{3,2,1,0:T(8,128)S(1)}, f32[8,1,16,128]{3,2,1,0:T(8,128)S(1)}, u32[]{:S(2)}, u32[]{:S(2)}) collective-permute-start(f32[8,1,16,128]{3,2,1,0:T(8,128)S(1)} %get-tuple-element.213), channel_id=1, source_target_pairs={{0,8},{8,16},{16,24},{24,32},{32,40},{40,48},{48,56},{56,0},{1,9},... | collective-permute-start | bytes 196616 | tf_op jit(solution)/shard_map/ppermute | solution.py:29
  97.7 33.2 %collective-permute-start.3 = (f32[8,1,16,128]{3,2,1,0:T(8,128)S(1)}, f32[8,1,16,128]{3,2,1,0:T(8,128)S(1)}, u32[]{:S(2)}, u32[]{:S(2)}) collective-permute-start(f32[8,1,16,128]{3,2,1,0:T(8,128)S(1)} %get-tuple-element.212), channel_id=1, source_target_pairs={{8,0},{16,8},{24,16},{32,24},{40,32},{48,40},{56,48},{0,56},{9,1},... | collective-permute-start | bytes 196616 | tf_op jit(solution)/shard_map/ppermute | solution.py:31
  130.8 0.2 fusion.35
  131.0 1.2 fusion.3
  132.2 0.8 collective-permute-done.2
  133.1 4.8 %collective-permute-done.3 = f32[8,1,16,128]{3,2,1,0:T(8,128)S(1)} collective-permute-done((f32[8,1,16,128]{3,2,1,0:T(8,128)S(1)}, f32[8,1,16,128]{3,2,1,0:T(8,128)S(1)}, u32[]{:S(2)}, u32[]{:S(2)}) %collective-permute-start.3) | collective-permute-done | bytes 65568 | tf_op jit(solution)/shard_map/ppermute | solution.py:31
  138.0 3.5 %collective-permute-start.4 = (f32[8,18,1,128]{3,2,1,0:T(1,128)S(1)}, f32[8,18,1,128]{3,2,1,0:T(1,128)S(1)}, u32[]{:S(2)}, u32[]{:S(2)}) collective-permute-start(f32[8,18,1,128]{3,2,1,0:T(1,128)S(1)} %get-tuple-element.206), channel_id=1, source_target_pairs={{0,1},{1,2},{2,3},{3,4},{4,5},{5,6},{6,7},{7,0},{8,9},{9,10},{10,1... | collective-permute-start | bytes 221192 | tf_op jit(solution)/shard_map/ppermute | solution.py:29
  142.3 0.2 fusion.12
  142.5 1.0 collective-permute-done.4
  143.5 4.5 %collective-permute-done.5 = f32[8,18,1,128]{3,2,1,0:T(1,128)S(1)} collective-permute-done((f32[8,18,1,128]{3,2,1,0:T(1,128)S(1)}, f32[8,18,1,128]{3,2,1,0:T(1,128)S(1)}, u32[]{:S(2)}, u32[]{:S(2)}) %collective-permute-start.5) | collective-permute-done | bytes 73760 | tf_op jit(solution)/shard_map/ppermute | solution.py:31
  148.0 0.2 broadcast_select_fusion.1
  148.2 0.3 pad_maximum_fusion.1
  148.4 0.2 multiply_reduce_fusion.3
  149.3 0.6 fusion.6
  149.9 1.5 fusion.17
  (68 shorter events, 4.2 us)
Async XLA Ops:
  1.8 1.8 %copy-start.1 = (s32[1,8,8]{2,1,0:T(8,128)S(1)}, s32[1,8,8]{2,1,0:T(8,128)}, u32[]{:S(2)}) copy-start(s32[1,8,8]{2,1,0:T(8,128)} %param.8) | copy-start | bytes 772
  1.9 7.3 %copy-start.2 = (s32[1,1,4,4]{3,2,1,0:T(4,128)S(1)}, s32[1,1,4,4]{3,2,1,0:T(4,128)}, u32[]{:S(2)}) copy-start(s32[1,1,4,4]{3,2,1,0:T(4,128)} %param.9) | copy-start | bytes 196
  4.4 14.7 %collective-permute-start.1 = (bf16[8,2,4096]{2,1,0:T(2,128)(2,1)S(1)}, bf16[8,2,4096]{2,1,0:T(2,128)(2,1)}, u32[]{:S(2)}, u32[]{:S(2)}) collective-permute-start(bf16[8,2,4096]{2,1,0:T(2,128)(2,1)S(1)} %reshape.140), channel_id=1, source_target_pairs={{0,64},{1,65},{2,66},{3,67},{4,68},{5,69},{6,70},{7,71},{8,72},{9,... | collective-permute-start | bytes 393224 | tf_op jit(solution)/shard_map/ppermute | solution.py:19
  7.3 2.2 %collective-permute-start = (s32[8,2]{1,0:T(8,128)S(1)}, s32[8,2]{1,0:T(8,128)}, u32[]{:S(2)}, u32[]{:S(2)}) collective-permute-start(s32[8,2]{1,0:T(8,128)S(1)} %select_n.183), channel_id=1, source_target_pairs={{0,64},{1,65},{2,66},{3,67},{4,68},{5,69},{6,70},{7,71},{8,72},{9,... | collective-permute-start | bytes 200 | tf_op jit(solution)/shard_map/ppermute | solution.py:19
  9.5 9.6 %all-to-all-start = ((s32[8,1,2]{2,1,0:T(1,128)}), s32[8,1,2]{2,1,0:T(1,128)S(1)}, u32[]{:S(2)}, u32[]{:S(2)}) async-start(s32[8,1,2]{2,1,0:T(1,128)} %bitcast.31), calls=%async_computation | async-start | bytes 8192 | tf_op jit(solution)/shard_map/all_to_all | solution.py:143
  19.1 10.0 %all-to-all-start.1 = ((bf16[8,2,4096]{2,1,0:T(2,128)(2,1)}), bf16[8,2,4096]{2,1,0:T(2,128)(2,1)S(1)}, u32[]{:S(2)}, u32[]{:S(2)}) async-start(bf16[8,2,4096]{2,1,0:T(2,128)(2,1)} %collective-permute-done.1), calls=%async_computation.1 | async-start | bytes 262144 | tf_op jit(solution)/shard_map/all_to_all | solution.py:142
  29.4 4.6 %copy-start = (s32[1,1,4]{2,1,0:T(1,128)S(1)}, s32[1,1,4]{2,1,0:T(1,128)}, u32[]{:S(2)}) copy-start(s32[1,1,4]{2,1,0:T(1,128)} %param.10) | copy-start | bytes 52
  95.6 37.4 %collective-permute-start.2 = (f32[8,1,16,128]{3,2,1,0:T(8,128)S(1)}, f32[8,1,16,128]{3,2,1,0:T(8,128)S(1)}, u32[]{:S(2)}, u32[]{:S(2)}) collective-permute-start(f32[8,1,16,128]{3,2,1,0:T(8,128)S(1)} %get-tuple-element.213), channel_id=1, source_target_pairs={{0,8},{8,16},{16,24},{24,32},{32,40},{40,48},{48,56},{56,0},{1,9},... | collective-permute-start | bytes 196616 | tf_op jit(solution)/shard_map/ppermute | solution.py:29
  97.7 40.2 %collective-permute-start.3 = (f32[8,1,16,128]{3,2,1,0:T(8,128)S(1)}, f32[8,1,16,128]{3,2,1,0:T(8,128)S(1)}, u32[]{:S(2)}, u32[]{:S(2)}) collective-permute-start(f32[8,1,16,128]{3,2,1,0:T(8,128)S(1)} %get-tuple-element.212), channel_id=1, source_target_pairs={{8,0},{16,8},{24,16},{32,24},{40,32},{48,40},{56,48},{0,56},{9,1},... | collective-permute-start | bytes 196616 | tf_op jit(solution)/shard_map/ppermute | solution.py:31
  138.0 5.5 %collective-permute-start.4 = (f32[8,18,1,128]{3,2,1,0:T(1,128)S(1)}, f32[8,18,1,128]{3,2,1,0:T(1,128)S(1)}, u32[]{:S(2)}, u32[]{:S(2)}) collective-permute-start(f32[8,18,1,128]{3,2,1,0:T(1,128)S(1)} %get-tuple-element.206), channel_id=1, source_target_pairs={{0,1},{1,2},{2,3},{3,4},{4,5},{5,6},{6,7},{7,0},{8,9},{9,10},{10,1... | collective-permute-start | bytes 221192 | tf_op jit(solution)/shard_map/ppermute | solution.py:29
  141.5 6.5 %collective-permute-start.5 = (f32[8,18,1,128]{3,2,1,0:T(1,128)S(1)}, f32[8,18,1,128]{3,2,1,0:T(1,128)S(1)}, u32[]{:S(2)}, u32[]{:S(2)}) collective-permute-start(f32[8,18,1,128]{3,2,1,0:T(1,128)S(1)} %get-tuple-element.207), channel_id=1, source_target_pairs={{1,0},{2,1},{3,2},{4,3},{5,4},{6,5},{7,6},{0,7},{9,8},{10,9},{11,1... | collective-permute-start | bytes 221192 | tf_op jit(solution)/shard_map/ppermute | solution.py:31
where the time goes:
time: 152 us; the launch traced here: 151 us
  starting transfers between devices  53.9 us (35%)
  local copies, waits for them, and re-layouts  46.7 us (31%)
  waiting for transfers between devices  19 us (12%)
  loops' own time  14.3 us (9%)
  other arithmetic  12 us (8%)
  matrix products  5.09 us (3%)
    dynamic_update_slice x4, local copies, waits for them, and re-layouts, place_block(): lax.dynamic_update_slice(grid_now, jnp.where(live_slot, new_block, old_bl...  40.8 us
    ppermute x2, starting transfers between devices, extended(): lax.ppermute(head, axis, [((i + 1) % count, i) for i in range(count)])  33.2 us
    another operation x1, loops' own time, local(): grid_cells = lax.fori_loop(0, slots_here, place_block, grid_cells)  14.3 us
    ppermute x2, waiting for transfers between devices, extended(): lax.ppermute(head, axis, [((i + 1) % count, i) for i in range(count)])  9.29 us
    ppermute x2, starting transfers between devices, extended(): lax.ppermute(tail, axis, [(i, (i + 1) % count) for i in range(count)])  5.61 us
    all_to_all x1, starting transfers between devices, local(): lax.all_to_all(moved_pair[1], 'yz', split_axis=0, concat_axis=0, tiled=True)  5.49 us
    all_to_all x1, starting transfers between devices, local(): lax.all_to_all(moved_pair[0], 'yz', split_axis=0, concat_axis=0, tiled=True)  5.35 us
    dot_general x1, matrix products, local(): jnp.einsum('jkcs,jkst->jct', picked, interp_weights[0, 0], preferred_elem...  4.57 us
  transfers between devices with their start and end apart: 8, of which 7 were waited for; matrix products, arithmetic and copies ran while one was open for 3% of the time, Pallas kernels for 0%

commit v1 on v0

--- a/solution.py
+++ b/solution.py
@@ -11,28 +11,6 @@
 HEAT_RATIO = 5.0 / 3.0
 CORONA_RATIO = 0.04
 HELIO_RATIO = 0.03
-
-
-def shifted(block, axis, distance):
-    devices = range(lax.axis_size(axis))
-    route = [(i - distance, i) for i in devices if i - distance in devices]
-    return lax.ppermute(block, axis, route)
-
-
-def extended(cells, sides, width):
-    for axis, dim in sides:
-        count = lax.axis_size(axis)
-        head = lax.slice_in_dim(cells, 0, width, axis=dim)
-        tail = lax.slice_in_dim(cells, cells.shape[dim] - width, cells.shape[dim], axis=dim)
-        cells = jnp.concatenate(
-            [
-                lax.ppermute(tail, axis, [(i, (i + 1) % count) for i in range(count)]),
-                cells,
-                lax.ppermute(head, axis, [((i + 1) % count, i) for i in range(count)]),
-            ],
-            axis=dim,
-        )
-    return cells
 
 
 def direction_flux(grid_cells, direction):
@@ -85,17 +63,21 @@
     return inner_cells - step_ratio * change
 
 
-def edge_copy(padded_line, direction, fix_low, fix_high):
-    array_dim = direction + 1
-    cell_count = padded_line.shape[array_dim]
-    first_layer = lax.slice_in_dim(padded_line, 0, 1, axis=array_dim)
-    second_layer = lax.slice_in_dim(padded_line, 1, 2, axis=array_dim)
-    before_last = lax.slice_in_dim(padded_line, cell_count - 2, cell_count - 1, axis=array_dim)
-    last_layer = lax.slice_in_dim(padded_line, cell_count - 1, cell_count, axis=array_dim)
-    middle = lax.slice_in_dim(padded_line, 1, cell_count - 1, axis=array_dim)
-    first_layer = jnp.where(fix_low, second_layer, first_layer)
-    last_layer = jnp.where(fix_high, before_last, last_layer)
-    return jnp.concatenate([first_layer, middle, last_layer], axis=array_dim)
+def ghost_pair(cells, axis, dim, wrap, fix_low, fix_high):
+    count = lax.axis_size(axis)
+    size = cells.shape[dim]
+    head = lax.slice_in_dim(cells, 0, 1, axis=dim)
+    tail = lax.slice_in_dim(cells, size - 1, size, axis=dim)
+    up = [(i, i + 1) for i in range(count - 1)]
+    down = [(i + 1, i) for i in range(count - 1)]
+    if wrap:
+        up.append((count - 1, 0))
+        down.append((0, count - 1))
+    from_low = lax.ppermute(tail, axis, up)
+    from_high = lax.ppermute(head, axis, down)
+    low = jnp.where(fix_low, head, from_low)
+    high = jnp.where(fix_high, tail, from_high)
+    return jnp.concatenate([low, cells, high], axis=dim)
 
 
 def local(field_state, shell_owner, block_sources, block_targets, interp_weights):
@@ -115,14 +97,8 @@
         shell_cells.transpose(1, 3, 5, 0, 2, 4, 6).reshape(-1, ncomp * volume).astype(jnp.bfloat16)
     )
     count_here = shell_cells.shape[0]
-    owners = shell_owner[0].reshape(-1)
-    own_owner = lax.dynamic_slice_in_dim(owners, yz_index * count_here, count_here)
-    own_spot = yz_index * count_here + jnp.arange(count_here, dtype=jnp.int32)
-    all_spots = jnp.arange(owners.shape[0], dtype=jnp.int32)
-    same_owner = owners[None, :] == own_owner[:, None]
-    rank_all = jnp.sum(
-        (same_owner & (all_spots[None, :] < own_spot[:, None])).astype(jnp.int32), axis=1
-    )
+    owner_table = shell_owner[0]
+    own_owner = lax.dynamic_index_in_dim(owner_table, yz_index, 0, keepdims=False)
     index_here = jnp.arange(count_here, dtype=jnp.int32)
     local_same = own_owner[None, :] == own_owner[:, None]
     rank_local = jnp.sum(
@@ -135,15 +111,16 @@
         select.astype(jnp.bfloat16), shell_cells, preferred_element_type=jnp.float32
     )
     send_cells = send_cells.astype(jnp.bfloat16).reshape(yz_count, CAP, ncomp * volume)
-    send_tags = jnp.sum(jnp.where(select, rank_all[None, :], 0), axis=1)
-    send_tags = jnp.where(jnp.any(select, axis=1), send_tags, -1).reshape(yz_count, CAP)
-    moved_pair = shifted((send_cells, send_tags), "dom", 1)
-    got_cells, got_tags = (
-        lax.all_to_all(moved_pair[0], "yz", split_axis=0, concat_axis=0, tiled=True),
-        lax.all_to_all(moved_pair[1], "yz", split_axis=0, concat_axis=0, tiled=True),
-    )
+    moved = lax.ppermute(send_cells, "dom", [(0, 1)])
+    got_cells = lax.all_to_all(moved, "yz", split_axis=0, concat_axis=0, tiled=True)
     got_cells = got_cells.reshape(slot_count, ncomp * volume)
-    got_tags = got_tags.reshape(slot_count)
+    mine = (owner_table == yz_index).astype(jnp.int32)
+    per_sender = jnp.sum(mine, axis=1)
+    before = jnp.cumsum(per_sender) - per_sender
+    rank_slot = jnp.arange(CAP, dtype=jnp.int32)
+    got_tags = jnp.where(
+        rank_slot[None, :] < per_sender[:, None], before[:, None] + rank_slot[None, :], -1
+    ).reshape(slot_count)
     wanted = block_sources[0, 0].reshape(-1)
     match_table = (wanted[:, None] == got_tags[None, :]) & (wanted[:, None] >= 0)
     picked = jnp.dot(
@@ -155,7 +132,7 @@
         "jkcs,jkst->jct", picked, interp_weights[0, 0], preferred_element_type=jnp.float32
     )
 
-    def place_block(slot_number, grid_now):
+    for slot_number in range(slots_here):
         target_block = block_targets[0, 0, slot_number]
         live_slot = (target_block >= 0) & (domain == 1)
         block_spot = jnp.maximum(target_block, 0)
@@ -163,24 +140,19 @@
         block_y = block_spot // per_z % per_y
         block_z = block_spot % per_z
         corner_start = (jnp.int32(0), block_x * BLK, block_y * BLK, block_z * BLK)
-        old_block = lax.dynamic_slice(grid_now, corner_start, (ncomp, BLK, BLK, BLK))
-        new_block = lax.dynamic_index_in_dim(interp_blocks, slot_number, 0, keepdims=False)
-        new_block = new_block.reshape(ncomp, BLK, BLK, BLK)
-        return lax.dynamic_update_slice(
-            grid_now, jnp.where(live_slot, new_block, old_block), corner_start
+        old_block = lax.dynamic_slice(grid_cells, corner_start, (ncomp, BLK, BLK, BLK))
+        new_block = interp_blocks[slot_number].reshape(ncomp, BLK, BLK, BLK)
+        grid_cells = lax.dynamic_update_slice(
+            grid_cells, jnp.where(live_slot, new_block, old_block), corner_start
         )
 
-    grid_cells = lax.fori_loop(0, slots_here, place_block, grid_cells)
     helio_side = domain == 1
     low_x = helio_side & (column == 0)
     high_x = helio_side & (column == gx_count - 1)
     low_y = yz_index == 0
     high_y = yz_index == yz_count - 1
-    padded = extended(grid_cells, (("gx", 1), ("yz", 2)), 1)
-    line_x = padded[:, :, 1:-1, :]
-    line_y = padded[:, 1:-1, :, :]
-    line_x = edge_copy(line_x, 0, low_x, high_x)
-    line_y = edge_copy(line_y, 1, low_y, high_y)
+    line_x = ghost_pair(grid_cells, "gx", 1, True, low_x, high_x)
+    line_y = ghost_pair(grid_cells, "yz", 2, False, low_y, high_y)
     line_z = jnp.pad(grid_cells, ((0, 0), (0, 0), (0, 0), (1, 1)), mode="edge")
     step_ratio = jnp.where(domain == 0, CORONA_RATIO, HELIO_RATIO).astype(jnp.float32)
     updated = advance((line_x, line_y, line_z), grid_cells, step_ratio)

time: 152 us -> 128 us (0.84)
  the two profiles are of different devices: /device:TPU:54 before, /device:TPU:8 now
where the time goes in v1:
time: 128 us
  local copies, waits for them, and re-layouts  81.1 us (63%)
  starting transfers between devices  21.8 us (17%)
  other arithmetic  8.73 us (7%)
  between operations  5.85 us (5%)
  waiting for transfers between devices  5.13 us (4%)
  matrix products  4.95 us (4%)
    dynamic_update_slice x4, local copies, waits for them, and re-layouts, local(): lax.dynamic_update_slice(grid_cells, jnp.where(live_slot, new_block, old_...  75.3 us
    ppermute x2, starting transfers between devices, ghost_pair(): from_high = lax.ppermute(head, axis, down)  11.7 us
    all_to_all x1, starting transfers between devices, local(): lax.all_to_all(moved, 'yz', split_axis=0, concat_axis=0, tiled=True)  5.77 us
    all_to_all x1, waiting for transfers between devices, local(): lax.all_to_all(moved, 'yz', split_axis=0, concat_axis=0, tiled=True)  5.12 us
    dot_general x1, matrix products, local(): jnp.einsum('jkcs,jkst->jct', picked, interp_weights[0, 0], preferred_elem...  4.56 us
  transfers between devices with their start and end apart: 6, of which 1 were waited for; matrix products, arithmetic and copies ran while one was open for 3% of the time, Pallas kernels for 0%

profile of v1, /device:TPU:8, one launch (start us, length us, event | category | flops | bytes accessed | tf_op | source)
XLA Modules:
  0.0 127.5 jit_solution(6995916996171291732)
XLA Ops:
  0.0 1.2 copy.38
  1.2 0.2 slice.627
  1.4 0.4 convert_element_type.27
  1.9 0.2 copy.11
  2.1 1.5 %convert_element_type.29 = bf16[8,4096]{1,0:T(8,128)(2,1)S(1)} reshape(bf16[2,2,2,8,8,8,8]{6,5,4,3,2,1,0:T(8,128)(2,1)S(1)} %bitcast.194) | data formatting | bytes 131072 | tf_op jit(solution)/shard_map/convert_element_type | solution.py:97
  3.6 0.2 convert_reduce_fusion
  3.8 0.2 convolution_convert_fusion.1
  4.0 0.1 reshape.238
  4.1 2.4 %collective-permute-start = (bf16[8,2,4096]{2,1,0:T(2,128)(2,1)S(1)}, bf16[8,2,4096]{2,1,0:T(2,128)(2,1)}, u32[]{:S(2)}, u32[]{:S(2)}) collective-permute-start(bf16[8,2,4096]{2,1,0:T(2,128)(2,1)S(1)} %reshape.238), channel_id=1, source_target_pairs={{0,64},{1,65},{2,66},{3,67},{4,68},{5,69},{6,70},{7,71},{8,72},{9,... | collective-permute-start | bytes 393224 | tf_op jit(solution)/shard_map/ppermute | solution.py:114
  6.5 0.1 convert_reduce_fusion.1
  6.6 0.7 fusion.85
  12.6 0.2 reduce-window.8
  13.1 5.8 %all-to-all-start = ((bf16[8,2,4096]{2,1,0:T(2,128)(2,1)}), bf16[8,2,4096]{2,1,0:T(2,128)(2,1)S(1)}, u32[]{:S(2)}, u32[]{:S(2)}) async-start(bf16[8,2,4096]{2,1,0:T(2,128)(2,1)} %collective-permute-done), calls=%async_computation | async-start | bytes 262144 | tf_op jit(solution)/shard_map/all_to_all | solution.py:115
  18.9 5.1 %all-to-all-done = bf16[8,2,4096]{2,1,0:T(2,128)(2,1)S(1)} async-done(((bf16[8,2,4096]{2,1,0:T(2,128)(2,1)}), bf16[8,2,4096]{2,1,0:T(2,128)(2,1)S(1)}, u32[]{:S(2)}, u32[]{:S(2)}) %all-to-all-start) | async-done | bytes 131104 | tf_op jit(solution)/shard_map/all_to_all | solution.py:115
  24.0 0.2 convolution_convert_fusion
  24.3 4.6 %fusion.8 = f32[4,8,512]{2,1,0:T(8,128)S(1)} fusion(bf16[4,4,8,512]{3,2,1,0:T(8,128)(2,1)S(1)} %bitcast.195, bf16[1,1,4,4,512,512]{5,4,3,2,1,0:T(8,128)(2,1)} %param.9), kind=kOutput, calls=%fused_computation.17 | convolution fusion | flops 67108864 | bytes 8585216 | tf_op jit(solution)/shard_map/jkcs,jkst->jct/dot_general | solution.py:131
  28.9 0.2 reshape_squeeze.12
  29.1 0.1 bitcast_select_fusion
  29.2 18.8 %dynamic_update_slice.12 = f32[8,16,16,128]{3,2,1,0:T(8,128)S(1)} dynamic-update-slice(f32[8,16,16,128]{3,2,1,0:T(8,128)S(1)} %bitcast.193, f32[8,8,8,8]{3,2,1,0:T(8,128)S(1)} %bitcast_select_fusion, s32[]{:T(128)} %constant.207.clone.1, s32[]{:T(128)S(6)} %select_n.186, s32[]{:T(128)S(6)} %select_n.189, s32[]{:T(128)S(6)} %select_n.191) | dynamic-update-slice | bytes 32772 | tf_op jit(solution)/shard_map/dynamic_update_slice | solution.py:145
  48.0 0.2 reshape_squeeze.13
  48.2 0.1 dynamic-slice_select_fusion.2
  48.3 18.8 %dynamic_update_slice.13 = f32[8,16,16,128]{3,2,1,0:T(8,128)S(1)} dynamic-update-slice(f32[8,16,16,128]{3,2,1,0:T(8,128)S(1)} %dynamic_update_slice.12, f32[8,8,8,8]{3,2,1,0:T(8,128)S(1)} %dynamic-slice_select_fusion.2, s32[]{:T(128)} %constant.207.clone.1, s32[]{:T(128)S(6)} %select_n.195, s32[]{:T(128)S(6)} %select_n.198, s32[]{:T(128)S(6)} %select_n.200) | dynamic-update-slice | bytes 32772 | tf_op jit(solution)/shard_map/dynamic_update_slice | solution.py:145
  67.2 0.2 reshape_squeeze.14
  67.4 0.1 dynamic-slice_select_fusion.1
  67.5 18.8 %dynamic_update_slice.14 = f32[8,16,16,128]{3,2,1,0:T(8,128)S(1)} dynamic-update-slice(f32[8,16,16,128]{3,2,1,0:T(8,128)S(1)} %dynamic_update_slice.13, f32[8,8,8,8]{3,2,1,0:T(8,128)S(1)} %dynamic-slice_select_fusion.1, s32[]{:T(128)} %constant.207.clone.1, s32[]{:T(128)S(6)} %select_n.204, s32[]{:T(128)S(6)} %select_n.207, s32[]{:T(128)S(6)} %select_n.209) | dynamic-update-slice | bytes 32772 | tf_op jit(solution)/shard_map/dynamic_update_slice | solution.py:145
  86.4 0.2 reshape_squeeze.15
  86.5 0.1 dynamic-slice_select_fusion
  86.7 18.8 %dynamic_update_slice.15 = f32[8,16,16,128]{3,2,1,0:T(8,128)S(1)} dynamic-update-slice(f32[8,16,16,128]{3,2,1,0:T(8,128)S(1)} %dynamic_update_slice.14, f32[8,8,8,8]{3,2,1,0:T(8,128)S(1)} %dynamic-slice_select_fusion, s32[]{:T(128)} %constant.207.clone.1, s32[]{:T(128)S(6)} %select_n.213, s32[]{:T(128)S(6)} %select_n.216, s32[]{:T(128)S(6)} %select_n.218) | dynamic-update-slice | bytes 32772 | tf_op jit(solution)/shard_map/dynamic_update_slice | solution.py:145
  105.5 0.3 fusion.83
  106.0 0.9 pad_maximum_fusion
  106.9 0.3 multiply_reduce_fusion
  107.4 0.2 fusion.33
  107.5 0.2 add_dynamic-update-slice_fusion
  108.0 0.1 fusion.19
  108.1 1.9 %collective-permute-start.3 = (f32[8,16,1,128]{3,2,1,0:T(1,128)S(1)}, f32[8,16,1,128]{3,2,1,0:T(1,128)S(1)}, u32[]{:S(2)}, u32[]{:S(2)}) collective-permute-start(f32[8,16,1,128]{3,2,1,0:T(1,128)S(1)} %get-tuple-element.29), channel_id=1, source_target_pairs={{0,1},{1,2},{2,3},{3,4},{4,5},{5,6},{6,7},{8,9},{9,10},{10,11},{11... | collective-permute-start | bytes 196616 | tf_op jit(solution)/shard_map/ppermute | solution.py:76
  110.0 6.0 %collective-permute-start.4 = (f32[8,16,1,128]{3,2,1,0:T(1,128)S(1)}, f32[8,16,1,128]{3,2,1,0:T(1,128)S(1)}, u32[]{:S(2)}, u32[]{:S(2)}) collective-permute-start(f32[8,16,1,128]{3,2,1,0:T(1,128)S(1)} %get-tuple-element.30), channel_id=1, source_target_pairs={{1,0},{2,1},{3,2},{4,3},{5,4},{6,5},{7,6},{9,8},{10,9},{11,10},{12... | collective-permute-start | bytes 196616 | tf_op jit(solution)/shard_map/ppermute | solution.py:77
  116.2 5.6 %collective-permute-start.2 = (f32[8,1,16,128]{3,2,1,0:T(8,128)S(1)}, f32[8,1,16,128]{3,2,1,0:T(8,128)S(1)}, u32[]{:S(2)}, u32[]{:S(2)}) collective-permute-start(f32[8,1,16,128]{3,2,1,0:T(8,128)S(1)} %get-tuple-element.26), channel_id=1, source_target_pairs={{8,0},{16,8},{24,16},{32,24},{40,32},{48,40},{56,48},{0,56},{9,1},... | collective-permute-start | bytes 196616 | tf_op jit(solution)/shard_map/ppermute | solution.py:77
  121.8 0.2 fusion.35
  121.9 1.2 fusion.3
  123.2 0.2 broadcast_select_fusion.1
  123.4 0.3 pad_maximum_fusion.1
  123.6 0.2 multiply_reduce_fusion.3
  123.9 0.1 fusion.51
  124.0 0.1 add_dynamic-update-slice_fusion.1
  124.5 0.1 multiply_reduce_fusion.6
  125.2 0.6 fusion.6
  125.8 0.2 fusion.12
  126.0 1.5 %fusion.17 = f32[1,8,16,16,128]{4,3,2,1,0:T(8,128)} fusion(f32[8,16,16,128]{3,2,1,0:T(8,128)S(1)} %dynamic_update_slice.15, f32[8,16,16,129]{3,2,1,0:T(8,128)S(1)} %fusion.3, f32[8,16,17,128]{3,2,1,0:T(8,128)S(1)} %fusion.6, f32[8,17,16,128]{3,2,1,0:T(8,128)S(1)} %fusion.12, f32[]{:T(128)S(6)} %select_n.220), kind=kLoop, calls=%fused_computation.27 | loop fusion | flops 1835008 | bytes 8388612 | tf_op jit(solution)/shard_map/broadcast_in_dim | solution.py:159
  (50 shorter events, 2.0 us)
Async XLA Ops:
  1.8 1.8 %copy-start.1 = (s32[1,8,8]{2,1,0:T(8,128)S(1)}, s32[1,8,8]{2,1,0:T(8,128)}, u32[]{:S(2)}) copy-start(s32[1,8,8]{2,1,0:T(8,128)} %param.6) | copy-start | bytes 772
  1.9 4.8 %copy-start = (s32[1,1,4]{2,1,0:T(1,128)S(1)}, s32[1,1,4]{2,1,0:T(1,128)}, u32[]{:S(2)}) copy-start(s32[1,1,4]{2,1,0:T(1,128)} %param.8) | copy-start | bytes 52
  1.9 11.1 %copy-start.2 = (s32[1,1,4,4]{3,2,1,0:T(4,128)S(1)}, s32[1,1,4,4]{3,2,1,0:T(4,128)}, u32[]{:S(2)}) copy-start(s32[1,1,4,4]{3,2,1,0:T(4,128)} %param.7) | copy-start | bytes 196
  4.1 9.0 %collective-permute-start = (bf16[8,2,4096]{2,1,0:T(2,128)(2,1)S(1)}, bf16[8,2,4096]{2,1,0:T(2,128)(2,1)}, u32[]{:S(2)}, u32[]{:S(2)}) collective-permute-start(bf16[8,2,4096]{2,1,0:T(2,128)(2,1)S(1)} %reshape.238), channel_id=1, source_target_pairs={{0,64},{1,65},{2,66},{3,67},{4,68},{5,69},{6,70},{7,71},{8,72},{9,... | collective-permute-start | bytes 393224 | tf_op jit(solution)/shard_map/ppermute | solution.py:114
  13.1 10.9 %all-to-all-start = ((bf16[8,2,4096]{2,1,0:T(2,128)(2,1)}), bf16[8,2,4096]{2,1,0:T(2,128)(2,1)S(1)}, u32[]{:S(2)}, u32[]{:S(2)}) async-start(bf16[8,2,4096]{2,1,0:T(2,128)(2,1)} %collective-permute-done), calls=%async_computation | async-start | bytes 262144 | tf_op jit(solution)/shard_map/all_to_all | solution.py:115
  108.1 15.1 %collective-permute-start.3 = (f32[8,16,1,128]{3,2,1,0:T(1,128)S(1)}, f32[8,16,1,128]{3,2,1,0:T(1,128)S(1)}, u32[]{:S(2)}, u32[]{:S(2)}) collective-permute-start(f32[8,16,1,128]{3,2,1,0:T(1,128)S(1)} %get-tuple-element.29), channel_id=1, source_target_pairs={{0,1},{1,2},{2,3},{3,4},{4,5},{5,6},{6,7},{8,9},{9,10},{10,11},{11... | collective-permute-start | bytes 196616 | tf_op jit(solution)/shard_map/ppermute | solution.py:76
  110.0 13.1 %collective-permute-start.4 = (f32[8,16,1,128]{3,2,1,0:T(1,128)S(1)}, f32[8,16,1,128]{3,2,1,0:T(1,128)S(1)}, u32[]{:S(2)}, u32[]{:S(2)}) collective-permute-start(f32[8,16,1,128]{3,2,1,0:T(1,128)S(1)} %get-tuple-element.30), channel_id=1, source_target_pairs={{1,0},{2,1},{3,2},{4,3},{5,4},{6,5},{7,6},{9,8},{10,9},{11,10},{12... | collective-permute-start | bytes 196616 | tf_op jit(solution)/shard_map/ppermute | solution.py:77
  116.1 8.3 %collective-permute-start.1 = (f32[8,1,16,128]{3,2,1,0:T(8,128)S(1)}, f32[8,1,16,128]{3,2,1,0:T(8,128)S(1)}, u32[]{:S(2)}, u32[]{:S(2)}) collective-permute-start(f32[8,1,16,128]{3,2,1,0:T(8,128)S(1)} %get-tuple-element.25), channel_id=1, source_target_pairs={{0,8},{8,16},{16,24},{24,32},{32,40},{40,48},{48,56},{56,0},{1,9},... | collective-permute-start | bytes 196616 | tf_op jit(solution)/shard_map/ppermute | solution.py:76
  116.2 8.2 %collective-permute-start.2 = (f32[8,1,16,128]{3,2,1,0:T(8,128)S(1)}, f32[8,1,16,128]{3,2,1,0:T(8,128)S(1)}, u32[]{:S(2)}, u32[]{:S(2)}) collective-permute-start(f32[8,1,16,128]{3,2,1,0:T(8,128)S(1)} %get-tuple-element.26), channel_id=1, source_target_pairs={{8,0},{16,8},{24,16},{32,24},{40,32},{48,40},{56,48},{0,56},{9,1},... | collective-permute-start | bytes 196616 | tf_op jit(solution)/shard_map/ppermute | solution.py:77

commit v2 on v1

--- a/solution.py
+++ b/solution.py
@@ -132,18 +132,18 @@
         "jkcs,jkst->jct", picked, interp_weights[0, 0], preferred_element_type=jnp.float32
     )
 
+    block_of = (
+        (lax.broadcasted_iota(jnp.int32, (len_x, len_y, len_z), 0) // BLK * per_y
+         + lax.broadcasted_iota(jnp.int32, (len_x, len_y, len_z), 1) // BLK) * per_z
+        + lax.broadcasted_iota(jnp.int32, (len_x, len_y, len_z), 2) // BLK
+    )
+    reps = (1, len_x // BLK, len_y // BLK, len_z // BLK)
     for slot_number in range(slots_here):
         target_block = block_targets[0, 0, slot_number]
-        live_slot = (target_block >= 0) & (domain == 1)
-        block_spot = jnp.maximum(target_block, 0)
-        block_x = block_spot // (per_y * per_z)
-        block_y = block_spot // per_z % per_y
-        block_z = block_spot % per_z
-        corner_start = (jnp.int32(0), block_x * BLK, block_y * BLK, block_z * BLK)
-        old_block = lax.dynamic_slice(grid_cells, corner_start, (ncomp, BLK, BLK, BLK))
+        target_block = jnp.where(domain == 1, target_block, -1)
         new_block = interp_blocks[slot_number].reshape(ncomp, BLK, BLK, BLK)
-        grid_cells = lax.dynamic_update_slice(
-            grid_cells, jnp.where(live_slot, new_block, old_block), corner_start
+        grid_cells = jnp.where(
+            (block_of == target_block)[None], jnp.tile(new_block, reps), grid_cells
         )
 
     helio_side = domain == 1

time: 128 us -> 130 us (1.016)
  between operations: 5.85 us -> 3.07 us
  local copies, waits for them, and re-layouts: 81.1 us -> 83.1 us
  other arithmetic: 8.73 us -> 10.6 us
    another operation x4 -> x12, local copies, waits for them, and re-layouts: 0.64 us -> 77.2 us  [local(): jnp.tile(new_block, reps)]
    dynamic_update_slice x4 -> x0, local copies, waits for them, and re-layouts: 75.3 us -> none  [local(): lax.dynamic_update_slice(grid_cells, jnp.where(live_slot, new_block, old_...]
    ppermute x2, starting transfers between devices: 2 us -> 5.12 us  [ghost_pair(): from_low = lax.ppermute(tail, axis, up)]
    ppermute x2, starting transfers between devices: 11.7 us -> 8.97 us  [ghost_pair(): from_high = lax.ppermute(head, axis, down)]
    select_n x4 -> x1, other arithmetic: 0.58 us -> 1.89 us  [local(): jnp.where((block_of == target_block)[None], jnp.tile(new_block, reps), gr...]
  transfers between devices with their start and end apart: 6 -> 6, of which waited for: 1 -> 1; matrix products, arithmetic and copies ran while one was open for 3% -> 4% of each run, Pallas kernels for 0% -> 0%
where the time goes in v2:
time: 130 us; the launch traced here: 129 us
  local copies, waits for them, and re-layouts  83.1 us (64%)
  starting transfers between devices  22.2 us (17%)
  other arithmetic  10.6 us (8%)
  waiting for transfers between devices  5.13 us (4%)
  matrix products  4.95 us (4%)
  between operations  3.07 us (2%)
    another operation x12, local copies, waits for them, and re-layouts, local(): jnp.tile(new_block, reps)  77.2 us
    ppermute x2, starting transfers between devices, ghost_pair(): from_high = lax.ppermute(head, axis, down)  8.97 us
    all_to_all x1, starting transfers between devices, local(): lax.all_to_all(moved, 'yz', split_axis=0, concat_axis=0, tiled=True)  5.77 us
    ppermute x2, starting transfers between devices, ghost_pair(): from_low = lax.ppermute(tail, axis, up)  5.12 us
    all_to_all x1, waiting for transfers between devices, local(): lax.all_to_all(moved, 'yz', split_axis=0, concat_axis=0, tiled=True)  5.11 us
    dot_general x1, matrix products, local(): jnp.einsum('jkcs,jkst->jct', picked, interp_weights[0, 0], preferred_elem...  4.56 us
  transfers between devices with their start and end apart: 6, of which 1 were waited for; matrix products, arithmetic and copies ran while one was open for 4% of the time, Pallas kernels for 0%

profile of v2, /device:TPU:8, one launch (start us, length us, event | category | flops | bytes accessed | tf_op | source)
XLA Modules:
  0.0 129.1 jit_solution(11474570953546929175)
XLA Ops:
  0.0 0.7 dynamic-slice_bitcast_fusion
  0.7 0.2 convert_reduce_fusion
  0.9 0.7 multiply_add_fusion
  1.6 1.4 %slice.627 = bf16[8,16,16,16]{3,2,1,0:T(8,128)(2,1)S(1)} slice(f32[8,16,16,128]{3,2,1,0:T(8,128)} %bitcast.180), slice={[0:8], [0:16], [0:16], [112:128]} | slice | bytes 131072 | tf_op jit(solution)/shard_map/slice | solution.py:94
  3.0 0.4 convert_element_type.27
  3.4 0.2 copy.11
  3.7 1.5 %convert_element_type.29 = bf16[8,4096]{1,0:T(8,128)(2,1)S(1)} reshape(bf16[2,2,2,8,8,8,8]{6,5,4,3,2,1,0:T(8,128)(2,1)S(1)} %bitcast.179) | data formatting | bytes 131072 | tf_op jit(solution)/shard_map/convert_element_type | solution.py:97
  5.2 0.2 convolution_convert_fusion.1
  5.5 2.4 %collective-permute-start = (bf16[8,2,4096]{2,1,0:T(2,128)(2,1)S(1)}, bf16[8,2,4096]{2,1,0:T(2,128)(2,1)}, u32[]{:S(2)}, u32[]{:S(2)}) collective-permute-start(bf16[8,2,4096]{2,1,0:T(2,128)(2,1)S(1)} %reshape.196), channel_id=1, source_target_pairs={{0,64},{1,65},{2,66},{3,67},{4,68},{5,69},{6,70},{7,71},{8,72},{9,... | collective-permute-start | bytes 393224 | tf_op jit(solution)/shard_map/ppermute | solution.py:114
  8.0 0.2 reduce-window.8
  8.5 0.7 fusion.88
  11.7 0.2 fusion.76
  11.9 5.8 %all-to-all-start = ((bf16[8,2,4096]{2,1,0:T(2,128)(2,1)}), bf16[8,2,4096]{2,1,0:T(2,128)(2,1)S(1)}, u32[]{:S(2)}, u32[]{:S(2)}) async-start(bf16[8,2,4096]{2,1,0:T(2,128)(2,1)} %collective-permute-done), calls=%async_computation | async-start | bytes 262144 | tf_op jit(solution)/shard_map/all_to_all | solution.py:115
  17.6 5.1 %all-to-all-done = bf16[8,2,4096]{2,1,0:T(2,128)(2,1)S(1)} async-done(((bf16[8,2,4096]{2,1,0:T(2,128)(2,1)}), bf16[8,2,4096]{2,1,0:T(2,128)(2,1)S(1)}, u32[]{:S(2)}, u32[]{:S(2)}) %all-to-all-start) | async-done | bytes 131104 | tf_op jit(solution)/shard_map/all_to_all | solution.py:115
  22.8 0.2 convolution_convert_fusion
  23.1 4.6 %fusion.8 = f32[4,8,512]{2,1,0:T(8,128)S(1)} fusion(bf16[4,4,8,512]{3,2,1,0:T(8,128)(2,1)S(1)} %bitcast.181, bf16[1,1,4,4,512,512]{5,4,3,2,1,0:T(8,128)(2,1)} %param.9), kind=kOutput, calls=%fused_computation.17 | convolution fusion | flops 67108864 | bytes 8585216 | tf_op jit(solution)/shard_map/jkcs,jkst->jct/dot_general | solution.py:131
  27.7 0.2 tile.40
  27.8 7.2 %tile.41 = f32[8,2,8,2,8,16,8]{6,5,4,3,2,1,0:T(8,128)} broadcast(f32[8,8,8,8]{3,2,1,0:T(8,128)S(1)} %tile.40), dimensions={0,2,4,6} | broadcast | bytes 1064960 | tf_op jit(solution)/shard_map/tile | solution.py:146
  35.0 11.8 %tile.42 = f32[8,16,16,128]{3,2,1,0:T(8,128)S(1)} reshape(f32[8,2,8,2,8,16,8]{6,5,4,3,2,1,0:T(8,128)} %tile.41) | data formatting | bytes 2097152 | tf_op jit(solution)/shard_map/tile | solution.py:146
  46.8 0.2 tile.43
  46.9 7.2 %tile.44 = f32[8,2,8,2,8,16,8]{6,5,4,3,2,1,0:T(8,128)} broadcast(f32[8,8,8,8]{3,2,1,0:T(8,128)S(1)} %tile.43), dimensions={0,2,4,6} | broadcast | bytes 1064960 | tf_op jit(solution)/shard_map/tile | solution.py:146
  54.1 11.8 %tile.45 = f32[8,16,16,128]{3,2,1,0:T(8,128)S(1)} reshape(f32[8,2,8,2,8,16,8]{6,5,4,3,2,1,0:T(8,128)} %tile.44) | data formatting | bytes 2097152 | tf_op jit(solution)/shard_map/tile | solution.py:146
  65.9 0.2 tile.46
  66.1 7.2 %tile.47 = f32[8,2,8,2,8,16,8]{6,5,4,3,2,1,0:T(8,128)} broadcast(f32[8,8,8,8]{3,2,1,0:T(8,128)S(1)} %tile.46), dimensions={0,2,4,6} | broadcast | bytes 1064960 | tf_op jit(solution)/shard_map/tile | solution.py:146
  73.2 11.8 %tile.48 = f32[8,16,16,128]{3,2,1,0:T(8,128)S(1)} reshape(f32[8,2,8,2,8,16,8]{6,5,4,3,2,1,0:T(8,128)} %tile.47) | data formatting | bytes 2097152 | tf_op jit(solution)/shard_map/tile | solution.py:146
  85.0 0.2 tile.49
  85.2 7.2 %tile.50 = f32[8,2,8,2,8,16,8]{6,5,4,3,2,1,0:T(8,128)} broadcast(f32[8,8,8,8]{3,2,1,0:T(8,128)S(1)} %tile.49), dimensions={0,2,4,6} | broadcast | bytes 1064960 | tf_op jit(solution)/shard_map/tile | solution.py:146
  92.3 12.6 %tile.51 = f32[8,16,16,128]{3,2,1,0:T(8,128)} reshape(f32[8,2,8,2,8,16,8]{6,5,4,3,2,1,0:T(8,128)} %tile.50) | data formatting | bytes 2097152 | tf_op jit(solution)/shard_map/tile | solution.py:146
  105.0 1.9 %select_select_fusion = f32[8,16,16,128]{3,2,1,0:T(8,128)S(1)} fusion(f32[8,16,16,128]{3,2,1,0:T(8,128)S(1)} %tile.42, f32[8,16,16,128]{3,2,1,0:T(8,128)S(1)} %tile.45, f32[8,16,16,128]{3,2,1,0:T(8,128)S(1)} %tile.48, f32[8,16,16,128]{3,2,1,0:T(8,128)} %tile.51, pred[16,16,128]{2,1,0:T(8,128)(4,1)S(1)} %get-tuple-element.40, ...), kind=kLoop, calls=%fused_computation.33 | loop fusion | flops 1048576 | bytes 6422528 | tf_op jit(solution)/shard_map/jit(_where)/select_n | solution.py:145
  107.0 0.4 fusion.86
  107.3 2.4 %collective-permute-start.1 = (f32[8,1,16,128]{3,2,1,0:T(8,128)S(1)}, f32[8,1,16,128]{3,2,1,0:T(8,128)S(1)}, u32[]{:S(2)}, u32[]{:S(2)}) collective-permute-start(f32[8,1,16,128]{3,2,1,0:T(8,128)S(1)} %get-tuple-element.25), channel_id=1, source_target_pairs={{0,8},{8,16},{16,24},{24,32},{32,40},{40,48},{48,56},{56,0},{1,9},... | collective-permute-start | bytes 196616 | tf_op jit(solution)/shard_map/ppermute | solution.py:76
  109.7 3.8 %collective-permute-start.2 = (f32[8,1,16,128]{3,2,1,0:T(8,128)S(1)}, f32[8,1,16,128]{3,2,1,0:T(8,128)S(1)}, u32[]{:S(2)}, u32[]{:S(2)}) collective-permute-start(f32[8,1,16,128]{3,2,1,0:T(8,128)S(1)} %get-tuple-element.26), channel_id=1, source_target_pairs={{8,0},{16,8},{24,16},{32,24},{40,32},{48,40},{56,48},{0,56},{9,1},... | collective-permute-start | bytes 196616 | tf_op jit(solution)/shard_map/ppermute | solution.py:77
  113.5 2.8 %collective-permute-start.3 = (f32[8,16,1,128]{3,2,1,0:T(1,128)S(1)}, f32[8,16,1,128]{3,2,1,0:T(1,128)S(1)}, u32[]{:S(2)}, u32[]{:S(2)}) collective-permute-start(f32[8,16,1,128]{3,2,1,0:T(1,128)S(1)} %get-tuple-element.29), channel_id=1, source_target_pairs={{0,1},{1,2},{2,3},{3,4},{4,5},{5,6},{6,7},{8,9},{9,10},{10,11},{11... | collective-permute-start | bytes 196616 | tf_op jit(solution)/shard_map/ppermute | solution.py:76
  116.2 5.2 %collective-permute-start.4 = (f32[8,16,1,128]{3,2,1,0:T(1,128)S(1)}, f32[8,16,1,128]{3,2,1,0:T(1,128)S(1)}, u32[]{:S(2)}, u32[]{:S(2)}) collective-permute-start(f32[8,16,1,128]{3,2,1,0:T(1,128)S(1)} %get-tuple-element.30), channel_id=1, source_target_pairs={{1,0},{2,1},{3,2},{4,3},{5,4},{6,5},{7,6},{9,8},{10,9},{11,10},{12... | collective-permute-start | bytes 196616 | tf_op jit(solution)/shard_map/ppermute | solution.py:77
  121.4 0.9 pad_maximum_fusion
  122.4 0.3 multiply_reduce_fusion
  122.6 0.2 fusion.33
  122.8 0.1 fusion.19
  123.1 0.2 add_dynamic-update-slice_fusion
  123.6 0.2 fusion.35
  123.7 1.1 fusion.3
  125.6 0.1 broadcast_select_fusion.1
  125.8 0.2 pad_maximum_fusion.1
  126.1 0.2 multiply_reduce_fusion.3
  126.2 0.1 fusion.51
  126.8 0.2 fusion.12
  127.1 0.5 fusion.6
  127.6 1.4 %fusion.17 = f32[1,8,16,16,128]{4,3,2,1,0:T(8,128)} fusion(f32[8,16,16,128]{3,2,1,0:T(8,128)S(1)} %select_select_fusion, f32[8,16,16,129]{3,2,1,0:T(8,128)S(1)} %fusion.3, f32[8,16,17,128]{3,2,1,0:T(8,128)S(1)} %fusion.6, f32[8,17,16,128]{3,2,1,0:T(8,128)S(1)} %fusion.12, f32[]{:T(128)S(6)} %select_n.155), kind=kLoop, calls=%fused_computation.27 | loop fusion | flops 1835008 | bytes 8388612 | tf_op jit(solution)/shard_map/broadcast_in_dim | solution.py:159
  (55 shorter events, 2.3 us)
Async XLA Ops:
  3.4 4.4 %copy-start.1 = (s32[1,8,8]{2,1,0:T(8,128)S(1)}, s32[1,8,8]{2,1,0:T(8,128)}, u32[]{:S(2)}) copy-start(s32[1,8,8]{2,1,0:T(8,128)} %param.6) | copy-start | bytes 772
  3.4 4.9 %copy-start.2 = (s32[1,1,4,4]{3,2,1,0:T(4,128)S(1)}, s32[1,1,4,4]{3,2,1,0:T(4,128)}, u32[]{:S(2)}) copy-start(s32[1,1,4,4]{3,2,1,0:T(4,128)} %param.7) | copy-start | bytes 196
  3.4 5.0 %copy-start = (s32[1,1,4]{2,1,0:T(1,128)S(1)}, s32[1,1,4]{2,1,0:T(1,128)}, u32[]{:S(2)}) copy-start(s32[1,1,4]{2,1,0:T(1,128)} %param.8) | copy-start | bytes 52
  5.5 6.4 %collective-permute-start = (bf16[8,2,4096]{2,1,0:T(2,128)(2,1)S(1)}, bf16[8,2,4096]{2,1,0:T(2,128)(2,1)}, u32[]{:S(2)}, u32[]{:S(2)}) collective-permute-start(bf16[8,2,4096]{2,1,0:T(2,128)(2,1)S(1)} %reshape.196), channel_id=1, source_target_pairs={{0,64},{1,65},{2,66},{3,67},{4,68},{5,69},{6,70},{7,71},{8,72},{9,... | collective-permute-start | bytes 393224 | tf_op jit(solution)/shard_map/ppermute | solution.py:114
  11.9 10.9 %all-to-all-start = ((bf16[8,2,4096]{2,1,0:T(2,128)(2,1)}), bf16[8,2,4096]{2,1,0:T(2,128)(2,1)S(1)}, u32[]{:S(2)}, u32[]{:S(2)}) async-start(bf16[8,2,4096]{2,1,0:T(2,128)(2,1)} %collective-permute-done), calls=%async_computation | async-start | bytes 262144 | tf_op jit(solution)/shard_map/all_to_all | solution.py:115
  107.3 17.6 %collective-permute-start.1 = (f32[8,1,16,128]{3,2,1,0:T(8,128)S(1)}, f32[8,1,16,128]{3,2,1,0:T(8,128)S(1)}, u32[]{:S(2)}, u32[]{:S(2)}) collective-permute-start(f32[8,1,16,128]{3,2,1,0:T(8,128)S(1)} %get-tuple-element.25), channel_id=1, source_target_pairs={{0,8},{8,16},{16,24},{24,32},{32,40},{40,48},{48,56},{56,0},{1,9},... | collective-permute-start | bytes 196616 | tf_op jit(solution)/shard_map/ppermute | solution.py:76
  109.7 15.2 %collective-permute-start.2 = (f32[8,1,16,128]{3,2,1,0:T(8,128)S(1)}, f32[8,1,16,128]{3,2,1,0:T(8,128)S(1)}, u32[]{:S(2)}, u32[]{:S(2)}) collective-permute-start(f32[8,1,16,128]{3,2,1,0:T(8,128)S(1)} %get-tuple-element.26), channel_id=1, source_target_pairs={{8,0},{16,8},{24,16},{32,24},{40,32},{48,40},{56,48},{0,56},{9,1},... | collective-permute-start | bytes 196616 | tf_op jit(solution)/shard_map/ppermute | solution.py:77
  113.5 12.1 %collective-permute-start.3 = (f32[8,16,1,128]{3,2,1,0:T(1,128)S(1)}, f32[8,16,1,128]{3,2,1,0:T(1,128)S(1)}, u32[]{:S(2)}, u32[]{:S(2)}) collective-permute-start(f32[8,16,1,128]{3,2,1,0:T(1,128)S(1)} %get-tuple-element.29), channel_id=1, source_target_pairs={{0,1},{1,2},{2,3},{3,4},{4,5},{5,6},{6,7},{8,9},{9,10},{10,11},{11... | collective-permute-start | bytes 196616 | tf_op jit(solution)/shard_map/ppermute | solution.py:76
  116.2 9.4 %collective-permute-start.4 = (f32[8,16,1,128]{3,2,1,0:T(1,128)S(1)}, f32[8,16,1,128]{3,2,1,0:T(1,128)S(1)}, u32[]{:S(2)}, u32[]{:S(2)}) collective-permute-start(f32[8,16,1,128]{3,2,1,0:T(1,128)S(1)} %get-tuple-element.30), channel_id=1, source_target_pairs={{1,0},{2,1},{3,2},{4,3},{5,4},{6,5},{7,6},{9,8},{10,9},{11,10},{12... | collective-permute-start | bytes 196616 | tf_op jit(solution)/shard_map/ppermute | solution.py:77

commit v3 on v2

--- a/solution.py
+++ b/solution.py
@@ -132,19 +132,27 @@
         "jkcs,jkst->jct", picked, interp_weights[0, 0], preferred_element_type=jnp.float32
     )
 
-    block_of = (
-        (lax.broadcasted_iota(jnp.int32, (len_x, len_y, len_z), 0) // BLK * per_y
-         + lax.broadcasted_iota(jnp.int32, (len_x, len_y, len_z), 1) // BLK) * per_z
-        + lax.broadcasted_iota(jnp.int32, (len_x, len_y, len_z), 2) // BLK
-    )
-    reps = (1, len_x // BLK, len_y // BLK, len_z // BLK)
+    rows = lax.broadcasted_iota(jnp.int32, (len_x, len_y, len_z), 0) // BLK
+    cols = lax.broadcasted_iota(jnp.int32, (len_x, len_y, len_z), 1) // BLK
+    lanes = lax.broadcasted_iota(jnp.int32, (len_x, len_y, len_z), 2)
+    spread_of = lax.broadcasted_iota(jnp.int32, (BLK, len_z), 1) % BLK
+    offset_of = lax.broadcasted_iota(jnp.int32, (BLK, len_z), 0)
+    spread = (spread_of == offset_of).astype(jnp.float32)
+    stacked = interp_blocks.reshape(slots_here * ncomp * BLK * BLK, BLK)
+    stacked = jnp.dot(stacked, spread, precision=lax.Precision.HIGHEST)
+    stacked = stacked.reshape(slots_here, ncomp, BLK, BLK, len_z)
     for slot_number in range(slots_here):
         target_block = block_targets[0, 0, slot_number]
         target_block = jnp.where(domain == 1, target_block, -1)
-        new_block = interp_blocks[slot_number].reshape(ncomp, BLK, BLK, BLK)
-        grid_cells = jnp.where(
-            (block_of == target_block)[None], jnp.tile(new_block, reps), grid_cells
+        block_spot = jnp.maximum(target_block, 0)
+        hit = (
+            (rows == block_spot // (per_y * per_z))
+            & (cols == block_spot // per_z % per_y)
+            & (lanes // BLK == block_spot % per_z)
+            & (target_block >= 0)
         )
+        placed = jnp.tile(stacked[slot_number], (1, len_x // BLK, len_y // BLK, 1))
+        grid_cells = jnp.where(hit[None], placed, grid_cells)
 
     helio_side = domain == 1
     low_x = helio_side & (column == 0)

time: 130 us -> 53 us (0.41)
  the two profiles are of different devices: /device:TPU:8 before, /device:TPU:56 now
where the time goes in v3:
time: 53 us; the launch traced here: 52.7 us
  starting transfers between devices  19.7 us (37%)
  other arithmetic  8.79 us (17%)
  waiting for transfers between devices  8.25 us (16%)
  local copies, waits for them, and re-layouts  7.16 us (14%)
  matrix products  5.57 us (11%)
  between operations  3.17 us (6%)
    ppermute x2, starting transfers between devices, ghost_pair(): from_high = lax.ppermute(head, axis, down)  6.13 us
    all_to_all x1, starting transfers between devices, local(): lax.all_to_all(moved, 'yz', split_axis=0, concat_axis=0, tiled=True)  5.77 us
    ppermute x2, starting transfers between devices, ghost_pair(): from_low = lax.ppermute(tail, axis, up)  5.42 us
    all_to_all x1, waiting for transfers between devices, local(): lax.all_to_all(moved, 'yz', split_axis=0, concat_axis=0, tiled=True)  5.03 us
    dot_general x1, matrix products, local(): jnp.einsum('jkcs,jkst->jct', picked, interp_weights[0, 0], preferred_elem...  4.56 us
    ppermute x2, waiting for transfers between devices, ghost_pair(): from_high = lax.ppermute(head, axis, down)  3.21 us
    ppermute x1, starting transfers between devices, local(): moved = lax.ppermute(send_cells, 'dom', [(0, 1)])  2.38 us
    convert_element_type x3, local copies, waits for them, and re-layouts, local(): shell_cells.transpose(1, 3, 5, 0, 2, 4, 6).reshape(-1, ncomp * volume)  2.12 us
  transfers between devices with their start and end apart: 6, of which 2 were waited for; matrix products, arithmetic and copies ran while one was open for 8% of the time, Pallas kernels for 0%

profile of v3, /device:TPU:56, one launch (start us, length us, event | category | flops | bytes accessed | tf_op | source)
XLA Modules:
  0.0 52.7 jit_solution(3426356747653776286)
XLA Ops:
  0.0 1.4 %slice.631 = bf16[8,16,16,16]{3,2,1,0:T(8,128)(2,1)S(1)} slice(f32[8,16,16,128]{3,2,1,0:T(8,128)} %bitcast.185), slice={[0:8], [0:16], [0:16], [112:128]} | slice | bytes 131072 | tf_op jit(solution)/shard_map/slice | solution.py:94
  1.4 0.4 convert_element_type.28
  1.9 0.2 copy.11
  2.1 1.5 %convert_element_type.30 = bf16[8,4096]{1,0:T(8,128)(2,1)S(1)} reshape(bf16[2,2,2,8,8,8,8]{6,5,4,3,2,1,0:T(8,128)(2,1)S(1)} %bitcast.184) | data formatting | bytes 131072 | tf_op jit(solution)/shard_map/convert_element_type | solution.py:97
  3.6 0.2 convert_reduce_fusion
  3.8 0.2 convolution_convert_fusion.1
  4.0 0.1 reshape.224
  4.1 2.4 %collective-permute-start = (bf16[8,2,4096]{2,1,0:T(2,128)(2,1)S(1)}, bf16[8,2,4096]{2,1,0:T(2,128)(2,1)}, u32[]{:S(2)}, u32[]{:S(2)}) collective-permute-start(bf16[8,2,4096]{2,1,0:T(2,128)(2,1)S(1)} %reshape.224), channel_id=1, source_target_pairs={{0,64},{1,65},{2,66},{3,67},{4,68},{5,69},{6,70},{7,71},{8,72},{9,... | collective-permute-start | bytes 393224 | tf_op jit(solution)/shard_map/ppermute | solution.py:114
  6.5 0.1 convert_reduce_fusion.1
  6.6 0.7 %fusion.100 = (s32[1,1,1]{2,1,0:T(1,128)}, s32[1,1,1]{2,1,0:T(1,128)}, s32[1,1,1]{2,1,0:T(1,128)}, s32[1,1,1]{2,1,0:T(1,128)}) fusion(s32[1,1,4]{2,1,0:T(1,128)S(1)} %copy-done.1), kind=kLoop, calls=%fused_computation.208 | loop fusion | bytes 32 | tf_op jit(solution)/shard_map/slice | solution.py:145
  10.0 0.2 reduce-window.8
  10.3 0.1 fusion.84
  10.5 0.2 fusion.75
  10.7 5.8 %all-to-all-start = ((bf16[8,2,4096]{2,1,0:T(2,128)(2,1)}), bf16[8,2,4096]{2,1,0:T(2,128)(2,1)S(1)}, u32[]{:S(2)}, u32[]{:S(2)}) async-start(bf16[8,2,4096]{2,1,0:T(2,128)(2,1)} %collective-permute-done), calls=%async_computation | async-start | bytes 262144 | tf_op jit(solution)/shard_map/all_to_all | solution.py:115
  16.5 5.0 %all-to-all-done = bf16[8,2,4096]{2,1,0:T(2,128)(2,1)S(1)} async-done(((bf16[8,2,4096]{2,1,0:T(2,128)(2,1)}), bf16[8,2,4096]{2,1,0:T(2,128)(2,1)S(1)}, u32[]{:S(2)}, u32[]{:S(2)}) %all-to-all-start) | async-done | bytes 131104 | tf_op jit(solution)/shard_map/all_to_all | solution.py:115
  21.6 0.2 convolution_convert_fusion
  21.9 4.6 %fusion.8 = f32[4,8,512]{2,1,0:T(8,128)S(1)} fusion(bf16[4,4,8,512]{3,2,1,0:T(8,128)(2,1)S(1)} %bitcast.190, bf16[1,1,4,4,512,512]{5,4,3,2,1,0:T(8,128)(2,1)} %param.9), kind=kOutput, calls=%fused_computation.17 | convolution fusion | flops 67108864 | bytes 8585216 | tf_op jit(solution)/shard_map/jkcs,jkst->jct/dot_general | solution.py:131
  26.5 0.6 %reshape.227 = f32[2048,8]{1,0:T(8,128)S(1)} reshape(f32[4,8,512]{2,1,0:T(8,128)S(1)} %fusion.8) | data formatting | bytes 131072 | tf_op jit(solution)/shard_map/reshape | solution.py:141
  27.1 0.6 %fusion.92 = f32[2048,128]{1,0:T(8,128)S(1)} fusion(f32[2048,8]{1,0:T(8,128)S(1)} %reshape.227, s32[128]{0:T(128)S(1)} %get-tuple-element.44, s32[128]{0:T(128)S(1)} %get-tuple-element.45, pred[128]{0:T(512)(128)(4,1)S(1)} %compare_and_fusion), kind=kOutput, calls=%fused_computation.184 | convolution fusion | flops 25167872 | bytes 1115264 | tf_op jit(solution)/shard_map/dot_general | solution.py:142
  28.1 1.0 %copy-done = f32[1,8,16,16,128]{4,3,2,1,0:T(8,128)S(1)} copy-done((f32[1,8,16,16,128]{4,3,2,1,0:T(8,128)S(1)}, f32[1,8,16,16,128]{4,3,2,1,0:T(8,128)}, u32[]{:S(2)}) %copy-start) | copy-done | bytes 1048600
  29.2 0.4 select_select_fusion
  29.6 0.4 fusion.98
  29.9 0.1 fusion.97
  30.0 0.9 %pad_maximum_fusion = f32[8,16,16,130]{3,2,1,0:T(8,128)S(1)} fusion(f32[8,16,16,1]{3,2,1,0:T(8,128)S(1)} %get-tuple-element.32, f32[8,16,16,128]{3,2,1,0:T(8,128)S(1)} %select_select_fusion, f32[8,16,16,1]{3,2,1,0:T(8,128)S(1)} %get-tuple-element.31), kind=kLoop, calls=%fused_computation.7 | loop fusion | flops 532480 | bytes 2129920 | tf_op jit(solution)/shard_map/jit(_pad)/concatenate | solution.py:164
  31.0 0.3 multiply_reduce_fusion
  31.4 0.2 fusion.33
  31.6 0.2 add_dynamic-update-slice_fusion
  31.9 0.1 fusion.21
  32.0 0.1 fusion.19
  32.2 2.8 %collective-permute-start.3 = (f32[8,16,1,128]{3,2,1,0:T(1,128)S(1)}, f32[8,16,1,128]{3,2,1,0:T(1,128)S(1)}, u32[]{:S(2)}, u32[]{:S(2)}) collective-permute-start(f32[8,16,1,128]{3,2,1,0:T(1,128)S(1)} %get-tuple-element.29), channel_id=1, source_target_pairs={{0,1},{1,2},{2,3},{3,4},{4,5},{5,6},{6,7},{8,9},{9,10},{10,11},{11... | collective-permute-start | bytes 196616 | tf_op jit(solution)/shard_map/ppermute | solution.py:76
  34.9 5.2 %collective-permute-start.4 = (f32[8,16,1,128]{3,2,1,0:T(1,128)S(1)}, f32[8,16,1,128]{3,2,1,0:T(1,128)S(1)}, u32[]{:S(2)}, u32[]{:S(2)}) collective-permute-start(f32[8,16,1,128]{3,2,1,0:T(1,128)S(1)} %get-tuple-element.30), channel_id=1, source_target_pairs={{1,0},{2,1},{3,2},{4,3},{5,4},{6,5},{7,6},{9,8},{10,9},{11,10},{12... | collective-permute-start | bytes 196616 | tf_op jit(solution)/shard_map/ppermute | solution.py:77
  40.1 2.7 %collective-permute-start.1 = (f32[8,1,16,128]{3,2,1,0:T(8,128)S(1)}, f32[8,1,16,128]{3,2,1,0:T(8,128)S(1)}, u32[]{:S(2)}, u32[]{:S(2)}) collective-permute-start(f32[8,1,16,128]{3,2,1,0:T(8,128)S(1)} %get-tuple-element.25), channel_id=1, source_target_pairs={{0,8},{8,16},{16,24},{24,32},{32,40},{40,48},{48,56},{56,0},{1,9},... | collective-permute-start | bytes 196616 | tf_op jit(solution)/shard_map/ppermute | solution.py:76
  42.8 0.9 %collective-permute-start.2 = (f32[8,1,16,128]{3,2,1,0:T(8,128)S(1)}, f32[8,1,16,128]{3,2,1,0:T(8,128)S(1)}, u32[]{:S(2)}, u32[]{:S(2)}) collective-permute-start(f32[8,1,16,128]{3,2,1,0:T(8,128)S(1)} %get-tuple-element.26), channel_id=1, source_target_pairs={{8,0},{16,8},{24,16},{32,24},{40,32},{48,40},{56,48},{0,56},{9,1},... | collective-permute-start | bytes 196616 | tf_op jit(solution)/shard_map/ppermute | solution.py:77
  43.7 0.2 fusion.35
  43.9 1.1 %fusion.3 = f32[8,16,16,129]{3,2,1,0:T(8,128)S(1)} fusion(f32[8,16,16,130]{3,2,1,0:T(8,128)S(1)} %fusion.35, f32[8,16,16,1]{3,2,1,0:T(8,128)S(1)} %get-tuple-element.32, f32[8,16,16,128]{3,2,1,0:T(8,128)S(1)} %select_select_fusion, f32[8,16,16,1]{3,2,1,0:T(8,128)S(1)} %get-tuple-element.31, f32[16,16,129]{2,1,0:T(8,128)S(1)} %fusion.19), kind=kLoop, calls=%fused_computation.6 | loop fusion | flops 1849344 | bytes 4367360 | tf_op jit(solution)/shard_map/sub | solution.py:54
  45.1 0.1 broadcast_select_fusion.1
  45.2 0.3 pad_maximum_fusion.1
  45.5 0.2 multiply_reduce_fusion.3
  45.8 0.1 fusion.51
  45.9 0.1 add_dynamic-update-slice_fusion.1
  46.2 3.2 %collective-permute-done.2 = f32[8,1,16,128]{3,2,1,0:T(8,128)S(1)} collective-permute-done((f32[8,1,16,128]{3,2,1,0:T(8,128)S(1)}, f32[8,1,16,128]{3,2,1,0:T(8,128)S(1)}, u32[]{:S(2)}, u32[]{:S(2)}) %collective-permute-start.2) | collective-permute-done | bytes 65568 | tf_op jit(solution)/shard_map/ppermute | solution.py:77
  49.5 0.1 pad_maximum_fusion.2
  49.6 0.1 multiply_reduce_fusion.6
  49.7 0.1 fusion.68
  50.1 0.1 fusion.53
  50.2 0.6 %fusion.6 = f32[8,16,17,128]{3,2,1,0:T(8,128)S(1)} fusion(f32[8,16,18,128]{3,2,1,0:T(8,128)S(1)} %fusion.53, f32[8,16,1,128]{3,2,1,0:T(1,128)S(1)} %get-tuple-element.28, f32[8,16,16,128]{3,2,1,0:T(8,128)S(1)} %select_select_fusion, f32[8,16,1,128]{3,2,1,0:T(1,128)S(1)} %get-tuple-element.27, f32[16,17,128]{2,1,0:T(8,128)S(1)} %fusion.37), kind=kLoop, calls=%fused_computation.12 | loop fusion | flops 1949696 | bytes 4661248 | tf_op jit(solution)/shard_map/sub | solution.py:54
  50.9 0.3 fusion.12
  51.2 1.4 %fusion.17 = f32[1,8,16,16,128]{4,3,2,1,0:T(8,128)} fusion(f32[8,16,16,128]{3,2,1,0:T(8,128)S(1)} %select_select_fusion, f32[8,16,16,129]{3,2,1,0:T(8,128)S(1)} %fusion.3, f32[8,16,17,128]{3,2,1,0:T(8,128)S(1)} %fusion.6, f32[8,17,16,128]{3,2,1,0:T(8,128)S(1)} %fusion.12, f32[]{:T(128)S(6)} %select_n.241), kind=kLoop, calls=%fused_computation.27 | loop fusion | flops 1835008 | bytes 8388612 | tf_op jit(solution)/shard_map/broadcast_in_dim | solution.py:167
  (54 shorter events, 1.8 us)
Async XLA Ops:
  1.8 1.8 %copy-start.2 = (s32[1,8,8]{2,1,0:T(8,128)S(1)}, s32[1,8,8]{2,1,0:T(8,128)}, u32[]{:S(2)}) copy-start(s32[1,8,8]{2,1,0:T(8,128)} %param.6) | copy-start | bytes 772
  1.9 4.8 %copy-start.1 = (s32[1,1,4]{2,1,0:T(1,128)S(1)}, s32[1,1,4]{2,1,0:T(1,128)}, u32[]{:S(2)}) copy-start(s32[1,1,4]{2,1,0:T(1,128)} %param.8) | copy-start | bytes 52
  1.9 8.4 %copy-start.3 = (s32[1,1,4,4]{3,2,1,0:T(4,128)S(1)}, s32[1,1,4,4]{3,2,1,0:T(4,128)}, u32[]{:S(2)}) copy-start(s32[1,1,4,4]{3,2,1,0:T(4,128)} %param.7) | copy-start | bytes 196
  4.1 6.6 %collective-permute-start = (bf16[8,2,4096]{2,1,0:T(2,128)(2,1)S(1)}, bf16[8,2,4096]{2,1,0:T(2,128)(2,1)}, u32[]{:S(2)}, u32[]{:S(2)}) collective-permute-start(bf16[8,2,4096]{2,1,0:T(2,128)(2,1)S(1)} %reshape.224), channel_id=1, source_target_pairs={{0,64},{1,65},{2,66},{3,67},{4,68},{5,69},{6,70},{7,71},{8,72},{9,... | collective-permute-start | bytes 393224 | tf_op jit(solution)/shard_map/ppermute | solution.py:114
  10.7 10.9 %all-to-all-start = ((bf16[8,2,4096]{2,1,0:T(2,128)(2,1)}), bf16[8,2,4096]{2,1,0:T(2,128)(2,1)S(1)}, u32[]{:S(2)}, u32[]{:S(2)}) async-start(bf16[8,2,4096]{2,1,0:T(2,128)(2,1)} %collective-permute-done), calls=%async_computation | async-start | bytes 262144 | tf_op jit(solution)/shard_map/all_to_all | solution.py:115
  27.9 1.2 %copy-start = (f32[1,8,16,16,128]{4,3,2,1,0:T(8,128)S(1)}, f32[1,8,16,16,128]{4,3,2,1,0:T(8,128)}, u32[]{:S(2)}) copy-start(f32[1,8,16,16,128]{4,3,2,1,0:T(8,128)} %param.5) | copy-start | bytes 3145732
  32.2 12.9 %collective-permute-start.3 = (f32[8,16,1,128]{3,2,1,0:T(1,128)S(1)}, f32[8,16,1,128]{3,2,1,0:T(1,128)S(1)}, u32[]{:S(2)}, u32[]{:S(2)}) collective-permute-start(f32[8,16,1,128]{3,2,1,0:T(1,128)S(1)} %get-tuple-element.29), channel_id=1, source_target_pairs={{0,1},{1,2},{2,3},{3,4},{4,5},{5,6},{6,7},{8,9},{9,10},{10,11},{11... | collective-permute-start | bytes 196616 | tf_op jit(solution)/shard_map/ppermute | solution.py:76
  34.9 10.1 %collective-permute-start.4 = (f32[8,16,1,128]{3,2,1,0:T(1,128)S(1)}, f32[8,16,1,128]{3,2,1,0:T(1,128)S(1)}, u32[]{:S(2)}, u32[]{:S(2)}) collective-permute-start(f32[8,16,1,128]{3,2,1,0:T(1,128)S(1)} %get-tuple-element.30), channel_id=1, source_target_pairs={{1,0},{2,1},{3,2},{4,3},{5,4},{6,5},{7,6},{9,8},{10,9},{11,10},{12... | collective-permute-start | bytes 196616 | tf_op jit(solution)/shard_map/ppermute | solution.py:77
  40.1 6.1 %collective-permute-start.1 = (f32[8,1,16,128]{3,2,1,0:T(8,128)S(1)}, f32[8,1,16,128]{3,2,1,0:T(8,128)S(1)}, u32[]{:S(2)}, u32[]{:S(2)}) collective-permute-start(f32[8,1,16,128]{3,2,1,0:T(8,128)S(1)} %get-tuple-element.25), channel_id=1, source_target_pairs={{0,8},{8,16},{16,24},{24,32},{32,40},{40,48},{48,56},{56,0},{1,9},... | collective-permute-start | bytes 196616 | tf_op jit(solution)/shard_map/ppermute | solution.py:76
  42.8 6.7 %collective-permute-start.2 = (f32[8,1,16,128]{3,2,1,0:T(8,128)S(1)}, f32[8,1,16,128]{3,2,1,0:T(8,128)S(1)}, u32[]{:S(2)}, u32[]{:S(2)}) collective-permute-start(f32[8,1,16,128]{3,2,1,0:T(8,128)S(1)} %get-tuple-element.26), channel_id=1, source_target_pairs={{8,0},{16,8},{24,16},{32,24},{40,32},{48,40},{56,48},{0,56},{9,1},... | collective-permute-start | bytes 196616 | tf_op jit(solution)/shard_map/ppermute | solution.py:77

commit v4 on v3

--- a/solution.py
+++ b/solution.py
@@ -1,7 +1,11 @@
 import jax
 import jax.numpy as jnp
 from jax import lax
+from jax.experimental import pallas as pl
+from jax.experimental.pallas import tpu as pltpu
 from jax.sharding import PartitionSpec as P
+
+MESH = pl.DeviceIdType.MESH
 
 BLK = 8
 SR = 2
@@ -80,6 +84,65 @@
     return jnp.concatenate([low, cells, high], axis=dim)
 
 
+def route_kernel(send_ref, out_ref, landed, send_sem, recv_sem):
+    domain = lax.axis_index("dom")
+    here = lax.axis_index("yz")
+    count = send_ref.shape[0]
+    barrier = pltpu.get_barrier_semaphore()
+    for partner in range(count):
+        pl.semaphore_signal(
+            barrier, inc=1, device_id={"dom": 1 - domain, "yz": partner}, device_id_type=MESH
+        )
+    pl.semaphore_wait(barrier, count)
+
+    @pl.when(domain == 0)
+    def _():
+        copies = []
+        for owner in range(count):
+            copy = pltpu.make_async_remote_copy(
+                src_ref=send_ref.at[owner],
+                dst_ref=landed.at[here],
+                send_sem=send_sem.at[owner],
+                recv_sem=recv_sem.at[here],
+                device_id={"dom": 1, "yz": owner},
+                device_id_type=MESH,
+            )
+            copy.start()
+            copies.append(copy)
+        for copy in copies:
+            copy.wait_send()
+        out_ref[...] = jnp.zeros_like(out_ref)
+
+    @pl.when(domain == 1)
+    def _():
+        for sender in range(count):
+            pltpu.make_async_remote_copy(
+                src_ref=send_ref.at[sender],
+                dst_ref=landed.at[sender],
+                send_sem=send_sem.at[sender],
+                recv_sem=recv_sem.at[sender],
+                device_id={"dom": 0, "yz": sender},
+                device_id_type=MESH,
+            ).wait_recv()
+        out_ref[...] = landed[...]
+
+
+def route_blocks(send_cells):
+    count = send_cells.shape[0]
+    return pl.pallas_call(
+        route_kernel,
+        out_shape=jax.ShapeDtypeStruct(send_cells.shape, send_cells.dtype),
+        in_specs=[pl.BlockSpec(memory_space=pltpu.VMEM)],
+        out_specs=pl.BlockSpec(memory_space=pltpu.VMEM),
+        scratch_shapes=[
+            pltpu.VMEM(send_cells.shape, send_cells.dtype),
+            pltpu.SemaphoreType.DMA((count,)),
+            pltpu.SemaphoreType.DMA((count,)),
+        ],
+        compiler_params=pltpu.CompilerParams(collective_id=0, has_side_effects=True),
+    )(send_cells)
+
+
 def local(field_state, shell_owner, block_sources, block_targets, interp_weights):
     grid_cells = field_state[0]
     ncomp, len_x, len_y, len_z = grid_cells.shape
@@ -110,10 +173,8 @@
     send_cells = jnp.dot(
         select.astype(jnp.bfloat16), shell_cells, preferred_element_type=jnp.float32
     )
-    send_cells = send_cells.astype(jnp.bfloat16).reshape(yz_count, CAP, ncomp * volume)
-    moved = lax.ppermute(send_cells, "dom", [(0, 1)])
-    got_cells = lax.all_to_all(moved, "yz", split_axis=0, concat_axis=0, tiled=True)
-    got_cells = got_cells.reshape(slot_count, ncomp * volume)
+    send_cells = send_cells.astype(jnp.bfloat16).reshape(yz_count, CAP * ncomp, volume)
+    got_cells = route_blocks(send_cells).reshape(slot_count, ncomp * volume)
     mine = (owner_table == yz_index).astype(jnp.int32)
     per_sender = jnp.sum(mine, axis=1)
     before = jnp.cumsum(per_sender) - per_sender

time: 53 us -> 50.7 us (0.957)
  the two profiles are of different devices: /device:TPU:56 before, /device:TPU:9 now
where the time goes in v4:
time: 50.7 us; the launch traced here: 50.3 us
  starting transfers between devices  13.2 us (26%)
  local copies, waits for them, and re-layouts  10.1 us (20%)
  other arithmetic  9.68 us (19%)
  Pallas kernels  8.42 us (17%)
  matrix products  5.58 us (11%)
  between operations  3.26 us (6%)
    ppermute x2, starting transfers between devices, ghost_pair(): from_high = lax.ppermute(head, axis, down)  8.64 us
    pallas_call x1, Pallas kernels, route_blocks(): pl.pallas_call(route_kernel, out_shape=jax.ShapeDtypeStruct(send_cells.sh...  8.42 us
    ppermute x2, starting transfers between devices, ghost_pair(): from_low = lax.ppermute(tail, axis, up)  4.56 us
    dot_general x1, matrix products, local(): jnp.einsum('jkcs,jkst->jct', picked, interp_weights[0, 0], preferred_elem...  4.56 us
    convert_element_type x3, local copies, waits for them, and re-layouts, local(): shell_cells.transpose(1, 3, 5, 0, 2, 4, 6).reshape(-1, ncomp * volume)  2.12 us
    sub x3, other arithmetic, interface_change(): 0.5 * (low_flux + high_flux)  2.01 us
    broadcast_in_dim x1, other arithmetic, local(): return updated[None]  1.54 us
    slice x1, local copies, waits for them, and re-layouts, local(): target_block = block_targets[0, 0, slot_number]  1.47 us
  transfers between devices with their start and end apart: 4, of which 0 were waited for; matrix products, arithmetic and copies ran while one was open for 12% of the time, Pallas kernels for 0%

profile of v4, /device:TPU:9, one launch (start us, length us, event | category | flops | bytes accessed | tf_op | source)
XLA Modules:
  0.0 50.3 jit_solution(11486048861194980405)
XLA Ops:
  0.0 1.5 %fusion.100 = (s32[1,1,1]{2,1,0:T(1,128)}, s32[1,1,1]{2,1,0:T(1,128)}, s32[1,1,1]{2,1,0:T(1,128)}, s32[1,1,1]{2,1,0:T(1,128)}) fusion(s32[1,1,4]{2,1,0:T(1,128)} %param.8), kind=kLoop, calls=%fused_computation.208 | loop fusion | bytes 32 | tf_op jit(solution)/shard_map/slice | solution.py:206
  4.2 1.4 %slice.631 = bf16[8,16,16,16]{3,2,1,0:T(8,128)(2,1)S(1)} slice(f32[8,16,16,128]{3,2,1,0:T(8,128)} %bitcast.185), slice={[0:8], [0:16], [0:16], [112:128]} | slice | bytes 131072 | tf_op jit(solution)/shard_map/slice | solution.py:157
  5.6 0.4 convert_element_type.28
  6.0 0.2 copy.11
  6.3 1.5 %convert_element_type.30 = bf16[8,4096]{1,0:T(8,128)(2,1)S(1)} reshape(bf16[2,2,2,8,8,8,8]{6,5,4,3,2,1,0:T(8,128)(2,1)S(1)} %bitcast.184) | data formatting | bytes 131072 | tf_op jit(solution)/shard_map/convert_element_type | solution.py:160
  7.8 0.1 convert_reduce_fusion.1
  7.9 0.2 convert_reduce_fusion
  8.1 0.2 convolution_convert_fusion.1
  8.3 0.7 %reshape.224.send_ref = bf16[8,16,512]{2,1,0:T(8,128)(2,1)} reshape(bf16[16,4096]{1,0:T(8,128)(2,1)S(1)} %convolution_convert_fusion.1) | data formatting | bytes 262144 | tf_op jit(solution)/shard_map/reshape | solution.py:176
  9.0 8.4 %shard_map.55 = bf16[8,16,512]{2,1,0:T(8,128)(2,1)} custom-call(bf16[8,16,512]{2,1,0:T(8,128)(2,1)} %reshape.224.send_ref), custom_call_target="tpu_custom_call" | custom-call | tf_op jit(solution)/shard_map/pallas_call | solution.py:132
  17.4 1.0 %reshape.225 = bf16[16,4096]{1,0:T(8,128)(2,1)S(1)} reshape(bf16[8,16,512]{2,1,0:T(8,128)(2,1)} %shard_map.55) | data formatting | bytes 262144 | tf_op jit(solution)/shard_map/reshape | solution.py:177
  18.4 0.2 reduce-window.8
  18.8 0.2 convolution_convert_fusion
  19.1 4.6 %fusion.8 = f32[4,8,512]{2,1,0:T(8,128)S(1)} fusion(bf16[4,4,8,512]{3,2,1,0:T(8,128)(2,1)S(1)} %bitcast.190, bf16[1,1,4,4,512,512]{5,4,3,2,1,0:T(8,128)(2,1)} %param.9), kind=kOutput, calls=%fused_computation.17 | convolution fusion | flops 67108864 | bytes 8585216 | tf_op jit(solution)/shard_map/jkcs,jkst->jct/dot_general | solution.py:192
  23.7 0.6 %reshape.227 = f32[2048,8]{1,0:T(8,128)S(1)} reshape(f32[4,8,512]{2,1,0:T(8,128)S(1)} %fusion.8) | data formatting | bytes 131072 | tf_op jit(solution)/shard_map/reshape | solution.py:202
  24.3 0.6 %fusion.92 = f32[2048,128]{1,0:T(8,128)S(1)} fusion(f32[2048,8]{1,0:T(8,128)S(1)} %reshape.227, s32[128]{0:T(128)S(1)} %get-tuple-element.44, s32[128]{0:T(128)S(1)} %get-tuple-element.45, pred[128]{0:T(512)(128)(4,1)S(1)} %compare_and_fusion), kind=kOutput, calls=%fused_computation.184 | convolution fusion | flops 25167872 | bytes 1115264 | tf_op jit(solution)/shard_map/dot_general | solution.py:203
  25.1 0.1 fusion.84
  25.2 0.2 fusion.75
  25.8 1.0 %copy-done = f32[1,8,16,16,128]{4,3,2,1,0:T(8,128)S(1)} copy-done((f32[1,8,16,16,128]{4,3,2,1,0:T(8,128)S(1)}, f32[1,8,16,16,128]{4,3,2,1,0:T(8,128)}, u32[]{:S(2)}) %copy-start) | copy-done | bytes 1048600
  26.8 0.4 select_select_fusion
  27.2 0.7 %fusion.97 = (f32[8,16,1,128]{3,2,1,0:T(1,128)}, f32[8,16,1,128]{3,2,1,0:T(1,128)S(1)}) fusion(f32[8,16,16,128]{3,2,1,0:T(8,128)S(1)} %select_select_fusion), kind=kLoop, calls=%fused_computation.205 | loop fusion | bytes 262144 | tf_op jit(solution)/shard_map/slice | solution.py:74
  27.9 2.5 %collective-permute-start.2 = (f32[8,16,1,128]{3,2,1,0:T(1,128)}, f32[8,16,1,128]{3,2,1,0:T(1,128)S(1)}, u32[]{:S(2)}, u32[]{:S(2)}) collective-permute-start(f32[8,16,1,128]{3,2,1,0:T(1,128)} %get-tuple-element.29), channel_id=1, source_target_pairs={{0,1},{1,2},{2,3},{3,4},{4,5},{5,6},{6,7},{8,9},{9,10},{10,11},{11... | collective-permute-start | bytes 196616 | tf_op jit(solution)/shard_map/ppermute | solution.py:80
  30.4 4.9 %collective-permute-start.3 = (f32[8,16,1,128]{3,2,1,0:T(1,128)S(1)}, f32[8,16,1,128]{3,2,1,0:T(1,128)}, u32[]{:S(2)}, u32[]{:S(2)}) collective-permute-start(f32[8,16,1,128]{3,2,1,0:T(1,128)S(1)} %get-tuple-element.30), channel_id=1, source_target_pairs={{1,0},{2,1},{3,2},{4,3},{5,4},{6,5},{7,6},{9,8},{10,9},{11,10},{12... | collective-permute-start | bytes 196616 | tf_op jit(solution)/shard_map/ppermute | solution.py:81
  35.3 2.1 %collective-permute-start = (f32[8,1,16,128]{3,2,1,0:T(8,128)S(1)}, f32[8,1,16,128]{3,2,1,0:T(8,128)S(1)}, u32[]{:S(2)}, u32[]{:S(2)}) collective-permute-start(f32[8,1,16,128]{3,2,1,0:T(8,128)S(1)} %get-tuple-element.25), channel_id=1, source_target_pairs={{0,8},{8,16},{16,24},{24,32},{32,40},{40,48},{48,56},{56,0},{1,9},... | collective-permute-start | bytes 196616 | tf_op jit(solution)/shard_map/ppermute | solution.py:80
  37.4 3.7 %collective-permute-start.1 = (f32[8,1,16,128]{3,2,1,0:T(8,128)S(1)}, f32[8,1,16,128]{3,2,1,0:T(8,128)S(1)}, u32[]{:S(2)}, u32[]{:S(2)}) collective-permute-start(f32[8,1,16,128]{3,2,1,0:T(8,128)S(1)} %get-tuple-element.26), channel_id=1, source_target_pairs={{8,0},{16,8},{24,16},{32,24},{40,32},{48,40},{56,48},{0,56},{9,1},... | collective-permute-start | bytes 196616 | tf_op jit(solution)/shard_map/ppermute | solution.py:81
  41.1 0.3 fusion.98
  41.5 0.9 %pad_maximum_fusion = f32[8,16,16,130]{3,2,1,0:T(8,128)S(1)} fusion(f32[8,16,16,1]{3,2,1,0:T(8,128)S(1)} %get-tuple-element.32, f32[8,16,16,128]{3,2,1,0:T(8,128)S(1)} %select_select_fusion, f32[8,16,16,1]{3,2,1,0:T(8,128)S(1)} %get-tuple-element.31), kind=kLoop, calls=%fused_computation.7 | loop fusion | flops 532480 | bytes 2129920 | tf_op jit(solution)/shard_map/jit(_pad)/concatenate | solution.py:225
  42.4 0.3 multiply_reduce_fusion
  42.7 0.1 fusion.27
  42.8 0.1 fusion.25
  42.9 0.2 fusion.33
  43.1 0.2 add_dynamic-update-slice_fusion
  43.3 0.1 fusion.23
  43.3 0.1 fusion.21
  43.5 0.1 fusion.19
  43.6 0.2 fusion.35
  43.8 1.2 %fusion.3 = f32[8,16,16,129]{3,2,1,0:T(8,128)S(1)} fusion(f32[8,16,16,130]{3,2,1,0:T(8,128)S(1)} %fusion.35, f32[8,16,16,1]{3,2,1,0:T(8,128)S(1)} %get-tuple-element.32, f32[8,16,16,128]{3,2,1,0:T(8,128)S(1)} %select_select_fusion, f32[8,16,16,1]{3,2,1,0:T(8,128)S(1)} %get-tuple-element.31, f32[16,16,129]{2,1,0:T(8,128)S(1)} %fusion.19), kind=kLoop, calls=%fused_computation.6 | loop fusion | flops 1849344 | bytes 4367360 | tf_op jit(solution)/shard_map/sub | solution.py:58
  45.1 1.0 %broadcast_select_fusion.1 = (f32[8,16,1,128]{3,2,1,0:T(1,128)S(1)}, f32[8,16,1,128]{3,2,1,0:T(1,128)S(1)}) fusion(f32[8,16,1,128]{3,2,1,0:T(1,128)S(1)} %collective-permute-done.2, pred[]{:T(512)S(6)} %eq.245, f32[8,16,16,128]{3,2,1,0:T(8,128)S(1)} %select_select_fusion, f32[8,16,1,128]{3,2,1,0:T(1,128)} %collective-permute-done.3, pred[]{:T(512)S(6)} %eq.246), kind=kLoop, calls=%fused_computation.167 | loop fusion | flops 32768 | bytes 393218 | tf_op jit(solution)/shard_map/jit(_where)/select_n | solution.py:82
  46.0 0.3 pad_maximum_fusion.1
  46.3 0.2 multiply_reduce_fusion.3
  46.6 0.1 fusion.51
  46.7 0.1 add_dynamic-update-slice_fusion.1
  47.2 0.1 multiply_reduce_fusion.6
  47.4 0.1 fusion.68
  47.8 0.1 fusion.53
  47.8 0.6 %fusion.6 = f32[8,16,17,128]{3,2,1,0:T(8,128)S(1)} fusion(f32[8,16,18,128]{3,2,1,0:T(8,128)S(1)} %fusion.53, f32[8,16,1,128]{3,2,1,0:T(1,128)S(1)} %get-tuple-element.28, f32[8,16,16,128]{3,2,1,0:T(8,128)S(1)} %select_select_fusion, f32[8,16,1,128]{3,2,1,0:T(1,128)S(1)} %get-tuple-element.27, f32[16,17,128]{2,1,0:T(8,128)S(1)} %fusion.37), kind=kLoop, calls=%fused_computation.12 | loop fusion | flops 1949696 | bytes 4661248 | tf_op jit(solution)/shard_map/sub | solution.py:58
  48.5 0.2 fusion.12
  48.7 1.5 %fusion.17 = f32[1,8,16,16,128]{4,3,2,1,0:T(8,128)} fusion(f32[8,16,16,128]{3,2,1,0:T(8,128)S(1)} %select_select_fusion, f32[8,16,16,129]{3,2,1,0:T(8,128)S(1)} %fusion.3, f32[8,16,17,128]{3,2,1,0:T(8,128)S(1)} %fusion.6, f32[8,17,16,128]{3,2,1,0:T(8,128)S(1)} %fusion.12, f32[]{:T(128)S(6)} %select_n.241), kind=kLoop, calls=%fused_computation.27 | loop fusion | flops 1835008 | bytes 8388612 | tf_op jit(solution)/shard_map/broadcast_in_dim | solution.py:228
  (49 shorter events, 1.6 us)
Async XLA Ops:
  6.0 1.8 %copy-start.1 = (s32[1,8,8]{2,1,0:T(8,128)S(1)}, s32[1,8,8]{2,1,0:T(8,128)}, u32[]{:S(2)}) copy-start(s32[1,8,8]{2,1,0:T(8,128)} %param.6) | copy-start | bytes 772
  6.3 12.5 %copy-start.2 = (s32[1,1,4,4]{3,2,1,0:T(4,128)S(1)}, s32[1,1,4,4]{3,2,1,0:T(4,128)}, u32[]{:S(2)}) copy-start(s32[1,1,4,4]{3,2,1,0:T(4,128)} %param.7) | copy-start | bytes 196
  25.6 1.2 %copy-start = (f32[1,8,16,16,128]{4,3,2,1,0:T(8,128)S(1)}, f32[1,8,16,16,128]{4,3,2,1,0:T(8,128)}, u32[]{:S(2)}) copy-start(f32[1,8,16,16,128]{4,3,2,1,0:T(8,128)} %param.5) | copy-start | bytes 3145732
  27.9 17.2 %collective-permute-start.2 = (f32[8,16,1,128]{3,2,1,0:T(1,128)}, f32[8,16,1,128]{3,2,1,0:T(1,128)S(1)}, u32[]{:S(2)}, u32[]{:S(2)}) collective-permute-start(f32[8,16,1,128]{3,2,1,0:T(1,128)} %get-tuple-element.29), channel_id=1, source_target_pairs={{0,1},{1,2},{2,3},{3,4},{4,5},{5,6},{6,7},{8,9},{9,10},{10,11},{11... | collective-permute-start | bytes 196616 | tf_op jit(solution)/shard_map/ppermute | solution.py:80
  30.4 14.7 %collective-permute-start.3 = (f32[8,16,1,128]{3,2,1,0:T(1,128)S(1)}, f32[8,16,1,128]{3,2,1,0:T(1,128)}, u32[]{:S(2)}, u32[]{:S(2)}) collective-permute-start(f32[8,16,1,128]{3,2,1,0:T(1,128)S(1)} %get-tuple-element.30), channel_id=1, source_target_pairs={{1,0},{2,1},{3,2},{4,3},{5,4},{6,5},{7,6},{9,8},{10,9},{11,10},{12... | collective-permute-start | bytes 196616 | tf_op jit(solution)/shard_map/ppermute | solution.py:81
  35.3 11.8 %collective-permute-start = (f32[8,1,16,128]{3,2,1,0:T(8,128)S(1)}, f32[8,1,16,128]{3,2,1,0:T(8,128)S(1)}, u32[]{:S(2)}, u32[]{:S(2)}) collective-permute-start(f32[8,1,16,128]{3,2,1,0:T(8,128)S(1)} %get-tuple-element.25), channel_id=1, source_target_pairs={{0,8},{8,16},{16,24},{24,32},{32,40},{40,48},{48,56},{56,0},{1,9},... | collective-permute-start | bytes 196616 | tf_op jit(solution)/shard_map/ppermute | solution.py:80
  37.4 9.7 %collective-permute-start.1 = (f32[8,1,16,128]{3,2,1,0:T(8,128)S(1)}, f32[8,1,16,128]{3,2,1,0:T(8,128)S(1)}, u32[]{:S(2)}, u32[]{:S(2)}) collective-permute-start(f32[8,1,16,128]{3,2,1,0:T(8,128)S(1)} %get-tuple-element.26), channel_id=1, source_target_pairs={{8,0},{16,8},{24,16},{32,24},{40,32},{48,40},{56,48},{0,56},{9,1},... | collective-permute-start | bytes 196616 | tf_op jit(solution)/shard_map/ppermute | solution.py:81

commit v5 on v4

--- a/solution.py
+++ b/solution.py
@@ -65,23 +65,6 @@
     change = interface_change(line_set[0], 0) + interface_change(line_set[1], 1)
     change = change + interface_change(line_set[2], 2)
     return inner_cells - step_ratio * change
-
-
-def ghost_pair(cells, axis, dim, wrap, fix_low, fix_high):
-    count = lax.axis_size(axis)
-    size = cells.shape[dim]
-    head = lax.slice_in_dim(cells, 0, 1, axis=dim)
-    tail = lax.slice_in_dim(cells, size - 1, size, axis=dim)
-    up = [(i, i + 1) for i in range(count - 1)]
-    down = [(i + 1, i) for i in range(count - 1)]
-    if wrap:
-        up.append((count - 1, 0))
-        down.append((0, count - 1))
-    from_low = lax.ppermute(tail, axis, up)
-    from_high = lax.ppermute(head, axis, down)
-    low = jnp.where(fix_low, head, from_low)
-    high = jnp.where(fix_high, tail, from_high)
-    return jnp.concatenate([low, cells, high], axis=dim)
 
 
 def route_kernel(send_ref, out_ref, landed, send_sem, recv_sem):
@@ -143,6 +126,60 @@
     )(send_cells)
 
 
+def halo_kernel(grid_ref, out_ref, landed, send_sem, recv_sem):
+    column = lax.axis_index("gx")
+    row = lax.axis_index("yz")
+    gx_count = lax.axis_size("gx")
+    yz_count = lax.axis_size("yz")
+    len_x, len_y = grid_ref.shape[1], grid_ref.shape[2]
+    up_x = {"gx": lax.rem(column + 1, gx_count)}
+    down_x = {"gx": lax.rem(column + gx_count - 1, gx_count)}
+    up_y = {"yz": lax.rem(row + 1, yz_count)}
+    down_y = {"yz": lax.rem(row + yz_count - 1, yz_count)}
+    barrier = pltpu.get_barrier_semaphore()
+    for partner in (up_x, down_x, up_y, down_y):
+        pl.semaphore_signal(barrier, inc=1, device_id=partner, device_id_type=MESH)
+    pl.semaphore_wait(barrier, 4)
+    sends = (
+        (grid_ref.at[:, len_x - 1], up_x),
+        (grid_ref.at[:, 0], down_x),
+        (grid_ref.at[:, :, len_y - 1], up_y),
+        (grid_ref.at[:, :, 0], down_y),
+    )
+    copies = []
+    for slot, (source, partner) in enumerate(sends):
+        copy = pltpu.make_async_remote_copy(
+            src_ref=source,
+            dst_ref=landed.at[slot],
+            send_sem=send_sem.at[slot],
+            recv_sem=recv_sem.at[slot],
+            device_id=partner,
+            device_id_type=MESH,
+        )
+        copy.start()
+        copies.append(copy)
+    for copy in copies:
+        copy.wait()
+    out_ref[...] = landed[...]
+
+
+def exchange_faces(grid_cells):
+    ncomp, len_x, len_y, len_z = grid_cells.shape
+    face = (4, ncomp, len_x, len_z)
+    return pl.pallas_call(
+        halo_kernel,
+        out_shape=jax.ShapeDtypeStruct(face, grid_cells.dtype),
+        in_specs=[pl.BlockSpec(memory_space=pl.ANY)],
+        out_specs=pl.BlockSpec(memory_space=pltpu.VMEM),
+        scratch_shapes=[
+            pltpu.VMEM(face, grid_cells.dtype),
+            pltpu.SemaphoreType.DMA((4,)),
+            pltpu.SemaphoreType.DMA((4,)),
+        ],
+        compiler_params=pltpu.CompilerParams(collective_id=1, has_side_effects=True),
+    )(grid_cells)
+
+
 def local(field_state, shell_owner, block_sources, block_targets, interp_weights):
     grid_cells = field_state[0]
     ncomp, len_x, len_y, len_z = grid_cells.shape
@@ -202,26 +239,40 @@
     stacked = interp_blocks.reshape(slots_here * ncomp * BLK * BLK, BLK)
     stacked = jnp.dot(stacked, spread, precision=lax.Precision.HIGHEST)
     stacked = stacked.reshape(slots_here, ncomp, BLK, BLK, len_z)
+    targets = jnp.where(domain == 1, block_targets[0, 0], -1)
+    spots = jnp.maximum(targets, 0)
+    hit = (
+        (rows[None] == (spots // (per_y * per_z))[:, None, None, None])
+        & (cols[None] == (spots // per_z % per_y)[:, None, None, None])
+        & (lanes[None] // BLK == (spots % per_z)[:, None, None, None])
+        & (targets >= 0)[:, None, None, None]
+    )
     for slot_number in range(slots_here):
-        target_block = block_targets[0, 0, slot_number]
-        target_block = jnp.where(domain == 1, target_block, -1)
-        block_spot = jnp.maximum(target_block, 0)
-        hit = (
-            (rows == block_spot // (per_y * per_z))
-            & (cols == block_spot // per_z % per_y)
-            & (lanes // BLK == block_spot % per_z)
-            & (target_block >= 0)
-        )
         placed = jnp.tile(stacked[slot_number], (1, len_x // BLK, len_y // BLK, 1))
-        grid_cells = jnp.where(hit[None], placed, grid_cells)
+        grid_cells = jnp.where(hit[slot_number][None], placed, grid_cells)
 
     helio_side = domain == 1
     low_x = helio_side & (column == 0)
     high_x = helio_side & (column == gx_count - 1)
     low_y = yz_index == 0
     high_y = yz_index == yz_count - 1
-    line_x = ghost_pair(grid_cells, "gx", 1, True, low_x, high_x)
-    line_y = ghost_pair(grid_cells, "yz", 2, False, low_y, high_y)
+    ghosts = exchange_faces(grid_cells)
+    from_low_x, from_high_x, from_low_y, from_high_y = (
+        lax.expand_dims(ghosts[0], (1,)),
+        lax.expand_dims(ghosts[1], (1,)),
+        lax.expand_dims(ghosts[2], (2,)),
+        lax.expand_dims(ghosts[3], (2,)),
+    )
+    head_x, tail_x = grid_cells[:, :1], grid_cells[:, -1:]
+    head_y, tail_y = grid_cells[:, :, :1], grid_cells[:, :, -1:]
+    line_x = jnp.concatenate(
+        [jnp.where(low_x, head_x, from_low_x), grid_cells, jnp.where(high_x, tail_x, from_high_x)],
+        axis=1,
+    )
+    line_y = jnp.concatenate(
+        [jnp.where(low_y, head_y, from_low_y), grid_cells, jnp.where(high_y, tail_y, from_high_y)],
+        axis=2,
+    )
     line_z = jnp.pad(grid_cells, ((0, 0), (0, 0), (0, 0), (1, 1)), mode="edge")
     step_ratio = jnp.where(domain == 0, CORONA_RATIO, HELIO_RATIO).astype(jnp.float32)
     updated = advance((line_x, line_y, line_z), grid_cells, step_ratio)

time: 50.7 us -> 52.8 us (1.041)
  the two profiles are of different devices: /device:TPU:9 before, /device:TPU:1 now
where the time goes in v5:
time: 52.8 us; the launch traced here: 52.5 us
  Pallas kernels  22 us (42%)
  other arithmetic  15.6 us (30%)
  local copies, waits for them, and re-layouts  8.77 us (17%)
  matrix products  5.57 us (11%)
    pallas_call x1, Pallas kernels, exchange_faces(): pl.pallas_call(halo_kernel, out_shape=jax.ShapeDtypeStruct(face, grid_cel...  12.8 us
    pallas_call x1, Pallas kernels, route_blocks(): pl.pallas_call(route_kernel, out_shape=jax.ShapeDtypeStruct(send_cells.sh...  9.19 us
    dot_general x1, matrix products, local(): jnp.einsum('jkcs,jkst->jct', picked, interp_weights[0, 0], preferred_elem...  4.56 us
    sub x3, other arithmetic, interface_change(): 0.5 * (low_flux + high_flux)  4.55 us
    broadcast_in_dim x1, other arithmetic, local(): return updated[None]  4.15 us
    convert_element_type x3, local copies, waits for them, and re-layouts, local(): shell_cells.transpose(1, 3, 5, 0, 2, 4, 6).reshape(-1, ncomp * volume)  2.12 us
    select_n x1, other arithmetic, local(): grid_cells = jnp.where(hit[slot_number][None], placed, grid_cells)  1.91 us
    slice x1, local copies, waits for them, and re-layouts, local(): shell_cells = grid_cells[:, :, :, len_z - SR * BLK:]  1.43 us

profile of v5, /device:TPU:1, one launch (start us, length us, event | category | flops | bytes accessed | tf_op | source)
XLA Modules:
  0.0 52.5 jit_solution(8298453423719608334)
XLA Ops:
  0.0 1.4 %slice.657 = bf16[8,16,16,16]{3,2,1,0:T(8,128)(2,1)S(1)} slice(f32[8,16,16,128]{3,2,1,0:T(8,128)} %bitcast.219), slice={[0:8], [0:16], [0:16], [112:128]} | slice | bytes 131072 | tf_op jit(solution)/shard_map/slice | solution.py:194
  1.4 0.4 convert_element_type.28
  1.9 0.2 copy.11
  2.1 1.5 %convert_element_type.30 = bf16[8,4096]{1,0:T(8,128)(2,1)S(1)} reshape(bf16[2,2,2,8,8,8,8]{6,5,4,3,2,1,0:T(8,128)(2,1)S(1)} %bitcast.218) | data formatting | bytes 131072 | tf_op jit(solution)/shard_map/convert_element_type | solution.py:197
  3.6 0.2 convert_reduce_fusion
  3.8 0.2 convolution_convert_fusion.1
  4.0 0.7 %reshape.303.send_ref = bf16[8,16,512]{2,1,0:T(8,128)(2,1)} reshape(bf16[16,4096]{1,0:T(8,128)(2,1)S(1)} %convolution_convert_fusion.1) | data formatting | bytes 262144 | tf_op jit(solution)/shard_map/reshape | solution.py:213
  4.7 9.2 %shard_map.55 = bf16[8,16,512]{2,1,0:T(8,128)(2,1)} custom-call(bf16[8,16,512]{2,1,0:T(8,128)(2,1)} %reshape.303.send_ref), custom_call_target="tpu_custom_call" | custom-call | tf_op jit(solution)/shard_map/pallas_call | solution.py:115
  13.9 1.0 %reshape.304 = bf16[16,4096]{1,0:T(8,128)(2,1)S(1)} reshape(bf16[8,16,512]{2,1,0:T(8,128)(2,1)} %shard_map.55) | data formatting | bytes 262144 | tf_op jit(solution)/shard_map/reshape | solution.py:214
  14.9 0.1 convert_reduce_fusion.1
  15.0 0.2 reduce-window.8
  15.3 0.1 select_n.159
  15.3 0.1 eq.124
  15.4 0.2 convolution_convert_fusion
  15.7 4.6 %fusion.8 = f32[4,8,512]{2,1,0:T(8,128)S(1)} fusion(bf16[4,4,8,512]{3,2,1,0:T(8,128)(2,1)S(1)} %bitcast.224, bf16[1,1,4,4,512,512]{5,4,3,2,1,0:T(8,128)(2,1)} %param.9), kind=kOutput, calls=%fused_computation.17 | convolution fusion | flops 67108864 | bytes 8585216 | tf_op jit(solution)/shard_map/jkcs,jkst->jct/dot_general | solution.py:229
  20.3 0.6 %reshape.306 = f32[2048,8]{1,0:T(8,128)S(1)} reshape(f32[4,8,512]{2,1,0:T(8,128)S(1)} %fusion.8) | data formatting | bytes 131072 | tf_op jit(solution)/shard_map/reshape | solution.py:239
  20.9 0.6 %fusion.83 = f32[2048,128]{1,0:T(8,128)S(1)} fusion(f32[2048,8]{1,0:T(8,128)S(1)} %reshape.306, s32[128]{0:T(128)S(1)} %get-tuple-element.46, s32[128]{0:T(128)S(1)} %get-tuple-element.47, pred[128]{0:T(512)(128)(4,1)S(1)} %compare_and_fusion), kind=kOutput, calls=%fused_computation.174 | convolution fusion | flops 25167872 | bytes 1115264 | tf_op jit(solution)/shard_map/dot_general | solution.py:240
  21.6 0.1 tile.41
  21.9 1.1 %tile.50 = f32[8,2,8,2,8,128]{5,4,3,2,1,0:T(8,128)} broadcast(f32[8,8,8,128]{3,2,1,0:T(8,128)S(1)} %bitcast.220), dimensions={0,2,4,5} | broadcast | bytes 1310720 | tf_op jit(solution)/shard_map/tile | solution.py:251
  23.0 0.1 broadcast_select_fusion.3
  23.2 0.2 and_and_fusion
  23.4 1.9 %select_select_fusion.grid_ref = f32[8,16,16,128]{3,2,1,0:T(8,128)S(1)} fusion(f32[8,16,16,128]{3,2,1,0:T(8,128)S(1)} %bitcast.214, f32[8,16,16,128]{3,2,1,0:T(8,128)S(1)} %bitcast.215, f32[8,16,16,128]{3,2,1,0:T(8,128)S(1)} %bitcast.216, f32[8,16,16,128]{3,2,1,0:T(8,128)} %bitcast.217, pred[16,16,128]{2,1,0:T(8,128)(4,1)S(1)} %get-tuple-element.38, ...), kind=kLoop, calls=%fused_computation.33 | loop fusion | flops 1048576 | bytes 6422528 | tf_op jit(solution)/shard_map/jit(_where)/select_n | solution.py:252
  25.3 0.4 fusion.90
  25.7 0.9 %pad_maximum_fusion = f32[8,16,16,130]{3,2,1,0:T(8,128)S(1)} fusion(f32[8,16,16,1]{3,2,1,0:T(8,128)S(1)} %get-tuple-element.30, f32[8,16,16,128]{3,2,1,0:T(8,128)S(1)} %select_select_fusion.grid_ref, f32[8,16,16,1]{3,2,1,0:T(8,128)S(1)} %get-tuple-element.29), kind=kLoop, calls=%fused_computation.7 | loop fusion | flops 532480 | bytes 2129920 | tf_op jit(solution)/shard_map/jit(_pad)/concatenate | solution.py:276
  26.6 0.3 multiply_reduce_fusion
  26.9 0.1 fusion.27
  27.0 0.1 fusion.25
  27.1 0.2 add_dynamic-update-slice_fusion
  27.3 0.1 fusion.23
  27.4 0.1 fusion.21
  27.5 0.2 fusion.35
  27.7 0.2 fusion.33
  27.9 0.1 fusion.19
  28.0 2.5 %fusion.3 = f32[8,16,16,129]{3,2,1,0:T(8,128)} fusion(f32[8,16,16,130]{3,2,1,0:T(8,128)S(1)} %fusion.35, f32[8,16,16,1]{3,2,1,0:T(8,128)S(1)} %get-tuple-element.30, f32[8,16,16,128]{3,2,1,0:T(8,128)S(1)} %select_select_fusion.grid_ref, f32[8,16,16,1]{3,2,1,0:T(8,128)S(1)} %get-tuple-element.29, f32[16,16,129]{2,1,0:T(8,128)S(1)} %fusion.19), kind=kLoop, calls=%fused_computation.6 | loop fusion | flops 1849344 | bytes 4367360 | tf_op jit(solution)/shard_map/sub | solution.py:58
  30.5 12.8 %shard_map.56 = f32[4,8,16,128]{3,2,1,0:T(8,128)} custom-call(f32[8,16,16,128]{3,2,1,0:T(8,128)} %copy-done), custom_call_target="tpu_custom_call" | custom-call | tf_op jit(solution)/shard_map/pallas_call | solution.py:169
  43.3 0.9 %fusion.92 = (f32[1,8,16,128]{3,2,1,0:T(8,128)S(1)}, f32[1,8,16,128]{3,2,1,0:T(8,128)S(1)}) fusion(f32[4,8,16,128]{3,2,1,0:T(8,128)} %shard_map.56), kind=kLoop, calls=%fused_computation.204 | loop fusion | bytes 262144 | tf_op jit(solution)/shard_map/slice | solution.py:263
  44.2 0.1 broadcast_select_fusion.1
  44.4 0.3 pad_maximum_fusion.1
  44.7 0.2 multiply_reduce_fusion.3
  44.9 0.1 add_dynamic-update-slice_fusion.1
  45.2 0.1 fusion.53
  45.3 0.1 fusion.51
  45.5 1.8 %fusion.6 = f32[8,16,17,128]{3,2,1,0:T(8,128)} fusion(f32[8,16,18,128]{3,2,1,0:T(8,128)S(1)} %fusion.53, f32[8,16,1,128]{3,2,1,0:T(1,128)S(1)} %get-tuple-element.28, f32[8,16,16,128]{3,2,1,0:T(8,128)S(1)} %copy-done.1, f32[8,16,1,128]{3,2,1,0:T(1,128)S(1)} %get-tuple-element.27, f32[16,17,128]{2,1,0:T(8,128)S(1)} %fusion.37), kind=kLoop, calls=%fused_computation.12 | loop fusion | flops 1949696 | bytes 4661248 | tf_op jit(solution)/shard_map/sub | solution.py:58
  47.3 0.1 pad_maximum_fusion.2
  47.4 0.1 multiply_reduce_fusion.6
  47.9 0.1 fusion.68
  48.0 0.3 fusion.12
  48.3 4.1 %fusion.17 = f32[1,8,16,16,128]{4,3,2,1,0:T(8,128)} fusion(f32[8,16,16,128]{3,2,1,0:T(8,128)S(1)} %copy-done.1, f32[8,16,16,129]{3,2,1,0:T(8,128)} %fusion.3, f32[8,16,17,128]{3,2,1,0:T(8,128)} %fusion.6, f32[8,17,16,128]{3,2,1,0:T(8,128)S(1)} %fusion.12, f32[]{:T(128)S(6)} %select_n.166), kind=kLoop, calls=%fused_computation.27 | loop fusion | flops 1835008 | bytes 8388612 | tf_op jit(solution)/shard_map/broadcast_in_dim | solution.py:279
  (48 shorter events, 1.2 us)
Async XLA Ops:
  1.8 1.8 %copy-start.3 = (s32[1,8,8]{2,1,0:T(8,128)S(1)}, s32[1,8,8]{2,1,0:T(8,128)}, u32[]{:S(2)}) copy-start(s32[1,8,8]{2,1,0:T(8,128)} %param.6) | copy-start | bytes 772
  2.1 13.2 %copy-start.4 = (s32[1,1,4,4]{3,2,1,0:T(4,128)S(1)}, s32[1,1,4,4]{3,2,1,0:T(4,128)}, u32[]{:S(2)}) copy-start(s32[1,1,4,4]{3,2,1,0:T(4,128)} %param.7) | copy-start | bytes 196
  21.8 1.3 %copy-start.5 = (s32[1,1,4]{2,1,0:T(1,128)S(1)}, s32[1,1,4]{2,1,0:T(1,128)}, u32[]{:S(2)}) copy-start(s32[1,1,4]{2,1,0:T(1,128)} %param.8) | copy-start | bytes 52
  25.3 2.7 %copy-start = (f32[8,16,16,128]{3,2,1,0:T(8,128)}, f32[8,16,16,128]{3,2,1,0:T(8,128)S(1)}, u32[]{:S(2)}) copy-start(f32[8,16,16,128]{3,2,1,0:T(8,128)S(1)} %select_select_fusion.grid_ref) | copy-start | bytes 3145732
  30.5 13.7 %copy-start.1 = (f32[8,16,16,128]{3,2,1,0:T(8,128)S(1)}, f32[8,16,16,128]{3,2,1,0:T(8,128)}, u32[]{:S(2)}) copy-start(f32[8,16,16,128]{3,2,1,0:T(8,128)} %copy-done) | copy-start | bytes 3145732
  45.5 1.8 %copy-start.2 = (f32[4,8,16,128]{3,2,1,0:T(8,128)S(1)}, f32[4,8,16,128]{3,2,1,0:T(8,128)}, u32[]{:S(2)}) copy-start(f32[4,8,16,128]{3,2,1,0:T(8,128)} %shard_map.56) | copy-start | bytes 786436

commit v6 on v5

--- a/solution.py
+++ b/solution.py
@@ -169,7 +169,7 @@
     return pl.pallas_call(
         halo_kernel,
         out_shape=jax.ShapeDtypeStruct(face, grid_cells.dtype),
-        in_specs=[pl.BlockSpec(memory_space=pl.ANY)],
+        in_specs=[pl.BlockSpec(memory_space=pltpu.VMEM)],
         out_specs=pl.BlockSpec(memory_space=pltpu.VMEM),
         scratch_shapes=[
             pltpu.VMEM(face, grid_cells.dtype),

time: 52.8 us -> 53.8 us (1.019)
  Pallas kernels: 22 us -> 23.1 us
    pallas_call x1, Pallas kernels: 12.8 us -> 13.9 us  [exchange_faces(): pl.pallas_call(halo_kernel, out_shape=jax.ShapeDtypeStruct(face, grid_cel...]
where the time goes in v6:
time: 53.8 us; the launch traced here: 53.5 us
  Pallas kernels  23.1 us (43%)
  other arithmetic  15.6 us (29%)
  local copies, waits for them, and re-layouts  8.77 us (16%)
  matrix products  5.57 us (10%)
    pallas_call x1, Pallas kernels, exchange_faces(): pl.pallas_call(halo_kernel, out_shape=jax.ShapeDtypeStruct(face, grid_cel...  13.9 us
    pallas_call x1, Pallas kernels, route_blocks(): pl.pallas_call(route_kernel, out_shape=jax.ShapeDtypeStruct(send_cells.sh...  9.19 us
    dot_general x1, matrix products, local(): jnp.einsum('jkcs,jkst->jct', picked, interp_weights[0, 0], preferred_elem...  4.56 us
    sub x3, other arithmetic, interface_change(): 0.5 * (low_flux + high_flux)  4.55 us
    broadcast_in_dim x1, other arithmetic, local(): return updated[None]  4.15 us
    convert_element_type x3, local copies, waits for them, and re-layouts, local(): shell_cells.transpose(1, 3, 5, 0, 2, 4, 6).reshape(-1, ncomp * volume)  2.12 us
    select_n x1, other arithmetic, local(): grid_cells = jnp.where(hit[slot_number][None], placed, grid_cells)  1.91 us
    slice x1, local copies, waits for them, and re-layouts, local(): shell_cells = grid_cells[:, :, :, len_z - SR * BLK:]  1.43 us

profile of v6, /device:TPU:1, one launch (start us, length us, event | category | flops | bytes accessed | tf_op | source)
XLA Modules:
  0.0 53.5 jit_solution(8320630567089991622)
XLA Ops:
  0.0 1.4 %slice.657 = bf16[8,16,16,16]{3,2,1,0:T(8,128)(2,1)S(1)} slice(f32[8,16,16,128]{3,2,1,0:T(8,128)} %bitcast.219), slice={[0:8], [0:16], [0:16], [112:128]} | slice | bytes 131072 | tf_op jit(solution)/shard_map/slice | solution.py:194
  1.4 0.4 convert_element_type.28
  1.9 0.2 copy.11
  2.1 1.5 %convert_element_type.30 = bf16[8,4096]{1,0:T(8,128)(2,1)S(1)} reshape(bf16[2,2,2,8,8,8,8]{6,5,4,3,2,1,0:T(8,128)(2,1)S(1)} %bitcast.218) | data formatting | bytes 131072 | tf_op jit(solution)/shard_map/convert_element_type | solution.py:197
  3.6 0.2 convert_reduce_fusion
  3.8 0.2 convolution_convert_fusion.1
  4.0 0.7 %reshape.303.send_ref = bf16[8,16,512]{2,1,0:T(8,128)(2,1)} reshape(bf16[16,4096]{1,0:T(8,128)(2,1)S(1)} %convolution_convert_fusion.1) | data formatting | bytes 262144 | tf_op jit(solution)/shard_map/reshape | solution.py:213
  4.7 9.2 %shard_map.55 = bf16[8,16,512]{2,1,0:T(8,128)(2,1)} custom-call(bf16[8,16,512]{2,1,0:T(8,128)(2,1)} %reshape.303.send_ref), custom_call_target="tpu_custom_call" | custom-call | tf_op jit(solution)/shard_map/pallas_call | solution.py:115
  13.9 1.0 %reshape.304 = bf16[16,4096]{1,0:T(8,128)(2,1)S(1)} reshape(bf16[8,16,512]{2,1,0:T(8,128)(2,1)} %shard_map.55) | data formatting | bytes 262144 | tf_op jit(solution)/shard_map/reshape | solution.py:214
  14.9 0.1 convert_reduce_fusion.1
  15.0 0.2 reduce-window.8
  15.3 0.1 select_n.159
  15.3 0.1 eq.124
  15.4 0.2 convolution_convert_fusion
  15.7 4.6 %fusion.8 = f32[4,8,512]{2,1,0:T(8,128)S(1)} fusion(bf16[4,4,8,512]{3,2,1,0:T(8,128)(2,1)S(1)} %bitcast.224, bf16[1,1,4,4,512,512]{5,4,3,2,1,0:T(8,128)(2,1)} %param.9), kind=kOutput, calls=%fused_computation.17 | convolution fusion | flops 67108864 | bytes 8585216 | tf_op jit(solution)/shard_map/jkcs,jkst->jct/dot_general | solution.py:229
  20.3 0.6 %reshape.306 = f32[2048,8]{1,0:T(8,128)S(1)} reshape(f32[4,8,512]{2,1,0:T(8,128)S(1)} %fusion.8) | data formatting | bytes 131072 | tf_op jit(solution)/shard_map/reshape | solution.py:239
  20.9 0.6 %fusion.83 = f32[2048,128]{1,0:T(8,128)S(1)} fusion(f32[2048,8]{1,0:T(8,128)S(1)} %reshape.306, s32[128]{0:T(128)S(1)} %get-tuple-element.46, s32[128]{0:T(128)S(1)} %get-tuple-element.47, pred[128]{0:T(512)(128)(4,1)S(1)} %compare_and_fusion), kind=kOutput, calls=%fused_computation.174 | convolution fusion | flops 25167872 | bytes 1115264 | tf_op jit(solution)/shard_map/dot_general | solution.py:240
  21.6 0.1 tile.41
  21.9 1.1 %tile.50 = f32[8,2,8,2,8,128]{5,4,3,2,1,0:T(8,128)} broadcast(f32[8,8,8,128]{3,2,1,0:T(8,128)S(1)} %bitcast.220), dimensions={0,2,4,5} | broadcast | bytes 1310720 | tf_op jit(solution)/shard_map/tile | solution.py:251
  23.0 0.1 broadcast_select_fusion.3
  23.2 0.2 and_and_fusion
  23.4 1.9 %select_select_fusion.grid_ref = f32[8,16,16,128]{3,2,1,0:T(8,128)S(1)} fusion(f32[8,16,16,128]{3,2,1,0:T(8,128)S(1)} %bitcast.214, f32[8,16,16,128]{3,2,1,0:T(8,128)S(1)} %bitcast.215, f32[8,16,16,128]{3,2,1,0:T(8,128)S(1)} %bitcast.216, f32[8,16,16,128]{3,2,1,0:T(8,128)} %bitcast.217, pred[16,16,128]{2,1,0:T(8,128)(4,1)S(1)} %get-tuple-element.38, ...), kind=kLoop, calls=%fused_computation.33 | loop fusion | flops 1048576 | bytes 6422528 | tf_op jit(solution)/shard_map/jit(_where)/select_n | solution.py:252
  25.3 0.4 fusion.90
  25.7 0.9 %pad_maximum_fusion = f32[8,16,16,130]{3,2,1,0:T(8,128)S(1)} fusion(f32[8,16,16,1]{3,2,1,0:T(8,128)S(1)} %get-tuple-element.30, f32[8,16,16,128]{3,2,1,0:T(8,128)S(1)} %select_select_fusion.grid_ref, f32[8,16,16,1]{3,2,1,0:T(8,128)S(1)} %get-tuple-element.29), kind=kLoop, calls=%fused_computation.7 | loop fusion | flops 532480 | bytes 2129920 | tf_op jit(solution)/shard_map/jit(_pad)/concatenate | solution.py:276
  26.6 0.3 multiply_reduce_fusion
  26.9 0.1 fusion.27
  27.0 0.1 fusion.25
  27.1 0.2 add_dynamic-update-slice_fusion
  27.3 0.1 fusion.23
  27.4 0.1 fusion.21
  27.5 0.2 fusion.35
  27.7 0.2 fusion.33
  27.9 0.1 fusion.19
  28.0 2.5 %fusion.3 = f32[8,16,16,129]{3,2,1,0:T(8,128)} fusion(f32[8,16,16,130]{3,2,1,0:T(8,128)S(1)} %fusion.35, f32[8,16,16,1]{3,2,1,0:T(8,128)S(1)} %get-tuple-element.30, f32[8,16,16,128]{3,2,1,0:T(8,128)S(1)} %select_select_fusion.grid_ref, f32[8,16,16,1]{3,2,1,0:T(8,128)S(1)} %get-tuple-element.29, f32[16,16,129]{2,1,0:T(8,128)S(1)} %fusion.19), kind=kLoop, calls=%fused_computation.6 | loop fusion | flops 1849344 | bytes 4367360 | tf_op jit(solution)/shard_map/sub | solution.py:58
  30.5 13.9 %shard_map.56 = f32[4,8,16,128]{3,2,1,0:T(8,128)} custom-call(f32[8,16,16,128]{3,2,1,0:T(8,128)} %copy-done), custom_call_target="tpu_custom_call" | custom-call | tf_op jit(solution)/shard_map/pallas_call | solution.py:169
  44.4 0.9 %fusion.92 = (f32[1,8,16,128]{3,2,1,0:T(8,128)S(1)}, f32[1,8,16,128]{3,2,1,0:T(8,128)S(1)}) fusion(f32[4,8,16,128]{3,2,1,0:T(8,128)} %shard_map.56), kind=kLoop, calls=%fused_computation.204 | loop fusion | bytes 262144 | tf_op jit(solution)/shard_map/slice | solution.py:263
  45.3 0.1 broadcast_select_fusion.1
  45.4 0.3 pad_maximum_fusion.1
  45.7 0.2 multiply_reduce_fusion.3
  46.0 0.1 add_dynamic-update-slice_fusion.1
  46.3 0.1 fusion.53
  46.4 0.1 fusion.51
  46.6 1.8 %fusion.6 = f32[8,16,17,128]{3,2,1,0:T(8,128)} fusion(f32[8,16,18,128]{3,2,1,0:T(8,128)S(1)} %fusion.53, f32[8,16,1,128]{3,2,1,0:T(1,128)S(1)} %get-tuple-element.28, f32[8,16,16,128]{3,2,1,0:T(8,128)S(1)} %copy-done.1, f32[8,16,1,128]{3,2,1,0:T(1,128)S(1)} %get-tuple-element.27, f32[16,17,128]{2,1,0:T(8,128)S(1)} %fusion.37), kind=kLoop, calls=%fused_computation.12 | loop fusion | flops 1949696 | bytes 4661248 | tf_op jit(solution)/shard_map/sub | solution.py:58
  48.4 0.1 pad_maximum_fusion.2
  48.5 0.1 multiply_reduce_fusion.6
  49.0 0.1 fusion.68
  49.1 0.3 fusion.12
  49.4 4.1 %fusion.17 = f32[1,8,16,16,128]{4,3,2,1,0:T(8,128)} fusion(f32[8,16,16,128]{3,2,1,0:T(8,128)S(1)} %copy-done.1, f32[8,16,16,129]{3,2,1,0:T(8,128)} %fusion.3, f32[8,16,17,128]{3,2,1,0:T(8,128)} %fusion.6, f32[8,17,16,128]{3,2,1,0:T(8,128)S(1)} %fusion.12, f32[]{:T(128)S(6)} %select_n.166), kind=kLoop, calls=%fused_computation.27 | loop fusion | flops 1835008 | bytes 8388612 | tf_op jit(solution)/shard_map/broadcast_in_dim | solution.py:279
  (48 shorter events, 1.2 us)
Async XLA Ops:
  1.8 1.8 %copy-start.3 = (s32[1,8,8]{2,1,0:T(8,128)S(1)}, s32[1,8,8]{2,1,0:T(8,128)}, u32[]{:S(2)}) copy-start(s32[1,8,8]{2,1,0:T(8,128)} %param.6) | copy-start | bytes 772
  2.1 13.2 %copy-start.4 = (s32[1,1,4,4]{3,2,1,0:T(4,128)S(1)}, s32[1,1,4,4]{3,2,1,0:T(4,128)}, u32[]{:S(2)}) copy-start(s32[1,1,4,4]{3,2,1,0:T(4,128)} %param.7) | copy-start | bytes 196
  21.8 1.3 %copy-start.5 = (s32[1,1,4]{2,1,0:T(1,128)S(1)}, s32[1,1,4]{2,1,0:T(1,128)}, u32[]{:S(2)}) copy-start(s32[1,1,4]{2,1,0:T(1,128)} %param.8) | copy-start | bytes 52
  25.3 2.7 %copy-start = (f32[8,16,16,128]{3,2,1,0:T(8,128)}, f32[8,16,16,128]{3,2,1,0:T(8,128)S(1)}, u32[]{:S(2)}) copy-start(f32[8,16,16,128]{3,2,1,0:T(8,128)S(1)} %select_select_fusion.grid_ref) | copy-start | bytes 3145732
  30.5 14.8 %copy-start.1 = (f32[8,16,16,128]{3,2,1,0:T(8,128)S(1)}, f32[8,16,16,128]{3,2,1,0:T(8,128)}, u32[]{:S(2)}) copy-start(f32[8,16,16,128]{3,2,1,0:T(8,128)} %copy-done) | copy-start | bytes 3145732
  46.6 1.8 %copy-start.2 = (f32[4,8,16,128]{3,2,1,0:T(8,128)S(1)}, f32[4,8,16,128]{3,2,1,0:T(8,128)}, u32[]{:S(2)}) copy-start(f32[4,8,16,128]{3,2,1,0:T(8,128)} %shard_map.56) | copy-start | bytes 786436

commit v7 on v4

--- a/solution.py
+++ b/solution.py
@@ -65,23 +65,6 @@
     change = interface_change(line_set[0], 0) + interface_change(line_set[1], 1)
     change = change + interface_change(line_set[2], 2)
     return inner_cells - step_ratio * change
-
-
-def ghost_pair(cells, axis, dim, wrap, fix_low, fix_high):
-    count = lax.axis_size(axis)
-    size = cells.shape[dim]
-    head = lax.slice_in_dim(cells, 0, 1, axis=dim)
-    tail = lax.slice_in_dim(cells, size - 1, size, axis=dim)
-    up = [(i, i + 1) for i in range(count - 1)]
-    down = [(i + 1, i) for i in range(count - 1)]
-    if wrap:
-        up.append((count - 1, 0))
-        down.append((0, count - 1))
-    from_low = lax.ppermute(tail, axis, up)
-    from_high = lax.ppermute(head, axis, down)
-    low = jnp.where(fix_low, head, from_low)
-    high = jnp.where(fix_high, tail, from_high)
-    return jnp.concatenate([low, cells, high], axis=dim)
 
 
 def route_kernel(send_ref, out_ref, landed, send_sem, recv_sem):
@@ -143,6 +126,23 @@
     )(send_cells)
 
 
+def ghost_pair(cells, axis, dim, wrap, fix_low, fix_high):
+    count = lax.axis_size(axis)
+    size = cells.shape[dim]
+    head = lax.slice_in_dim(cells, 0, 1, axis=dim)
+    tail = lax.slice_in_dim(cells, size - 1, size, axis=dim)
+    up = [(i, i + 1) for i in range(count - 1)]
+    down = [(i + 1, i) for i in range(count - 1)]
+    if wrap:
+        up.append((count - 1, 0))
+        down.append((0, count - 1))
+    from_low = lax.ppermute(tail, axis, up)
+    from_high = lax.ppermute(head, axis, down)
+    low = jnp.where(fix_low, head, from_low)
+    high = jnp.where(fix_high, tail, from_high)
+    return jnp.concatenate([low, cells, high], axis=dim)
+
+
 def local(field_state, shell_owner, block_sources, block_targets, interp_weights):
     grid_cells = field_state[0]
     ncomp, len_x, len_y, len_z = grid_cells.shape
@@ -202,18 +202,17 @@
     stacked = interp_blocks.reshape(slots_here * ncomp * BLK * BLK, BLK)
     stacked = jnp.dot(stacked, spread, precision=lax.Precision.HIGHEST)
     stacked = stacked.reshape(slots_here, ncomp, BLK, BLK, len_z)
+    targets = jnp.where(domain == 1, block_targets[0, 0], -1)
+    spots = jnp.maximum(targets, 0)
+    hit = (
+        (rows[None] == (spots // (per_y * per_z))[:, None, None, None])
+        & (cols[None] == (spots // per_z % per_y)[:, None, None, None])
+        & (lanes[None] // BLK == (spots % per_z)[:, None, None, None])
+        & (targets >= 0)[:, None, None, None]
+    )
     for slot_number in range(slots_here):
-        target_block = block_targets[0, 0, slot_number]
-        target_block = jnp.where(domain == 1, target_block, -1)
-        block_spot = jnp.maximum(target_block, 0)
-        hit = (
-            (rows == block_spot // (per_y * per_z))
-            & (cols == block_spot // per_z % per_y)
-            & (lanes // BLK == block_spot % per_z)
-            & (target_block >= 0)
-        )
         placed = jnp.tile(stacked[slot_number], (1, len_x // BLK, len_y // BLK, 1))
-        grid_cells = jnp.where(hit[None], placed, grid_cells)
+        grid_cells = jnp.where(hit[slot_number][None], placed, grid_cells)
 
     helio_side = domain == 1
     low_x = helio_side & (column == 0)

time: 50.7 us -> 47.1 us (0.929)
  between operations: 3.26 us -> 0.52 us
  local copies, waits for them, and re-layouts: 10.1 us -> 9.23 us
    slice x1 -> x0, local copies, waits for them, and re-layouts: 1.47 us -> none  [local(): target_block = block_targets[0, 0, slot_number]]
    unnamed x7 -> x9, local copies, waits for them, and re-layouts: 1.1 us -> 1.67 us
where the time goes in v7:
time: 47.1 us; the launch traced here: 46.7 us
  starting transfers between devices  13.2 us (28%)
  other arithmetic  9.78 us (21%)
  local copies, waits for them, and re-layouts  9.23 us (20%)
  Pallas kernels  8.43 us (18%)
  matrix products  5.58 us (12%)
  between operations  0.52 us (1%)
    ppermute x2, starting transfers between devices, ghost_pair(): from_high = lax.ppermute(head, axis, down)  8.64 us
    pallas_call x1, Pallas kernels, route_blocks(): pl.pallas_call(route_kernel, out_shape=jax.ShapeDtypeStruct(send_cells.sh...  8.43 us
    dot_general x1, matrix products, local(): jnp.einsum('jkcs,jkst->jct', picked, interp_weights[0, 0], preferred_elem...  4.56 us
    ppermute x2, starting transfers between devices, ghost_pair(): from_low = lax.ppermute(tail, axis, up)  4.56 us
    convert_element_type x3, local copies, waits for them, and re-layouts, local(): shell_cells.transpose(1, 3, 5, 0, 2, 4, 6).reshape(-1, ncomp * volume)  2.12 us
    sub x3, other arithmetic, interface_change(): 0.5 * (low_flux + high_flux)  2.01 us
    unnamed x9, local copies, waits for them, and re-layouts  1.67 us
    broadcast_in_dim x1, other arithmetic, local(): return updated[None]  1.54 us
  transfers between devices with their start and end apart: 4, of which 0 were waited for; matrix products, arithmetic and copies ran while one was open for 12% of the time, Pallas kernels for 0%

profile of v7, /device:TPU:9, one launch (start us, length us, event | category | flops | bytes accessed | tf_op | source)
XLA Modules:
  0.0 46.7 jit_solution(756237901086914401)
XLA Ops:
  0.1 1.4 %slice.639 = bf16[8,16,16,16]{3,2,1,0:T(8,128)(2,1)S(1)} slice(f32[8,16,16,128]{3,2,1,0:T(8,128)} %bitcast.213), slice={[0:8], [0:16], [0:16], [112:128]} | slice | bytes 131072 | tf_op jit(solution)/shard_map/slice | solution.py:157
  1.5 0.4 convert_element_type.28
  1.9 0.2 copy.11
  2.2 1.5 %convert_element_type.30 = bf16[8,4096]{1,0:T(8,128)(2,1)S(1)} reshape(bf16[2,2,2,8,8,8,8]{6,5,4,3,2,1,0:T(8,128)(2,1)S(1)} %bitcast.212) | data formatting | bytes 131072 | tf_op jit(solution)/shard_map/convert_element_type | solution.py:160
  3.7 0.1 convert_reduce_fusion.1
  3.8 0.2 convert_reduce_fusion
  4.0 0.2 convolution_convert_fusion.1
  4.1 0.7 %reshape.303.send_ref = bf16[8,16,512]{2,1,0:T(8,128)(2,1)} reshape(bf16[16,4096]{1,0:T(8,128)(2,1)S(1)} %convolution_convert_fusion.1) | data formatting | bytes 262144 | tf_op jit(solution)/shard_map/reshape | solution.py:176
  4.9 8.4 %shard_map.55 = bf16[8,16,512]{2,1,0:T(8,128)(2,1)} custom-call(bf16[8,16,512]{2,1,0:T(8,128)(2,1)} %reshape.303.send_ref), custom_call_target="tpu_custom_call" | custom-call | tf_op jit(solution)/shard_map/pallas_call | solution.py:115
  13.3 1.0 %reshape.304 = bf16[16,4096]{1,0:T(8,128)(2,1)S(1)} reshape(bf16[8,16,512]{2,1,0:T(8,128)(2,1)} %shard_map.55) | data formatting | bytes 262144 | tf_op jit(solution)/shard_map/reshape | solution.py:177
  14.3 0.2 reduce-window.8
  14.7 0.2 convolution_convert_fusion
  15.0 4.6 %fusion.8 = f32[4,8,512]{2,1,0:T(8,128)S(1)} fusion(bf16[4,4,8,512]{3,2,1,0:T(8,128)(2,1)S(1)} %bitcast.218, bf16[1,1,4,4,512,512]{5,4,3,2,1,0:T(8,128)(2,1)} %param.9), kind=kOutput, calls=%fused_computation.17 | convolution fusion | flops 67108864 | bytes 8585216 | tf_op jit(solution)/shard_map/jkcs,jkst->jct/dot_general | solution.py:192
  19.6 0.6 %reshape.306 = f32[2048,8]{1,0:T(8,128)S(1)} reshape(f32[4,8,512]{2,1,0:T(8,128)S(1)} %fusion.8) | data formatting | bytes 131072 | tf_op jit(solution)/shard_map/reshape | solution.py:202
  20.2 0.6 %fusion.83 = f32[2048,128]{1,0:T(8,128)S(1)} fusion(f32[2048,8]{1,0:T(8,128)S(1)} %reshape.306, s32[128]{0:T(128)S(1)} %get-tuple-element.48, s32[128]{0:T(128)S(1)} %get-tuple-element.49, pred[128]{0:T(512)(128)(4,1)S(1)} %compare_and_fusion), kind=kOutput, calls=%fused_computation.174 | convolution fusion | flops 25167872 | bytes 1115264 | tf_op jit(solution)/shard_map/dot_general | solution.py:203
  20.9 0.6 %copy-done.3 = s32[1,1,4]{2,1,0:T(1,128)S(1)} copy-done((s32[1,1,4]{2,1,0:T(1,128)S(1)}, s32[1,1,4]{2,1,0:T(1,128)}, u32[]{:S(2)}) %copy-start.3) | copy-done | bytes 40
  21.5 0.1 broadcast_select_fusion.3
  21.6 0.2 and_and_fusion
  22.2 1.0 %copy-done = f32[1,8,16,16,128]{4,3,2,1,0:T(8,128)S(1)} copy-done((f32[1,8,16,16,128]{4,3,2,1,0:T(8,128)S(1)}, f32[1,8,16,16,128]{4,3,2,1,0:T(8,128)}, u32[]{:S(2)}) %copy-start) | copy-done | bytes 1048600
  23.3 0.4 select_select_fusion
  23.6 0.7 %fusion.91 = (f32[8,16,1,128]{3,2,1,0:T(1,128)}, f32[8,16,1,128]{3,2,1,0:T(1,128)S(1)}) fusion(f32[8,16,16,128]{3,2,1,0:T(8,128)S(1)} %select_select_fusion), kind=kLoop, calls=%fused_computation.203 | loop fusion | bytes 262144 | tf_op jit(solution)/shard_map/slice | solution.py:133
  24.4 2.5 %collective-permute-start.2 = (f32[8,16,1,128]{3,2,1,0:T(1,128)}, f32[8,16,1,128]{3,2,1,0:T(1,128)S(1)}, u32[]{:S(2)}, u32[]{:S(2)}) collective-permute-start(f32[8,16,1,128]{3,2,1,0:T(1,128)} %get-tuple-element.31), channel_id=1, source_target_pairs={{0,1},{1,2},{2,3},{3,4},{4,5},{5,6},{6,7},{8,9},{9,10},{10,11},{11... | collective-permute-start | bytes 196616 | tf_op jit(solution)/shard_map/ppermute | solution.py:139
  26.8 4.9 %collective-permute-start.3 = (f32[8,16,1,128]{3,2,1,0:T(1,128)S(1)}, f32[8,16,1,128]{3,2,1,0:T(1,128)}, u32[]{:S(2)}, u32[]{:S(2)}) collective-permute-start(f32[8,16,1,128]{3,2,1,0:T(1,128)S(1)} %get-tuple-element.32), channel_id=1, source_target_pairs={{1,0},{2,1},{3,2},{4,3},{5,4},{6,5},{7,6},{9,8},{10,9},{11,10},{12... | collective-permute-start | bytes 196616 | tf_op jit(solution)/shard_map/ppermute | solution.py:140
  31.8 2.1 %collective-permute-start = (f32[8,1,16,128]{3,2,1,0:T(8,128)S(1)}, f32[8,1,16,128]{3,2,1,0:T(8,128)S(1)}, u32[]{:S(2)}, u32[]{:S(2)}) collective-permute-start(f32[8,1,16,128]{3,2,1,0:T(8,128)S(1)} %get-tuple-element.27), channel_id=1, source_target_pairs={{0,8},{8,16},{16,24},{24,32},{32,40},{40,48},{48,56},{56,0},{1,9},... | collective-permute-start | bytes 196616 | tf_op jit(solution)/shard_map/ppermute | solution.py:139
  33.9 3.7 %collective-permute-start.1 = (f32[8,1,16,128]{3,2,1,0:T(8,128)S(1)}, f32[8,1,16,128]{3,2,1,0:T(8,128)S(1)}, u32[]{:S(2)}, u32[]{:S(2)}) collective-permute-start(f32[8,1,16,128]{3,2,1,0:T(8,128)S(1)} %get-tuple-element.28), channel_id=1, source_target_pairs={{8,0},{16,8},{24,16},{32,24},{40,32},{48,40},{56,48},{0,56},{9,1},... | collective-permute-start | bytes 196616 | tf_op jit(solution)/shard_map/ppermute | solution.py:140
  37.6 0.3 fusion.92
  37.9 0.9 %pad_maximum_fusion = f32[8,16,16,130]{3,2,1,0:T(8,128)S(1)} fusion(f32[8,16,16,1]{3,2,1,0:T(8,128)S(1)} %get-tuple-element.34, f32[8,16,16,128]{3,2,1,0:T(8,128)S(1)} %select_select_fusion, f32[8,16,16,1]{3,2,1,0:T(8,128)S(1)} %get-tuple-element.33), kind=kLoop, calls=%fused_computation.7 | loop fusion | flops 532480 | bytes 2129920 | tf_op jit(solution)/shard_map/jit(_pad)/concatenate | solution.py:224
  38.9 0.3 multiply_reduce_fusion
  39.2 0.1 fusion.27
  39.3 0.1 fusion.25
  39.4 0.2 fusion.33
  39.5 0.2 add_dynamic-update-slice_fusion
  39.7 0.1 fusion.23
  39.8 0.1 fusion.21
  40.0 0.1 fusion.19
  40.1 0.2 fusion.35
  40.3 1.2 %fusion.3 = f32[8,16,16,129]{3,2,1,0:T(8,128)S(1)} fusion(f32[8,16,16,130]{3,2,1,0:T(8,128)S(1)} %fusion.35, f32[8,16,16,1]{3,2,1,0:T(8,128)S(1)} %get-tuple-element.34, f32[8,16,16,128]{3,2,1,0:T(8,128)S(1)} %select_select_fusion, f32[8,16,16,1]{3,2,1,0:T(8,128)S(1)} %get-tuple-element.33, f32[16,16,129]{2,1,0:T(8,128)S(1)} %fusion.19), kind=kLoop, calls=%fused_computation.6 | loop fusion | flops 1849344 | bytes 4367360 | tf_op jit(solution)/shard_map/sub | solution.py:58
  41.5 1.0 %broadcast_select_fusion.1 = (f32[8,16,1,128]{3,2,1,0:T(1,128)S(1)}, f32[8,16,1,128]{3,2,1,0:T(1,128)S(1)}) fusion(f32[8,16,1,128]{3,2,1,0:T(1,128)S(1)} %collective-permute-done.2, pred[]{:T(512)S(6)} %eq.140, f32[8,16,16,128]{3,2,1,0:T(8,128)S(1)} %select_select_fusion, f32[8,16,1,128]{3,2,1,0:T(1,128)} %collective-permute-done.3, pred[]{:T(512)S(6)} %eq.141), kind=kLoop, calls=%fused_computation.155 | loop fusion | flops 32768 | bytes 393218 | tf_op jit(solution)/shard_map/jit(_where)/select_n | solution.py:141
  42.5 0.3 pad_maximum_fusion.1
  42.8 0.2 multiply_reduce_fusion.3
  43.1 0.1 fusion.51
  43.2 0.1 add_dynamic-update-slice_fusion.1
  43.7 0.1 multiply_reduce_fusion.6
  43.8 0.1 fusion.68
  44.2 0.1 fusion.53
  44.3 0.6 %fusion.6 = f32[8,16,17,128]{3,2,1,0:T(8,128)S(1)} fusion(f32[8,16,18,128]{3,2,1,0:T(8,128)S(1)} %fusion.53, f32[8,16,1,128]{3,2,1,0:T(1,128)S(1)} %get-tuple-element.30, f32[8,16,16,128]{3,2,1,0:T(8,128)S(1)} %select_select_fusion, f32[8,16,1,128]{3,2,1,0:T(1,128)S(1)} %get-tuple-element.29, f32[16,17,128]{2,1,0:T(8,128)S(1)} %fusion.37), kind=kLoop, calls=%fused_computation.12 | loop fusion | flops 1949696 | bytes 4661248 | tf_op jit(solution)/shard_map/sub | solution.py:58
  45.0 0.2 fusion.12
  45.2 1.5 %fusion.17 = f32[1,8,16,16,128]{4,3,2,1,0:T(8,128)} fusion(f32[8,16,16,128]{3,2,1,0:T(8,128)S(1)} %select_select_fusion, f32[8,16,16,129]{3,2,1,0:T(8,128)S(1)} %fusion.3, f32[8,16,17,128]{3,2,1,0:T(8,128)S(1)} %fusion.6, f32[8,17,16,128]{3,2,1,0:T(8,128)S(1)} %fusion.12, f32[]{:T(128)S(6)} %select_n.166), kind=kLoop, calls=%fused_computation.27 | loop fusion | flops 1835008 | bytes 8388612 | tf_op jit(solution)/shard_map/broadcast_in_dim | solution.py:227
  (52 shorter events, 1.6 us)
Async XLA Ops:
  1.9 1.8 %copy-start.1 = (s32[1,8,8]{2,1,0:T(8,128)S(1)}, s32[1,8,8]{2,1,0:T(8,128)}, u32[]{:S(2)}) copy-start(s32[1,8,8]{2,1,0:T(8,128)} %param.6) | copy-start | bytes 772
  2.2 12.5 %copy-start.2 = (s32[1,1,4,4]{3,2,1,0:T(4,128)S(1)}, s32[1,1,4,4]{3,2,1,0:T(4,128)}, u32[]{:S(2)}) copy-start(s32[1,1,4,4]{3,2,1,0:T(4,128)} %param.7) | copy-start | bytes 196
  20.8 0.7 %copy-start.3 = (s32[1,1,4]{2,1,0:T(1,128)S(1)}, s32[1,1,4]{2,1,0:T(1,128)}, u32[]{:S(2)}) copy-start(s32[1,1,4]{2,1,0:T(1,128)} %param.8) | copy-start | bytes 52
  22.0 1.2 %copy-start = (f32[1,8,16,16,128]{4,3,2,1,0:T(8,128)S(1)}, f32[1,8,16,16,128]{4,3,2,1,0:T(8,128)}, u32[]{:S(2)}) copy-start(f32[1,8,16,16,128]{4,3,2,1,0:T(8,128)} %param.5) | copy-start | bytes 3145732
  24.4 17.2 %collective-permute-start.2 = (f32[8,16,1,128]{3,2,1,0:T(1,128)}, f32[8,16,1,128]{3,2,1,0:T(1,128)S(1)}, u32[]{:S(2)}, u32[]{:S(2)}) collective-permute-start(f32[8,16,1,128]{3,2,1,0:T(1,128)} %get-tuple-element.31), channel_id=1, source_target_pairs={{0,1},{1,2},{2,3},{3,4},{4,5},{5,6},{6,7},{8,9},{9,10},{10,11},{11... | collective-permute-start | bytes 196616 | tf_op jit(solution)/shard_map/ppermute | solution.py:139
  26.8 14.7 %collective-permute-start.3 = (f32[8,16,1,128]{3,2,1,0:T(1,128)S(1)}, f32[8,16,1,128]{3,2,1,0:T(1,128)}, u32[]{:S(2)}, u32[]{:S(2)}) collective-permute-start(f32[8,16,1,128]{3,2,1,0:T(1,128)S(1)} %get-tuple-element.32), channel_id=1, source_target_pairs={{1,0},{2,1},{3,2},{4,3},{5,4},{6,5},{7,6},{9,8},{10,9},{11,10},{12... | collective-permute-start | bytes 196616 | tf_op jit(solution)/shard_map/ppermute | solution.py:140
  31.8 11.8 %collective-permute-start = (f32[8,1,16,128]{3,2,1,0:T(8,128)S(1)}, f32[8,1,16,128]{3,2,1,0:T(8,128)S(1)}, u32[]{:S(2)}, u32[]{:S(2)}) collective-permute-start(f32[8,1,16,128]{3,2,1,0:T(8,128)S(1)} %get-tuple-element.27), channel_id=1, source_target_pairs={{0,8},{8,16},{16,24},{24,32},{32,40},{40,48},{48,56},{56,0},{1,9},... | collective-permute-start | bytes 196616 | tf_op jit(solution)/shard_map/ppermute | solution.py:139
  33.9 9.7 %collective-permute-start.1 = (f32[8,1,16,128]{3,2,1,0:T(8,128)S(1)}, f32[8,1,16,128]{3,2,1,0:T(8,128)S(1)}, u32[]{:S(2)}, u32[]{:S(2)}) collective-permute-start(f32[8,1,16,128]{3,2,1,0:T(8,128)S(1)} %get-tuple-element.28), channel_id=1, source_target_pairs={{8,0},{16,8},{24,16},{32,24},{40,32},{48,40},{56,48},{0,56},{9,1},... | collective-permute-start | bytes 196616 | tf_op jit(solution)/shard_map/ppermute | solution.py:140

commit v8 on v7

--- a/solution.py
+++ b/solution.py
@@ -140,7 +140,117 @@
     from_high = lax.ppermute(head, axis, down)
     low = jnp.where(fix_low, head, from_low)
     high = jnp.where(fix_high, tail, from_high)
-    return jnp.concatenate([low, cells, high], axis=dim)
+    return lax.squeeze(low, (dim,)), lax.squeeze(high, (dim,))
+
+
+def cell_flux(parts, direction):
+    density = parts[0]
+    momentum = parts[1:4]
+    magnetic = parts[4:7]
+    energy = parts[7]
+    velocity = [m / density for m in momentum]
+    field_sq = magnetic[0] * magnetic[0] + magnetic[1] * magnetic[1] + magnetic[2] * magnetic[2]
+    kinetic = momentum[0] * velocity[0] + momentum[1] * velocity[1] + momentum[2] * velocity[2]
+    pressure = (HEAT_RATIO - 1.0) * (energy - 0.5 * kinetic - 0.5 * field_sq)
+    total_pressure = pressure + 0.5 * field_sq
+    normal_speed = velocity[direction]
+    normal_field = magnetic[direction]
+    velocity_dot = velocity[0] * magnetic[0] + velocity[1] * magnetic[1] + velocity[2] * magnetic[2]
+    flux = [momentum[direction]]
+    for other in range(3):
+        term = momentum[other] * normal_speed - magnetic[other] * normal_field
+        if other == direction:
+            term = term + total_pressure
+        flux.append(term)
+    for other in range(3):
+        flux.append(normal_speed * magnetic[other] - normal_field * velocity[other])
+    flux.append((energy + total_pressure) * normal_speed - normal_field * velocity_dot)
+    speed = jnp.abs(normal_speed) + jnp.sqrt((HEAT_RATIO * pressure + field_sq) / density)
+    return flux, speed
+
+
+def face_change(low, mid, high, low_flux, mid_flux, high_flux):
+    (fl, sl), (fm, sm), (fh, sh) = low_flux, mid_flux, high_flux
+    fast_low = jnp.maximum(sl, sm)
+    fast_high = jnp.maximum(sm, sh)
+    change = []
+    for c in range(len(mid)):
+        upper = 0.5 * (fm[c] + fh[c]) - 0.5 * fast_high * (high[c] - mid[c])
+        lower = 0.5 * (fl[c] + fm[c]) - 0.5 * fast_low * (mid[c] - low[c])
+        change.append(upper - lower)
+    return change
+
+
+def stencil_kernel(grid_ref, low_x_ref, high_x_ref, low_y_ref, high_y_ref, out_ref):
+    ncomp, len_x, len_y, len_z = grid_ref.shape
+    domain = lax.axis_index("dom")
+    ratio = jnp.where(domain == 0, CORONA_RATIO, HELIO_RATIO).astype(jnp.float32)
+    rows = lax.broadcasted_iota(jnp.int32, (len_y, len_z), 0)
+    lanes = lax.broadcasted_iota(jnp.int32, (len_y, len_z), 1)
+
+    def plane(x):
+        if x < 0:
+            return [low_x_ref[c] for c in range(ncomp)]
+        if x >= len_x:
+            return [high_x_ref[c] for c in range(ncomp)]
+        return [grid_ref[c, x] for c in range(ncomp)]
+
+    def shift(values, edge, step, axis, index, last):
+        moved = pltpu.roll(values, step, axis)
+        return jnp.where(index == last, edge, moved)
+
+    low = plane(-1)
+    mid = plane(0)
+    low_flux = cell_flux(low, 0)
+    mid_flux = cell_flux(mid, 0)
+    for x in range(len_x):
+        high = plane(x + 1)
+        high_flux = cell_flux(high, 0)
+        change = face_change(low, mid, high, low_flux, mid_flux, high_flux)
+        y_low = [low_y_ref[c, pl.ds(x, 1), :] for c in range(ncomp)]
+        y_high = [high_y_ref[c, pl.ds(x, 1), :] for c in range(ncomp)]
+        y_flux = cell_flux(mid, 1)
+        y_low_flux = cell_flux(y_low, 1)
+        y_high_flux = cell_flux(y_high, 1)
+        down = [shift(mid[c], y_low[c], 1, 0, rows, 0) for c in range(ncomp)]
+        up = [shift(mid[c], y_high[c], len_y - 1, 0, rows, len_y - 1) for c in range(ncomp)]
+        down_flux = (
+            [shift(y_flux[0][c], y_low_flux[0][c], 1, 0, rows, 0) for c in range(ncomp)],
+            shift(y_flux[1], y_low_flux[1], 1, 0, rows, 0),
+        )
+        up_flux = (
+            [shift(y_flux[0][c], y_high_flux[0][c], len_y - 1, 0, rows, len_y - 1) for c in range(ncomp)],
+            shift(y_flux[1], y_high_flux[1], len_y - 1, 0, rows, len_y - 1),
+        )
+        change_y = face_change(down, mid, up, down_flux, y_flux, up_flux)
+        z_flux = cell_flux(mid, 2)
+        back = [shift(mid[c], mid[c], 1, 1, lanes, 0) for c in range(ncomp)]
+        front = [shift(mid[c], mid[c], len_z - 1, 1, lanes, len_z - 1) for c in range(ncomp)]
+        back_flux = (
+            [shift(z_flux[0][c], z_flux[0][c], 1, 1, lanes, 0) for c in range(ncomp)],
+            shift(z_flux[1], z_flux[1], 1, 1, lanes, 0),
+        )
+        front_flux = (
+            [shift(z_flux[0][c], z_flux[0][c], len_z - 1, 1, lanes, len_z - 1) for c in range(ncomp)],
+            shift(z_flux[1], z_flux[1], len_z - 1, 1, lanes, len_z - 1),
+        )
+        change_z = face_change(back, mid, front, back_flux, z_flux, front_flux)
+        for c in range(ncomp):
+            total = change[c] + change_y[c]
+            total = total + change_z[c]
+            out_ref[c, x] = mid[c] - ratio * total
+        low, mid = mid, high
+        low_flux, mid_flux = mid_flux, high_flux
+
+
+def stencil(grid_cells, low_x, high_x, low_y, high_y):
+    vmem = pl.BlockSpec(memory_space=pltpu.VMEM)
+    return pl.pallas_call(
+        stencil_kernel,
+        out_shape=jax.ShapeDtypeStruct(grid_cells.shape, grid_cells.dtype),
+        in_specs=[vmem] * 5,
+        out_specs=vmem,
+    )(grid_cells, low_x, high_x, low_y, high_y)
 
 
 def local(field_state, shell_owner, block_sources, block_targets, interp_weights):
@@ -219,11 +329,9 @@
     high_x = helio_side & (column == gx_count - 1)
     low_y = yz_index == 0
     high_y = yz_index == yz_count - 1
-    line_x = ghost_pair(grid_cells, "gx", 1, True, low_x, high_x)
-    line_y = ghost_pair(grid_cells, "yz", 2, False, low_y, high_y)
-    line_z = jnp.pad(grid_cells, ((0, 0), (0, 0), (0, 0), (1, 1)), mode="edge")
-    step_ratio = jnp.where(domain == 0, CORONA_RATIO, HELIO_RATIO).astype(jnp.float32)
-    updated = advance((line_x, line_y, line_z), grid_cells, step_ratio)
+    ghost_low_x, ghost_high_x = ghost_pair(grid_cells, "gx", 1, True, low_x, high_x)
+    ghost_low_y, ghost_high_y = ghost_pair(grid_cells, "yz", 2, False, low_y, high_y)
+    updated = stencil(grid_cells, ghost_low_x, ghost_high_x, ghost_low_y, ghost_high_y)
     return updated[None]
 
 

time: 47.1 us -> 47.9 us (1.017)
  other arithmetic: 9.78 us -> 4.15 us
  Pallas kernels: 8.43 us -> 13.3 us
  local copies, waits for them, and re-layouts: 9.23 us -> 11.1 us
    pallas_call x0 -> x1, Pallas kernels: none -> 4.91 us  [stencil(): pl.pallas_call(stencil_kernel, out_shape=jax.ShapeDtypeStruct(grid_cells....]
    sub x3 -> x0, other arithmetic: 2.01 us -> none  [interface_change(): 0.5 * (low_flux + high_flux)]
    select_n x0 -> x1, local copies, waits for them, and re-layouts: none -> 1.57 us  [local(): grid_cells = jnp.where(hit[slot_number][None], placed, grid_cells)]
    broadcast_in_dim x1 -> x0, other arithmetic: 1.54 us -> none  [local(): return updated[None]]
    squeeze x0 -> x2, local copies, waits for them, and re-layouts: none -> 1.27 us  [ghost_pair(): return (lax.squeeze(low, (dim,)), lax.squeeze(high, (dim,)))]
    concatenate x3 -> x0, other arithmetic: 1.24 us -> none  [the longest x1 0.9 us: local(): line_z = jnp.pad(grid_cells, ((0, 0), (0, 0), (0, 0), (1, 1)), mode='edge')]
    slice x1, local copies, waits for them, and re-layouts: 1.43 us -> 0.21 us  [local(): shell_cells = grid_cells[:, :, :, len_z - SR * BLK:]]
    unnamed x18 -> x0, other arithmetic: 1.17 us -> none
  transfers between devices with their start and end apart: 4 -> 4, of which waited for: 0 -> 0; matrix products, arithmetic and copies ran while one was open for 12% -> 6% of each run, Pallas kernels for 0% -> 0%
where the time goes in v8:
time: 47.9 us; the launch traced here: 47.5 us
  Pallas kernels  13.3 us (28%)
  starting transfers between devices  13 us (27%)
  local copies, waits for them, and re-layouts  11.1 us (23%)
  matrix products  5.58 us (12%)
  other arithmetic  4.15 us (9%)
    ppermute x2, starting transfers between devices, ghost_pair(): from_high = lax.ppermute(head, axis, down)  8.46 us
    pallas_call x1, Pallas kernels, route_blocks(): pl.pallas_call(route_kernel, out_shape=jax.ShapeDtypeStruct(send_cells.sh...  8.43 us
    pallas_call x1, Pallas kernels, stencil(): pl.pallas_call(stencil_kernel, out_shape=jax.ShapeDtypeStruct(grid_cells....  4.91 us
    ppermute x2, starting transfers between devices, ghost_pair(): from_low = lax.ppermute(tail, axis, up)  4.58 us
    dot_general x1, matrix products, local(): jnp.einsum('jkcs,jkst->jct', picked, interp_weights[0, 0], preferred_elem...  4.56 us
    convert_element_type x3, local copies, waits for them, and re-layouts, local(): shell_cells.transpose(1, 3, 5, 0, 2, 4, 6).reshape(-1, ncomp * volume)  2.55 us
    unnamed x8, local copies, waits for them, and re-layouts  1.62 us
    select_n x1, local copies, waits for them, and re-layouts, local(): grid_cells = jnp.where(hit[slot_number][None], placed, grid_cells)  1.57 us
  transfers between devices with their start and end apart: 4, of which 0 were waited for; matrix products, arithmetic and copies ran while one was open for 6% of the time, Pallas kernels for 0%

profile of v8, /device:TPU:9, one launch (start us, length us, event | category | flops | bytes accessed | tf_op | source)
XLA Modules:
  0.0 47.5 jit_solution(907805419464156326)
XLA Ops:
  0.1 0.8 %convert_reduce_fusion.1 = s32[8]{0:T(128)S(1)} fusion(s32[1,8,8]{2,1,0:T(8,128)} %param.6, s32[]{:T(128)S(6)} %axis_index.35), kind=kLoop, calls=%fused_computation.36 | loop fusion | flops 184 | bytes 292 | tf_op jit(solution)/shard_map/reduce_sum | solution.py:289
  0.9 0.7 %dynamic-slice_bitcast_fusion = s32[8]{0:T(128)S(1)} fusion(s32[1,8,8]{2,1,0:T(8,128)} %param.6, s32[]{:T(128)S(6)} %select_n.156), kind=kLoop, calls=%fused_computation.64 | loop fusion | bytes 68 | tf_op jit(solution)/shard_map/jit(dynamic_index_in_dim)/squeeze | solution.py:274
  1.6 0.2 convert_reduce_fusion
  1.7 0.7 %multiply_add_fusion = s32[8]{0:T(128)S(1)} fusion(s32[8]{0:T(128)S(1)} %convert_reduce_fusion, s32[1,8,8]{2,1,0:T(8,128)} %param.6, s32[]{:T(128)S(6)} %select_n.156), kind=kLoop, calls=%fused_computation.63 | loop fusion | flops 16 | bytes 100 | tf_op jit(solution)/shard_map/add | solution.py:280
  2.4 1.6 %copy.39 = bf16[1,8,16,16,128]{4,2,1,3,0:T(8,128)(2,1)S(1)} copy(f32[1,8,16,16,128]{4,3,2,1,0:T(8,128)} %param.5) | data formatting | bytes 1572864 | tf_op args[0]
  4.0 0.2 slice.79
  4.2 0.4 convert_element_type.28
  4.6 0.7 %copy.38 = bf16[8,2,8,2,8,2,8]{6,4,2,0,5,3,1:T(8,128)(2,1)S(1)} copy(bf16[8,2,8,2,8,2,8]{6,5,2,1,0,4,3:T(2,128)(2,1)S(1)} %convert_element_type.28) | data formatting | bytes 131072 | tf_op jit(solution)/shard_map/convert_element_type | solution.py:270
  5.3 1.5 %convert_element_type.30 = bf16[8,4096]{1,0:T(8,128)(2,1)S(1)} reshape(bf16[2,2,2,8,8,8,8]{6,5,4,3,2,1,0:T(8,128)(2,1)S(1)} %bitcast.87) | data formatting | bytes 131072 | tf_op jit(solution)/shard_map/convert_element_type | solution.py:270
  6.8 0.2 convolution_convert_fusion.1
  7.0 0.7 %reshape.231.send_ref = bf16[8,16,512]{2,1,0:T(8,128)(2,1)} reshape(bf16[16,4096]{1,0:T(8,128)(2,1)S(1)} %convolution_convert_fusion.1) | data formatting | bytes 262144 | tf_op jit(solution)/shard_map/reshape | solution.py:286
  7.7 8.4 %shard_map.55 = bf16[8,16,512]{2,1,0:T(8,128)(2,1)} custom-call(bf16[8,16,512]{2,1,0:T(8,128)(2,1)} %reshape.231.send_ref), custom_call_target="tpu_custom_call" | custom-call | tf_op jit(solution)/shard_map/pallas_call | solution.py:115
  16.1 0.0 copy-start.2
  16.1 1.0 %reshape.232 = bf16[16,4096]{1,0:T(8,128)(2,1)S(1)} reshape(bf16[8,16,512]{2,1,0:T(8,128)(2,1)} %shard_map.55) | data formatting | bytes 262144 | tf_op jit(solution)/shard_map/reshape | solution.py:287
  17.1 0.2 reduce-window.8
  17.3 0.1 add_select_fusion.1
  17.4 0.1 select_n.155
  17.5 0.1 eq.121
  17.5 0.2 convolution_convert_fusion
  17.8 4.6 %fusion.2 = f32[4,8,512]{2,1,0:T(8,128)S(1)} fusion(bf16[4,4,8,512]{3,2,1,0:T(8,128)(2,1)S(1)} %bitcast.93, bf16[1,1,4,4,512,512]{5,4,3,2,1,0:T(8,128)(2,1)} %param.9), kind=kOutput, calls=%fused_computation.4 | convolution fusion | flops 67108864 | bytes 8585216 | tf_op jit(solution)/shard_map/jkcs,jkst->jct/dot_general | solution.py:302
  22.4 0.6 %reshape.234 = f32[2048,8]{1,0:T(8,128)S(1)} reshape(f32[4,8,512]{2,1,0:T(8,128)S(1)} %fusion.2) | data formatting | bytes 131072 | tf_op jit(solution)/shard_map/reshape | solution.py:312
  23.0 0.6 %fusion.15 = f32[2048,128]{1,0:T(8,128)S(1)} fusion(f32[2048,8]{1,0:T(8,128)S(1)} %reshape.234, s32[128]{0:T(128)S(1)} %get-tuple-element.28, s32[128]{0:T(128)S(1)} %get-tuple-element.29, pred[128]{0:T(512)(128)(4,1)S(1)} %compare_and_fusion), kind=kOutput, calls=%fused_computation.41 | convolution fusion | flops 25167872 | bytes 1115264 | tf_op jit(solution)/shard_map/dot_general | solution.py:313
  23.6 0.1 fusion.24
  23.7 0.1 copy.25
  23.8 0.1 copy.26
  23.8 0.1 copy.27
  23.9 0.1 copy.28
  24.0 0.1 broadcast_select_fusion.3
  24.1 0.2 and_and_fusion
  24.4 0.1 tile.41
  24.5 0.1 tile.44
  24.6 0.1 tile.47
  24.6 0.1 tile.50
  24.7 1.0 %select_select_fusion = f32[8,16,16,128]{3,1,0,2:T(8,128)S(1)} fusion(f32[8,16,16,128]{3,1,0,2:T(8,128)S(1)} %bitcast.83, f32[8,16,16,128]{3,1,0,2:T(8,128)S(1)} %bitcast.84, f32[8,16,16,128]{3,1,0,2:T(8,128)S(1)} %bitcast.85, f32[8,16,16,128]{3,1,0,2:T(8,128)S(1)} %bitcast.86, pred[16,16,128]{2,0,1:T(8,128)(4,1)S(1)} %get-tuple-element.20, ...), kind=kLoop, calls=%fused_computation.8 | loop fusion | flops 1048576 | bytes 6422528 | tf_op jit(solution)/shard_map/jit(_where)/select_n | solution.py:325
  25.7 0.1 fusion.23
  25.8 2.1 %collective-permute-start = (f32[8,1,16,128]{3,1,0,2:T(1,128)S(1)}, f32[8,1,16,128]{3,1,0,2:T(1,128)S(1)}, u32[]{:S(2)}, u32[]{:S(2)}) collective-permute-start(f32[8,1,16,128]{3,1,0,2:T(1,128)S(1)} %get-tuple-element.14), channel_id=1, source_target_pairs={{0,8},{8,16},{16,24},{24,32},{32,40},{40,48},{48,56},{56,0},{1,9},... | collective-permute-start | bytes 196616 | tf_op jit(solution)/shard_map/ppermute | solution.py:139
  27.9 3.6 %collective-permute-start.1 = (f32[8,1,16,128]{3,1,0,2:T(1,128)S(1)}, f32[8,1,16,128]{3,1,0,2:T(1,128)S(1)}, u32[]{:S(2)}, u32[]{:S(2)}) collective-permute-start(f32[8,1,16,128]{3,1,0,2:T(1,128)S(1)} %get-tuple-element.13), channel_id=1, source_target_pairs={{8,0},{16,8},{24,16},{32,24},{40,32},{48,40},{56,48},{0,56},{9,1},... | collective-permute-start | bytes 196616 | tf_op jit(solution)/shard_map/ppermute | solution.py:140
  31.5 2.5 %collective-permute-start.2 = (f32[8,16,1,128]{3,1,0,2:T(8,128)S(1)}, f32[8,16,1,128]{3,1,0,2:T(8,128)S(1)}, u32[]{:S(2)}, u32[]{:S(2)}) collective-permute-start(f32[8,16,1,128]{3,1,0,2:T(8,128)S(1)} %get-tuple-element.10), channel_id=1, source_target_pairs={{0,1},{1,2},{2,3},{3,4},{4,5},{5,6},{6,7},{8,9},{9,10},{10,11},{11... | collective-permute-start | bytes 196616 | tf_op jit(solution)/shard_map/ppermute | solution.py:139
  34.0 4.9 %collective-permute-start.3 = (f32[8,16,1,128]{3,1,0,2:T(8,128)S(1)}, f32[8,16,1,128]{3,1,0,2:T(8,128)S(1)}, u32[]{:S(2)}, u32[]{:S(2)}) collective-permute-start(f32[8,16,1,128]{3,1,0,2:T(8,128)S(1)} %get-tuple-element.9), channel_id=1, source_target_pairs={{1,0},{2,1},{3,2},{4,3},{5,4},{6,5},{7,6},{9,8},{10,9},{11,10},{12... | collective-permute-start | bytes 196616 | tf_op jit(solution)/shard_map/ppermute | solution.py:140
  38.9 1.6 %copy.29.grid_ref = f32[8,16,16,128]{3,2,1,0:T(8,128)} copy(f32[8,16,16,128]{3,1,0,2:T(8,128)S(1)} %select_select_fusion) | data formatting | bytes 2097152 | tf_op jit(solution)/shard_map/jit(_where)/select_n | solution.py:325
  40.5 0.0 collective-permute-done
  40.5 0.0 collective-permute-done.1
  40.5 0.1 broadcast_select_fusion
  40.6 0.6 %copy.30.low_x_ref = f32[8,16,128]{2,1,0:T(8,128)} copy(f32[8,16,128]{2,0,1:T(8,128)S(1)} %bitcast.96) | data formatting | bytes 131072 | tf_op jit(solution)/shard_map/squeeze | solution.py:143
  41.3 0.6 %copy.31.high_x_ref = f32[8,16,128]{2,1,0:T(8,128)} copy(f32[8,16,128]{2,0,1:T(8,128)S(1)} %bitcast.95) | data formatting | bytes 131072 | tf_op jit(solution)/shard_map/squeeze | solution.py:143
  41.9 0.0 collective-permute-done.2
  41.9 0.7 %select_bitcast_fusion = (f32[8,16,128]{2,1,0:T(8,128)}, f32[8,16,128]{2,1,0:T(8,128)}) fusion(f32[8,16,1,128]{3,1,0,2:T(8,128)S(1)} %collective-permute-done.3, pred[]{:T(512)S(6)} %eq.137, f32[8,16,16,128]{3,1,0,2:T(8,128)S(1)} %select_select_fusion, f32[8,16,1,128]{3,1,0,2:T(8,128)S(1)} %collective-permute-done.2, pred[]{:T(512)S(6)} %eq.136), kind=kLoop, calls=%fused_computation.23 | loop fusion | flops 32768 | bytes 393218 | tf_op jit(solution)/shard_map/squeeze | solution.py:143
  42.6 4.9 %shard_map.56 = f32[8,16,16,128]{3,2,1,0:T(8,128)} custom-call(f32[8,16,16,128]{3,2,1,0:T(8,128)} %copy.29.grid_ref, f32[8,16,128]{2,1,0:T(8,128)} %copy.30.low_x_ref, f32[8,16,128]{2,1,0:T(8,128)} %copy.31.high_x_ref, f32[8,16,128]{2,1,0:T(8,128)} %get-tuple-element.8.low_y_ref, f32[8,16,128]{2,1,0:T(8,128)} %get-tuple-element.7.high_y_ref), custom_call_target="tpu_custom_call" | custom-call | tf_op jit(solution)/shard_map/pallas_call | solution.py:248
  (18 shorter events, 0.2 us)
Async XLA Ops:
  0.0 17.5 %copy-start.1 = (s32[1,1,4,4]{3,2,1,0:T(4,128)S(1)}, s32[1,1,4,4]{3,2,1,0:T(4,128)}, u32[]{:S(2)}) copy-start(s32[1,1,4,4]{3,2,1,0:T(4,128)} %param.7) | copy-start | bytes 196
  16.1 7.8 %copy-start.2 = (s32[1,1,4]{2,1,0:T(1,128)S(1)}, s32[1,1,4]{2,1,0:T(1,128)}, u32[]{:S(2)}) copy-start(s32[1,1,4]{2,1,0:T(1,128)} %param.8) | copy-start | bytes 52
  22.4 2.3 %copy-start = (f32[1,8,16,16,128]{4,3,2,1,0:T(8,128)S(1)}, f32[1,8,16,16,128]{4,3,2,1,0:T(8,128)}, u32[]{:S(2)}) copy-start(f32[1,8,16,16,128]{4,3,2,1,0:T(8,128)} %param.5) | copy-start | bytes 3145732
  25.8 14.7 %collective-permute-start = (f32[8,1,16,128]{3,1,0,2:T(1,128)S(1)}, f32[8,1,16,128]{3,1,0,2:T(1,128)S(1)}, u32[]{:S(2)}, u32[]{:S(2)}) collective-permute-start(f32[8,1,16,128]{3,1,0,2:T(1,128)S(1)} %get-tuple-element.14), channel_id=1, source_target_pairs={{0,8},{8,16},{16,24},{24,32},{32,40},{40,48},{48,56},{56,0},{1,9},... | collective-permute-start | bytes 196616 | tf_op jit(solution)/shard_map/ppermute | solution.py:139
  27.9 12.6 %collective-permute-start.1 = (f32[8,1,16,128]{3,1,0,2:T(1,128)S(1)}, f32[8,1,16,128]{3,1,0,2:T(1,128)S(1)}, u32[]{:S(2)}, u32[]{:S(2)}) collective-permute-start(f32[8,1,16,128]{3,1,0,2:T(1,128)S(1)} %get-tuple-element.13), channel_id=1, source_target_pairs={{8,0},{16,8},{24,16},{32,24},{40,32},{48,40},{56,48},{0,56},{9,1},... | collective-permute-start | bytes 196616 | tf_op jit(solution)/shard_map/ppermute | solution.py:140
  31.5 10.4 %collective-permute-start.2 = (f32[8,16,1,128]{3,1,0,2:T(8,128)S(1)}, f32[8,16,1,128]{3,1,0,2:T(8,128)S(1)}, u32[]{:S(2)}, u32[]{:S(2)}) collective-permute-start(f32[8,16,1,128]{3,1,0,2:T(8,128)S(1)} %get-tuple-element.10), channel_id=1, source_target_pairs={{0,1},{1,2},{2,3},{3,4},{4,5},{5,6},{6,7},{8,9},{9,10},{10,11},{11... | collective-permute-start | bytes 196616 | tf_op jit(solution)/shard_map/ppermute | solution.py:139
  34.0 7.9 %collective-permute-start.3 = (f32[8,16,1,128]{3,1,0,2:T(8,128)S(1)}, f32[8,16,1,128]{3,1,0,2:T(8,128)S(1)}, u32[]{:S(2)}, u32[]{:S(2)}) collective-permute-start(f32[8,16,1,128]{3,1,0,2:T(8,128)S(1)} %get-tuple-element.9), channel_id=1, source_target_pairs={{1,0},{2,1},{3,2},{4,3},{5,4},{6,5},{7,6},{9,8},{10,9},{11,10},{12... | collective-permute-start | bytes 196616 | tf_op jit(solution)/shard_map/ppermute | solution.py:140

commit v9 on v8

--- a/solution.py
+++ b/solution.py
@@ -126,22 +126,14 @@
     )(send_cells)
 
 
-def ghost_pair(cells, axis, dim, wrap, fix_low, fix_high):
+def ghost_pair(head, tail, axis, wrap):
     count = lax.axis_size(axis)
-    size = cells.shape[dim]
-    head = lax.slice_in_dim(cells, 0, 1, axis=dim)
-    tail = lax.slice_in_dim(cells, size - 1, size, axis=dim)
     up = [(i, i + 1) for i in range(count - 1)]
     down = [(i + 1, i) for i in range(count - 1)]
     if wrap:
         up.append((count - 1, 0))
         down.append((0, count - 1))
-    from_low = lax.ppermute(tail, axis, up)
-    from_high = lax.ppermute(head, axis, down)
-    low = jnp.where(fix_low, head, from_low)
-    high = jnp.where(fix_high, tail, from_high)
-    return lax.squeeze(low, (dim,)), lax.squeeze(high, (dim,))
-
+    return lax.ppermute(tail, axis, up), lax.ppermute(head, axis, down)
 
 def cell_flux(parts, direction):
     density = parts[0]
@@ -184,15 +176,24 @@
 def stencil_kernel(grid_ref, low_x_ref, high_x_ref, low_y_ref, high_y_ref, out_ref):
     ncomp, len_x, len_y, len_z = grid_ref.shape
     domain = lax.axis_index("dom")
+    column = lax.axis_index("gx")
+    row = lax.axis_index("yz")
+    helio_side = domain == 1
+    fix_low_x = helio_side & (column == 0)
+    fix_high_x = helio_side & (column == lax.axis_size("gx") - 1)
+    fix_low_y = row == 0
+    fix_high_y = row == lax.axis_size("yz") - 1
     ratio = jnp.where(domain == 0, CORONA_RATIO, HELIO_RATIO).astype(jnp.float32)
     rows = lax.broadcasted_iota(jnp.int32, (len_y, len_z), 0)
     lanes = lax.broadcasted_iota(jnp.int32, (len_y, len_z), 1)
 
     def plane(x):
         if x < 0:
-            return [low_x_ref[c] for c in range(ncomp)]
+            return [jnp.where(fix_low_x, grid_ref[c, 0], low_x_ref[c]) for c in range(ncomp)]
         if x >= len_x:
-            return [high_x_ref[c] for c in range(ncomp)]
+            return [
+                jnp.where(fix_high_x, grid_ref[c, len_x - 1], high_x_ref[c]) for c in range(ncomp)
+            ]
         return [grid_ref[c, x] for c in range(ncomp)]
 
     def shift(values, edge, step, axis, index, last):
@@ -207,8 +208,16 @@
         high = plane(x + 1)
         high_flux = cell_flux(high, 0)
         change = face_change(low, mid, high, low_flux, mid_flux, high_flux)
-        y_low = [low_y_ref[c, pl.ds(x, 1), :] for c in range(ncomp)]
-        y_high = [high_y_ref[c, pl.ds(x, 1), :] for c in range(ncomp)]
+        y_low = [
+            jnp.where(fix_low_y, grid_ref[c, x, pl.ds(0, 1), :], low_y_ref[c, pl.ds(x, 1), :])
+            for c in range(ncomp)
+        ]
+        y_high = [
+            jnp.where(
+                fix_high_y, grid_ref[c, x, pl.ds(len_y - 1, 1), :], high_y_ref[c, pl.ds(x, 1), :]
+            )
+            for c in range(ncomp)
+        ]
         y_flux = cell_flux(mid, 1)
         y_low_flux = cell_flux(y_low, 1)
         y_high_flux = cell_flux(y_high, 1)
@@ -251,7 +260,6 @@
         in_specs=[vmem] * 5,
         out_specs=vmem,
     )(grid_cells, low_x, high_x, low_y, high_y)
-
 
 def local(field_state, shell_owner, block_sources, block_targets, interp_weights):
     grid_cells = field_state[0]
@@ -320,17 +328,26 @@
         & (lanes[None] // BLK == (spots % per_z)[:, None, None, None])
         & (targets >= 0)[:, None, None, None]
     )
-    for slot_number in range(slots_here):
-        placed = jnp.tile(stacked[slot_number], (1, len_x // BLK, len_y // BLK, 1))
-        grid_cells = jnp.where(hit[slot_number][None], placed, grid_cells)
-
-    helio_side = domain == 1
-    low_x = helio_side & (column == 0)
-    high_x = helio_side & (column == gx_count - 1)
-    low_y = yz_index == 0
-    high_y = yz_index == yz_count - 1
-    ghost_low_x, ghost_high_x = ghost_pair(grid_cells, "gx", 1, True, low_x, high_x)
-    ghost_low_y, ghost_high_y = ghost_pair(grid_cells, "yz", 2, False, low_y, high_y)
+    placed = [
+        jnp.tile(stacked[slot_number], (1, len_x // BLK, len_y // BLK, 1))
+        for slot_number in range(slots_here)
+    ]
+
+    def filled(view):
+        cells = view(grid_cells)
+        for slot_number in range(slots_here):
+            cells = jnp.where(view(hit[slot_number][None]), view(placed[slot_number]), cells)
+        return cells
+
+    def at_x(index):
+        return lambda cells: lax.index_in_dim(cells, index, axis=1, keepdims=False)
+
+    def at_y(index):
+        return lambda cells: lax.index_in_dim(cells, index, axis=2, keepdims=False)
+
+    ghost_low_x, ghost_high_x = ghost_pair(filled(at_x(0)), filled(at_x(len_x - 1)), "gx", True)
+    ghost_low_y, ghost_high_y = ghost_pair(filled(at_y(0)), filled(at_y(len_y - 1)), "yz", False)
+    grid_cells = filled(lambda cells: cells)
     updated = stencil(grid_cells, ghost_low_x, ghost_high_x, ghost_low_y, ghost_high_y)
     return updated[None]
 

time: 47.9 us -> 51.4 us (1.073)
  waiting for transfers between devices: 0.01 us -> 2.59 us
  local copies, waits for them, and re-layouts: 11.1 us -> 12.5 us
  starting transfers between devices: 13 us -> 12 us
  other arithmetic: 4.15 us -> 4.69 us
    ppermute x4, waiting for transfers between devices: 0.01 us -> 2.59 us  [ghost_pair(): return (lax.ppermute(tail, axis, up), lax.ppermute(head, axis, down))]
    another operation x1 -> x2, other arithmetic: 0.18 us -> 1.7 us  [the longest x1 1.52 us: local(): jnp.tile(stacked[slot_number], (1, len_x // BLK, len_y // BLK, 1))]
    ppermute x0 -> x2, local copies, waits for them, and re-layouts: none -> 1.27 us  [ghost_pair(): return (lax.ppermute(tail, axis, up), lax.ppermute(head, axis, down))]
    squeeze x2 -> x3, local copies, waits for them, and re-layouts: 1.27 us -> 0.03 us  [at_y(): return lambda cells: lax.index_in_dim(cells, index, axis=2, keepdims=False)]
    ppermute x4, starting transfers between devices: 13 us -> 12 us  [ghost_pair(): return (lax.ppermute(tail, axis, up), lax.ppermute(head, axis, down))]
    select_n x2, other arithmetic: 1.12 us -> 0.16 us  [filled(): jnp.where(view(hit[slot_number][None]), view(placed[slot_number]), cells)]
    eq x1, local copies, waits for them, and re-layouts: 0.08 us -> 0.76 us  [local(): wanted[:, None] == got_tags[None, :]]
    squeeze x1 -> x0, other arithmetic: 0.67 us -> none  [ghost_pair(): return (lax.squeeze(low, (dim,)), lax.squeeze(high, (dim,)))]
  transfers between devices with their start and end apart: 4 -> 4, of which waited for: 0 -> 1; matrix products, arithmetic and copies ran while one was open for 6% -> 5% of each run, Pallas kernels for 0% -> 0%
where the time goes in v9:
time: 51.4 us; the launch traced here: 51 us
  Pallas kernels  13.4 us (26%)
  local copies, waits for them, and re-layouts  12.5 us (24%)
  starting transfers between devices  12 us (23%)
  matrix products  5.57 us (11%)
  other arithmetic  4.69 us (9%)
  waiting for transfers between devices  2.59 us (5%)
    ppermute x4, starting transfers between devices, ghost_pair(): return (lax.ppermute(tail, axis, up), lax.ppermute(head, axis, down))  12 us
    pallas_call x1, Pallas kernels, route_blocks(): pl.pallas_call(route_kernel, out_shape=jax.ShapeDtypeStruct(send_cells.sh...  8.44 us
    pallas_call x1, Pallas kernels, stencil(): pl.pallas_call(stencil_kernel, out_shape=jax.ShapeDtypeStruct(grid_cells....  5.01 us
    dot_general x1, matrix products, local(): jnp.einsum('jkcs,jkst->jct', picked, interp_weights[0, 0], preferred_elem...  4.56 us
    ppermute x4, waiting for transfers between devices, ghost_pair(): return (lax.ppermute(tail, axis, up), lax.ppermute(head, axis, down))  2.59 us
    convert_element_type x3, local copies, waits for them, and re-layouts, local(): shell_cells.transpose(1, 3, 5, 0, 2, 4, 6).reshape(-1, ncomp * volume)  2.55 us
    unnamed x16, local copies, waits for them, and re-layouts  2.28 us
    another operation x1, other arithmetic, local(): jnp.tile(stacked[slot_number], (1, len_x // BLK, len_y // BLK, 1))  1.52 us
  transfers between devices with their start and end apart: 4, of which 1 were waited for; matrix products, arithmetic and copies ran while one was open for 5% of the time, Pallas kernels for 0%

profile of v9, /device:TPU:9, one launch (start us, length us, event | category | flops | bytes accessed | tf_op | source)
XLA Modules:
  0.0 51.0 jit_solution(17428840330692497431)
XLA Ops:
  0.1 0.7 %compare_bitcast_fusion = (pred[4]{0:T(512)(128)(4,1)S(1)}, s32[1,1,4]{2,1,0:T(1,128)S(1)}) fusion(s32[1,1,4]{2,1,0:T(1,128)} %param.8, pred[]{:T(512)S(6)} %eq.99), kind=kLoop, calls=%fused_computation.99 | loop fusion | flops 8 | bytes 37 | tf_op jit(solution)/shard_map/ge | solution.py:329
  0.8 0.1 broadcast_select_fusion.1
  0.9 0.2 and_and_fusion
  1.2 0.8 %convert_reduce_fusion.1 = s32[8]{0:T(128)S(1)} fusion(s32[1,8,8]{2,1,0:T(8,128)} %param.6, s32[]{:T(128)S(6)} %axis_index.25), kind=kLoop, calls=%fused_computation.83 | loop fusion | flops 184 | bytes 292 | tf_op jit(solution)/shard_map/reduce_sum | solution.py:297
  2.0 0.8 %eq.108 = s32[16]{0:T(128)S(1)} reshape(s32[1,1,4,4]{3,2,1,0:T(4,128)} %param.7) | data formatting | bytes 128 | tf_op jit(solution)/shard_map/eq | solution.py:304
  2.7 0.2 reduce-window.8
  2.9 0.7 %dynamic-slice_bitcast_fusion = s32[8]{0:T(128)S(1)} fusion(s32[1,8,8]{2,1,0:T(8,128)} %param.6, s32[]{:T(128)S(6)} %select_n.177), kind=kLoop, calls=%fused_computation.111 | loop fusion | bytes 68 | tf_op jit(solution)/shard_map/jit(dynamic_index_in_dim)/squeeze | solution.py:282
  3.6 0.2 convert_reduce_fusion
  3.8 0.7 %multiply_add_fusion = s32[8]{0:T(128)S(1)} fusion(s32[8]{0:T(128)S(1)} %convert_reduce_fusion, s32[1,8,8]{2,1,0:T(8,128)} %param.6, s32[]{:T(128)S(6)} %select_n.177), kind=kLoop, calls=%fused_computation.110 | loop fusion | flops 16 | bytes 100 | tf_op jit(solution)/shard_map/add | solution.py:288
  4.5 0.1 add_select_fusion.1
  4.6 0.1 select_n.176
  4.6 1.6 %copy.123 = f32[1,8,16,16,128]{4,2,1,3,0:T(8,128)S(1)} copy(f32[1,8,16,16,128]{4,3,2,1,0:T(8,128)} %param.5) | data formatting | bytes 2097152 | tf_op args[0]
  6.2 0.2 slice.344
  6.4 0.4 convert_element_type.28
  6.8 0.7 %copy.122 = bf16[8,2,8,2,8,2,8]{6,4,2,0,5,3,1:T(8,128)(2,1)S(1)} copy(bf16[8,2,8,2,8,2,8]{6,5,2,1,0,4,3:T(2,128)(2,1)S(1)} %convert_element_type.28) | data formatting | bytes 131072 | tf_op jit(solution)/shard_map/convert_element_type | solution.py:278
  7.5 1.5 %convert_element_type.30 = bf16[8,4096]{1,0:T(8,128)(2,1)S(1)} reshape(bf16[2,2,2,8,8,8,8]{6,5,4,3,2,1,0:T(8,128)(2,1)S(1)} %bitcast.219) | data formatting | bytes 131072 | tf_op jit(solution)/shard_map/convert_element_type | solution.py:278
  9.0 0.2 convolution_convert_fusion.1
  9.2 0.7 %reshape.247.send_ref = bf16[8,16,512]{2,1,0:T(8,128)(2,1)} reshape(bf16[16,4096]{1,0:T(8,128)(2,1)S(1)} %convolution_convert_fusion.1) | data formatting | bytes 262144 | tf_op jit(solution)/shard_map/reshape | solution.py:294
  9.9 8.4 %shard_map.55 = bf16[8,16,512]{2,1,0:T(8,128)(2,1)} custom-call(bf16[8,16,512]{2,1,0:T(8,128)(2,1)} %reshape.247.send_ref), custom_call_target="tpu_custom_call" | custom-call | tf_op jit(solution)/shard_map/pallas_call | solution.py:115
  18.3 1.0 %reshape.248 = bf16[16,4096]{1,0:T(8,128)(2,1)S(1)} reshape(bf16[8,16,512]{2,1,0:T(8,128)(2,1)} %shard_map.55) | data formatting | bytes 262144 | tf_op jit(solution)/shard_map/reshape | solution.py:295
  19.3 0.2 convolution_convert_fusion
  19.6 4.6 %fusion.2 = f32[4,8,512]{2,1,0:T(8,128)S(1)} fusion(bf16[4,4,8,512]{3,2,1,0:T(8,128)(2,1)S(1)} %bitcast.227, bf16[1,1,4,4,512,512]{5,4,3,2,1,0:T(8,128)(2,1)} %param.9), kind=kOutput, calls=%fused_computation.4 | convolution fusion | flops 67108864 | bytes 8585216 | tf_op jit(solution)/shard_map/jkcs,jkst->jct/dot_general | solution.py:310
  24.2 0.6 %reshape.250 = f32[2048,8]{1,0:T(8,128)S(1)} reshape(f32[4,8,512]{2,1,0:T(8,128)S(1)} %fusion.2) | data formatting | bytes 131072 | tf_op jit(solution)/shard_map/reshape | solution.py:320
  24.8 0.6 %fusion.31 = f32[2048,128]{1,0:T(8,128)S(1)} fusion(f32[2048,8]{1,0:T(8,128)S(1)} %reshape.250, s32[128]{0:T(128)S(1)} %get-tuple-element.49, s32[128]{0:T(128)S(1)} %get-tuple-element.50, pred[128]{0:T(512)(128)(4,1)S(1)} %compare_and_fusion), kind=kOutput, calls=%fused_computation.88 | convolution fusion | flops 25167872 | bytes 1115264 | tf_op jit(solution)/shard_map/dot_general | solution.py:321
  25.4 0.1 fusion.39
  25.5 0.1 copy.71
  25.5 0.2 copy.74
  25.7 0.2 copy.73
  25.8 0.2 copy.72
  26.0 0.1 tile.41
  26.1 0.1 tile.44
  26.3 0.1 tile.47
  26.4 0.1 tile.50
  26.5 1.5 %fusion.38 = (f32[8,16,16,128]{3,0,2,1:T(8,128)S(1)}, f32[8,16,16,128]{3,0,2,1:T(8,128)S(1)}, f32[8,16,16,128]{3,0,2,1:T(8,128)S(1)}) fusion(f32[8,16,16,128]{3,1,0,2:T(8,128)S(1)} %bitcast.217, f32[8,16,16,128]{3,0,2,1:T(8,128)S(1)} %bitcast.213, f32[8,16,16,128]{3,0,2,1:T(8,128)S(1)} %bitcast.210, f32[8,16,16,128]{3,0,2,1:T(8,128)S(1)} %bitcast.207, ...), kind=kLoop, calls=%fused_computation.116 | loop fusion | flops 1048576 | bytes 8519680 | tf_op jit(solution)/shard_map/tile | solution.py:332
  28.0 0.1 fusion.19
  28.1 5.6 %collective-permute-start.1 = (f32[8,16,128]{2,0,1:T(8,128)S(1)}, f32[8,16,128]{2,0,1:T(8,128)S(1)}, u32[]{:S(2)}, u32[]{:S(2)}) collective-permute-start(f32[8,16,128]{2,0,1:T(8,128)S(1)} %get-tuple-element.7), channel_id=1, source_target_pairs={{8,0},{16,8},{24,16},{32,24},{40,32},{48,40},{56,48},{0,56},{9,1},... | collective-permute-start | bytes 196616 | tf_op jit(solution)/shard_map/ppermute | solution.py:136
  33.7 0.1 fusion.40
  33.9 0.1 fusion.11
  34.0 4.3 %collective-permute-start.3 = (f32[8,16,128]{2,1,0:T(8,128)S(1)}, f32[8,16,128]{2,1,0:T(8,128)S(1)}, u32[]{:S(2)}, u32[]{:S(2)}) collective-permute-start(f32[8,16,128]{2,1,0:T(8,128)S(1)} %get-tuple-element.9), channel_id=1, source_target_pairs={{1,0},{2,1},{3,2},{4,3},{5,4},{6,5},{7,6},{9,8},{10,9},{11,10},{12... | collective-permute-start | bytes 196616 | tf_op jit(solution)/shard_map/ppermute | solution.py:136
  38.3 2.1 %collective-permute-start.2 = (f32[8,16,128]{2,1,0:T(8,128)S(1)}, f32[8,16,128]{2,1,0:T(8,128)S(1)}, u32[]{:S(2)}, u32[]{:S(2)}) collective-permute-start(f32[8,16,128]{2,1,0:T(8,128)S(1)} %get-tuple-element.10), channel_id=1, source_target_pairs={{0,1},{1,2},{2,3},{3,4},{4,5},{5,6},{6,7},{8,9},{9,10},{10,11},{11... | collective-permute-start | bytes 196616 | tf_op jit(solution)/shard_map/ppermute | solution.py:136
  40.4 1.2 %copy.86.grid_ref = f32[8,16,16,128]{3,2,1,0:T(8,128)} copy(f32[8,16,16,128]{3,0,2,1:T(8,128)S(1)} %get-tuple-element.18) | data formatting | bytes 2097152 | tf_op jit(solution)/shard_map/jit(_where)/select_n | solution.py:339
  41.5 0.0 collective-permute-done.1
  41.5 0.6 %copy.88.high_x_ref = f32[8,16,128]{2,1,0:T(8,128)} copy(f32[8,16,128]{2,0,1:T(8,128)S(1)} %collective-permute-done.1) | data formatting | bytes 131072 | tf_op jit(solution)/shard_map/ppermute | solution.py:136
  42.2 0.6 %copy.87.low_x_ref = f32[8,16,128]{2,1,0:T(8,128)} copy(f32[8,16,128]{2,0,1:T(8,128)S(1)} %collective-permute-done) | data formatting | bytes 131072 | tf_op jit(solution)/shard_map/ppermute | solution.py:136
  42.8 0.0 collective-permute-done.3.high_y_ref
  42.8 2.6 %collective-permute-done.2.low_y_ref = f32[8,16,128]{2,1,0:T(8,128)S(1)} collective-permute-done((f32[8,16,128]{2,1,0:T(8,128)S(1)}, f32[8,16,128]{2,1,0:T(8,128)S(1)}, u32[]{:S(2)}, u32[]{:S(2)}) %collective-permute-start.2) | collective-permute-done | bytes 65568 | tf_op jit(solution)/shard_map/ppermute | solution.py:136
  45.4 0.6 %copy-done.2 = f32[8,16,128]{2,1,0:T(8,128)} copy-done((f32[8,16,128]{2,1,0:T(8,128)}, f32[8,16,128]{2,1,0:T(8,128)S(1)}, u32[]{:S(2)}) %copy-start.2) | copy-done | bytes 65560
  46.0 5.0 %shard_map.56 = f32[8,16,16,128]{3,2,1,0:T(8,128)} custom-call(f32[8,16,16,128]{3,2,1,0:T(8,128)} %copy.86.grid_ref, f32[8,16,128]{2,1,0:T(8,128)} %copy.87.low_x_ref, f32[8,16,128]{2,1,0:T(8,128)} %copy.88.high_x_ref, f32[8,16,128]{2,1,0:T(8,128)} %copy-done.2, f32[8,16,128]{2,1,0:T(8,128)} %copy-done.1), custom_call_target="tpu_custom_call" | custom-call | tf_op jit(solution)/shard_map/pallas_call | solution.py:257
  (30 shorter events, 0.3 us)
Async XLA Ops:
  24.2 2.3 %copy-start = (f32[1,8,16,16,128]{4,3,2,1,0:T(8,128)S(1)}, f32[1,8,16,16,128]{4,3,2,1,0:T(8,128)}, u32[]{:S(2)}) copy-start(f32[1,8,16,16,128]{4,3,2,1,0:T(8,128)} %param.5) | copy-start | bytes 3145732
  28.1 13.4 %collective-permute-start.1 = (f32[8,16,128]{2,0,1:T(8,128)S(1)}, f32[8,16,128]{2,0,1:T(8,128)S(1)}, u32[]{:S(2)}, u32[]{:S(2)}) collective-permute-start(f32[8,16,128]{2,0,1:T(8,128)S(1)} %get-tuple-element.7), channel_id=1, source_target_pairs={{8,0},{16,8},{24,16},{32,24},{40,32},{48,40},{56,48},{0,56},{9,1},... | collective-permute-start | bytes 196616 | tf_op jit(solution)/shard_map/ppermute | solution.py:136
  33.7 8.5 %collective-permute-start = (f32[8,16,128]{2,0,1:T(8,128)S(1)}, f32[8,16,128]{2,0,1:T(8,128)S(1)}, u32[]{:S(2)}, u32[]{:S(2)}) collective-permute-start(f32[8,16,128]{2,0,1:T(8,128)S(1)} %get-tuple-element.8), channel_id=1, source_target_pairs={{0,8},{8,16},{16,24},{24,32},{32,40},{40,48},{48,56},{56,0},{1,9},... | collective-permute-start | bytes 196616 | tf_op jit(solution)/shard_map/ppermute | solution.py:136
  34.0 8.9 %collective-permute-start.3 = (f32[8,16,128]{2,1,0:T(8,128)S(1)}, f32[8,16,128]{2,1,0:T(8,128)S(1)}, u32[]{:S(2)}, u32[]{:S(2)}) collective-permute-start(f32[8,16,128]{2,1,0:T(8,128)S(1)} %get-tuple-element.9), channel_id=1, source_target_pairs={{1,0},{2,1},{3,2},{4,3},{5,4},{6,5},{7,6},{9,8},{10,9},{11,10},{12... | collective-permute-start | bytes 196616 | tf_op jit(solution)/shard_map/ppermute | solution.py:136
  38.3 7.1 %collective-permute-start.2 = (f32[8,16,128]{2,1,0:T(8,128)S(1)}, f32[8,16,128]{2,1,0:T(8,128)S(1)}, u32[]{:S(2)}, u32[]{:S(2)}) collective-permute-start(f32[8,16,128]{2,1,0:T(8,128)S(1)} %get-tuple-element.10), channel_id=1, source_target_pairs={{0,1},{1,2},{2,3},{3,4},{4,5},{5,6},{6,7},{8,9},{9,10},{10,11},{11... | collective-permute-start | bytes 196616 | tf_op jit(solution)/shard_map/ppermute | solution.py:136
  42.8 2.6 %copy-start.1 = (f32[8,16,128]{2,1,0:T(8,128)}, f32[8,16,128]{2,1,0:T(8,128)S(1)}, u32[]{:S(2)}) copy-start(f32[8,16,128]{2,1,0:T(8,128)S(1)} %collective-permute-done.3.high_y_ref) | copy-start | bytes 196612
  45.4 0.6 %copy-start.2 = (f32[8,16,128]{2,1,0:T(8,128)}, f32[8,16,128]{2,1,0:T(8,128)S(1)}, u32[]{:S(2)}) copy-start(f32[8,16,128]{2,1,0:T(8,128)S(1)} %collective-permute-done.2.low_y_ref) | copy-start | bytes 196612

commit v10 on v9

--- a/solution.py
+++ b/solution.py
@@ -261,6 +261,46 @@
         out_specs=vmem,
     )(grid_cells, low_x, high_x, low_y, high_y)
 
+def fill_kernel(targets_ref, grid_ref, stacked_ref, out_ref, low_x_ref, high_x_ref, low_y_ref, high_y_ref):
+    ncomp, len_x, len_y, len_z = grid_ref.shape
+    per_y = len_y // BLK
+    per_z = len_z // BLK
+    out_ref[...] = grid_ref[...]
+    helio_side = lax.axis_index("dom") == 1
+    lanes = lax.broadcasted_iota(jnp.int32, (BLK, len_z), 1) // BLK
+    for slot in range(stacked_ref.shape[0]):
+        target = targets_ref[slot]
+
+        @pl.when(helio_side & (target >= 0))
+        def _():
+            corner_x = target // (per_y * per_z) * BLK
+            corner_y = pl.multiple_of(target // per_z % per_y * BLK, BLK)
+            lane_hit = lanes == target % per_z
+            for c in range(ncomp):
+                for a in range(BLK):
+                    window = (c, corner_x + a, pl.ds(corner_y, BLK), slice(None))
+                    out_ref[window] = jnp.where(lane_hit, stacked_ref[slot, c, a], out_ref[window])
+
+    low_x_ref[...] = out_ref[:, 0]
+    high_x_ref[...] = out_ref[:, len_x - 1]
+    for c in range(ncomp):
+        for x in range(len_x):
+            low_y_ref[c, pl.ds(x, 1), :] = out_ref[c, x, pl.ds(0, 1), :]
+            high_y_ref[c, pl.ds(x, 1), :] = out_ref[c, x, pl.ds(len_y - 1, 1), :]
+
+
+def fill_blocks(targets, grid_cells, stacked):
+    ncomp, len_x, len_y, len_z = grid_cells.shape
+    vmem = pl.BlockSpec(memory_space=pltpu.VMEM)
+    face = jax.ShapeDtypeStruct((ncomp, len_x, len_z), grid_cells.dtype)
+    return pl.pallas_call(
+        fill_kernel,
+        out_shape=(jax.ShapeDtypeStruct(grid_cells.shape, grid_cells.dtype),) + (face,) * 4,
+        in_specs=[pl.BlockSpec(memory_space=pltpu.SMEM), vmem, vmem],
+        out_specs=(vmem,) * 5,
+    )(targets, grid_cells, stacked)
+
+
 def local(field_state, shell_owner, block_sources, block_targets, interp_weights):
     grid_cells = field_state[0]
     ncomp, len_x, len_y, len_z = grid_cells.shape
@@ -311,43 +351,15 @@
         "jkcs,jkst->jct", picked, interp_weights[0, 0], preferred_element_type=jnp.float32
     )
 
-    rows = lax.broadcasted_iota(jnp.int32, (len_x, len_y, len_z), 0) // BLK
-    cols = lax.broadcasted_iota(jnp.int32, (len_x, len_y, len_z), 1) // BLK
-    lanes = lax.broadcasted_iota(jnp.int32, (len_x, len_y, len_z), 2)
     spread_of = lax.broadcasted_iota(jnp.int32, (BLK, len_z), 1) % BLK
     offset_of = lax.broadcasted_iota(jnp.int32, (BLK, len_z), 0)
     spread = (spread_of == offset_of).astype(jnp.float32)
     stacked = interp_blocks.reshape(slots_here * ncomp * BLK * BLK, BLK)
     stacked = jnp.dot(stacked, spread, precision=lax.Precision.HIGHEST)
     stacked = stacked.reshape(slots_here, ncomp, BLK, BLK, len_z)
-    targets = jnp.where(domain == 1, block_targets[0, 0], -1)
-    spots = jnp.maximum(targets, 0)
-    hit = (
-        (rows[None] == (spots // (per_y * per_z))[:, None, None, None])
-        & (cols[None] == (spots // per_z % per_y)[:, None, None, None])
-        & (lanes[None] // BLK == (spots % per_z)[:, None, None, None])
-        & (targets >= 0)[:, None, None, None]
-    )
-    placed = [
-        jnp.tile(stacked[slot_number], (1, len_x // BLK, len_y // BLK, 1))
-        for slot_number in range(slots_here)
-    ]
-
-    def filled(view):
-        cells = view(grid_cells)
-        for slot_number in range(slots_here):
-            cells = jnp.where(view(hit[slot_number][None]), view(placed[slot_number]), cells)
-        return cells
-
-    def at_x(index):
-        return lambda cells: lax.index_in_dim(cells, index, axis=1, keepdims=False)
-
-    def at_y(index):
-        return lambda cells: lax.index_in_dim(cells, index, axis=2, keepdims=False)
-
-    ghost_low_x, ghost_high_x = ghost_pair(filled(at_x(0)), filled(at_x(len_x - 1)), "gx", True)
-    ghost_low_y, ghost_high_y = ghost_pair(filled(at_y(0)), filled(at_y(len_y - 1)), "yz", False)
-    grid_cells = filled(lambda cells: cells)
+    grid_cells, head_x, tail_x, head_y, tail_y = fill_blocks(block_targets[0, 0], grid_cells, stacked)
+    ghost_low_x, ghost_high_x = ghost_pair(head_x, tail_x, "gx", True)
+    ghost_low_y, ghost_high_y = ghost_pair(head_y, tail_y, "yz", False)
     updated = stencil(grid_cells, ghost_low_x, ghost_high_x, ghost_low_y, ghost_high_y)
     return updated[None]
 

time: 51.4 us -> 49.3 us (0.959)
  the two profiles are of different devices: /device:TPU:9 before, /device:TPU:7 now
where the time goes in v10:
time: 49.3 us; the launch traced here: 48.9 us
  Pallas kernels  15.5 us (31%)
  starting transfers between devices  11.5 us (23%)
  local copies, waits for them, and re-layouts  8.05 us (16%)
  matrix products  6.54 us (13%)
  waiting for transfers between devices  5.24 us (11%)
  other arithmetic  1.96 us (4%)
    ppermute x4, starting transfers between devices, ghost_pair(): return (lax.ppermute(tail, axis, up), lax.ppermute(head, axis, down))  11.5 us
    pallas_call x1, Pallas kernels, route_blocks(): pl.pallas_call(route_kernel, out_shape=jax.ShapeDtypeStruct(send_cells.sh...  7.65 us
    ppermute x4, waiting for transfers between devices, ghost_pair(): return (lax.ppermute(tail, axis, up), lax.ppermute(head, axis, down))  5.24 us
    pallas_call x1, Pallas kernels, stencil(): pl.pallas_call(stencil_kernel, out_shape=jax.ShapeDtypeStruct(grid_cells....  5.01 us
    dot_general x1, matrix products, local(): jnp.einsum('jkcs,jkst->jct', picked, interp_weights[0, 0], preferred_elem...  4.56 us
    pallas_call x1, Pallas kernels, fill_blocks(): pl.pallas_call(fill_kernel, out_shape=(jax.ShapeDtypeStruct(grid_cells.sh...  2.81 us
    convert_element_type x3, local copies, waits for them, and re-layouts, local(): shell_cells.transpose(1, 3, 5, 0, 2, 4, 6).reshape(-1, ncomp * volume)  2.12 us
    dot_general x1, matrix products, local(): stacked = jnp.dot(stacked, spread, precision=lax.Precision.HIGHEST)  1.58 us
  transfers between devices with their start and end apart: 4, of which 1 were waited for; matrix products, arithmetic and copies ran while one was open for 0% of the time, Pallas kernels for 0%

profile of v10, /device:TPU:7, one launch (start us, length us, event | category | flops | bytes accessed | tf_op | source)
XLA Modules:
  0.0 48.9 jit_solution(10232173300760273647)
XLA Ops:
  0.0 0.8 %convert_reduce_fusion.1 = s32[8]{0:T(128)S(1)} fusion(s32[1,8,8]{2,1,0:T(8,128)} %param.6, s32[]{:T(128)S(6)} %axis_index.12), kind=kLoop, calls=%fused_computation.16 | loop fusion | flops 184 | bytes 292 | tf_op jit(solution)/shard_map/reduce_sum | solution.py:337
  0.8 0.8 %eq.53 = s32[16]{0:T(128)S(1)} reshape(s32[1,1,4,4]{3,2,1,0:T(4,128)} %param.7) | data formatting | bytes 128 | tf_op jit(solution)/shard_map/eq | solution.py:344
  1.6 0.2 reduce-window.8
  1.8 0.7 %dynamic-slice_bitcast_fusion = s32[8]{0:T(128)S(1)} fusion(s32[1,8,8]{2,1,0:T(8,128)} %param.6, s32[]{:T(128)S(6)} %select_n.24), kind=kLoop, calls=%fused_computation.30 | loop fusion | bytes 68 | tf_op jit(solution)/shard_map/jit(dynamic_index_in_dim)/squeeze | solution.py:322
  2.5 0.2 convert_reduce_fusion
  2.7 0.7 %multiply_add_fusion = s32[8]{0:T(128)S(1)} fusion(s32[8]{0:T(128)S(1)} %convert_reduce_fusion, s32[1,8,8]{2,1,0:T(8,128)} %param.6, s32[]{:T(128)S(6)} %select_n.24), kind=kLoop, calls=%fused_computation.29 | loop fusion | flops 16 | bytes 100 | tf_op jit(solution)/shard_map/add | solution.py:328
  3.4 0.1 add_select_fusion
  3.4 0.1 select_n.23
  3.5 1.4 %slice.7 = bf16[8,16,16,16]{3,2,1,0:T(8,128)(2,1)S(1)} slice(f32[8,16,16,128]{3,2,1,0:T(8,128)} %bitcast.38), slice={[0:8], [0:16], [0:16], [112:128]} | slice | bytes 131072 | tf_op jit(solution)/shard_map/slice | solution.py:315
  4.9 0.4 convert_element_type.28
  5.3 0.2 copy.12
  5.6 1.5 %convert_element_type.30 = bf16[8,4096]{1,0:T(8,128)(2,1)S(1)} reshape(bf16[2,2,2,8,8,8,8]{6,5,4,3,2,1,0:T(8,128)(2,1)S(1)} %bitcast.37) | data formatting | bytes 131072 | tf_op jit(solution)/shard_map/convert_element_type | solution.py:318
  7.1 0.2 convolution_convert_fusion.1
  7.3 0.7 %reshape.101.send_ref = bf16[8,16,512]{2,1,0:T(8,128)(2,1)} reshape(bf16[16,4096]{1,0:T(8,128)(2,1)S(1)} %convolution_convert_fusion.1) | data formatting | bytes 262144 | tf_op jit(solution)/shard_map/reshape | solution.py:334
  8.0 7.7 %shard_map.55 = bf16[8,16,512]{2,1,0:T(8,128)(2,1)} custom-call(bf16[8,16,512]{2,1,0:T(8,128)(2,1)} %reshape.101.send_ref), custom_call_target="tpu_custom_call" | custom-call | tf_op jit(solution)/shard_map/pallas_call | solution.py:115
  15.6 1.0 %reshape.102 = bf16[16,4096]{1,0:T(8,128)(2,1)S(1)} reshape(bf16[8,16,512]{2,1,0:T(8,128)(2,1)} %shard_map.55) | data formatting | bytes 262144 | tf_op jit(solution)/shard_map/reshape | solution.py:335
  16.6 0.2 convolution_convert_fusion
  16.9 4.6 %fusion.2 = f32[4,8,512]{2,1,0:T(8,128)S(1)} fusion(bf16[4,4,8,512]{3,2,1,0:T(8,128)(2,1)S(1)} %bitcast.40, bf16[1,1,4,4,512,512]{5,4,3,2,1,0:T(8,128)(2,1)} %param.9), kind=kOutput, calls=%fused_computation.4 | convolution fusion | flops 67108864 | bytes 8585216 | tf_op jit(solution)/shard_map/jkcs,jkst->jct/dot_general | solution.py:350
  21.5 0.6 %dot_general.17 = f32[4,8,8,8,8]{4,3,2,1,0:T(8,128)S(1)} reshape(f32[4,8,512]{2,1,0:T(8,128)S(1)} %fusion.2) | data formatting | bytes 131072 | tf_op jit(solution)/shard_map/dot_general | solution.py:358
  22.1 1.6 %fusion.13.stacked_ref = f32[4,8,8,8,128]{4,3,2,1,0:T(8,128)} fusion(f32[4,8,8,8,8]{4,3,2,1,0:T(8,128)S(1)} %dot_general.17, s32[128]{0:T(128)S(1)} %get-tuple-element.15, s32[128]{0:T(128)S(1)} %get-tuple-element.16, pred[128]{0:T(512)(128)(4,1)S(1)} %compare_and_fusion), kind=kOutput, calls=%fused_computation.22 | convolution fusion | flops 25167872 | bytes 1115264 | tf_op jit(solution)/shard_map/dot_general | solution.py:358
  23.6 2.8 %shard_map.56 = (f32[8,16,16,128]{3,2,1,0:T(8,128)}, f32[8,16,128]{2,1,0:T(8,128)}, f32[8,16,128]{2,1,0:T(8,128)}, f32[8,16,128]{2,1,0:T(8,128)}, f32[8,16,128]{2,1,0:T(8,128)}) custom-call(s32[4]{0:T(128)} %bitcast.43, f32[8,16,16,128]{3,2,1,0:T(8,128)} %bitcast.39, f32[4,8,8,8,128]{4,3,2,1,0:T(8,128)} %fusion.13.stacked_ref), custom_call_target="tpu_custom_call" | custom-call | tf_op jit(solution)/shard_map/pallas_call | solution.py:296
  26.5 2.8 %collective-permute-start = (f32[8,16,128]{2,1,0:T(8,128)}, f32[8,16,128]{2,1,0:T(8,128)S(1)}, u32[]{:S(2)}, u32[]{:S(2)}) collective-permute-start(f32[8,16,128]{2,1,0:T(8,128)} %get-tuple-element.11), channel_id=1, source_target_pairs={{0,8},{8,16},{16,24},{24,32},{32,40},{40,48},{48,56},{56,0},{1,9},... | collective-permute-start | bytes 196616 | tf_op jit(solution)/shard_map/ppermute | solution.py:136
  29.2 3.5 %collective-permute-start.1 = (f32[8,16,128]{2,1,0:T(8,128)}, f32[8,16,128]{2,1,0:T(8,128)S(1)}, u32[]{:S(2)}, u32[]{:S(2)}) collective-permute-start(f32[8,16,128]{2,1,0:T(8,128)} %get-tuple-element.12), channel_id=1, source_target_pairs={{8,0},{16,8},{24,16},{32,24},{40,32},{48,40},{56,48},{0,56},{9,1},... | collective-permute-start | bytes 196616 | tf_op jit(solution)/shard_map/ppermute | solution.py:136
  32.7 3.1 %collective-permute-start.2 = (f32[8,16,128]{2,1,0:T(8,128)}, f32[8,16,128]{2,1,0:T(8,128)S(1)}, u32[]{:S(2)}, u32[]{:S(2)}) collective-permute-start(f32[8,16,128]{2,1,0:T(8,128)} %get-tuple-element.13), channel_id=1, source_target_pairs={{0,1},{1,2},{2,3},{3,4},{4,5},{5,6},{6,7},{8,9},{9,10},{10,11},{11... | collective-permute-start | bytes 196616 | tf_op jit(solution)/shard_map/ppermute | solution.py:136
  35.8 2.2 %collective-permute-start.3 = (f32[8,16,128]{2,1,0:T(8,128)}, f32[8,16,128]{2,1,0:T(8,128)S(1)}, u32[]{:S(2)}, u32[]{:S(2)}) collective-permute-start(f32[8,16,128]{2,1,0:T(8,128)} %get-tuple-element.14), channel_id=1, source_target_pairs={{1,0},{2,1},{3,2},{4,3},{5,4},{6,5},{7,6},{9,8},{10,9},{11,10},{12... | collective-permute-start | bytes 196616 | tf_op jit(solution)/shard_map/ppermute | solution.py:136
  38.0 0.0 collective-permute-done.low_x_ref
  38.0 0.0 copy-start
  38.0 0.0 collective-permute-done.1.high_x_ref
  38.0 0.0 copy-start.1
  38.0 0.0 collective-permute-done.2.low_y_ref
  38.0 0.0 copy-start.2
  38.0 5.2 %collective-permute-done.3.high_y_ref = f32[8,16,128]{2,1,0:T(8,128)S(1)} collective-permute-done((f32[8,16,128]{2,1,0:T(8,128)}, f32[8,16,128]{2,1,0:T(8,128)S(1)}, u32[]{:S(2)}, u32[]{:S(2)}) %collective-permute-start.3) | collective-permute-done | bytes 65568 | tf_op jit(solution)/shard_map/ppermute | solution.py:136
  43.3 0.0 copy-start.3
  43.3 0.0 copy-done
  43.3 0.0 copy-done.1
  43.3 0.0 copy-done.2
  43.3 0.6 %copy-done.3 = f32[8,16,128]{2,1,0:T(8,128)} copy-done((f32[8,16,128]{2,1,0:T(8,128)}, f32[8,16,128]{2,1,0:T(8,128)S(1)}, u32[]{:S(2)}) %copy-start.3) | copy-done | bytes 65560
  43.9 5.0 %shard_map.57 = f32[8,16,16,128]{3,2,1,0:T(8,128)} custom-call(f32[8,16,16,128]{3,2,1,0:T(8,128)} %get-tuple-element.10.grid_ref, f32[8,16,128]{2,1,0:T(8,128)} %copy-done, f32[8,16,128]{2,1,0:T(8,128)} %copy-done.1, f32[8,16,128]{2,1,0:T(8,128)} %copy-done.2, f32[8,16,128]{2,1,0:T(8,128)} %copy-done.3), custom_call_target="tpu_custom_call" | custom-call | tf_op jit(solution)/shard_map/pallas_call | solution.py:257
  (5 shorter events, 0.1 us)
Async XLA Ops:
  26.5 11.5 %collective-permute-start = (f32[8,16,128]{2,1,0:T(8,128)}, f32[8,16,128]{2,1,0:T(8,128)S(1)}, u32[]{:S(2)}, u32[]{:S(2)}) collective-permute-start(f32[8,16,128]{2,1,0:T(8,128)} %get-tuple-element.11), channel_id=1, source_target_pairs={{0,8},{8,16},{16,24},{24,32},{32,40},{40,48},{48,56},{56,0},{1,9},... | collective-permute-start | bytes 196616 | tf_op jit(solution)/shard_map/ppermute | solution.py:136
  29.2 8.8 %collective-permute-start.1 = (f32[8,16,128]{2,1,0:T(8,128)}, f32[8,16,128]{2,1,0:T(8,128)S(1)}, u32[]{:S(2)}, u32[]{:S(2)}) collective-permute-start(f32[8,16,128]{2,1,0:T(8,128)} %get-tuple-element.12), channel_id=1, source_target_pairs={{8,0},{16,8},{24,16},{32,24},{40,32},{48,40},{56,48},{0,56},{9,1},... | collective-permute-start | bytes 196616 | tf_op jit(solution)/shard_map/ppermute | solution.py:136
  32.7 5.3 %collective-permute-start.2 = (f32[8,16,128]{2,1,0:T(8,128)}, f32[8,16,128]{2,1,0:T(8,128)S(1)}, u32[]{:S(2)}, u32[]{:S(2)}) collective-permute-start(f32[8,16,128]{2,1,0:T(8,128)} %get-tuple-element.13), channel_id=1, source_target_pairs={{0,1},{1,2},{2,3},{3,4},{4,5},{5,6},{6,7},{8,9},{9,10},{10,11},{11... | collective-permute-start | bytes 196616 | tf_op jit(solution)/shard_map/ppermute | solution.py:136
  35.8 7.5 %collective-permute-start.3 = (f32[8,16,128]{2,1,0:T(8,128)}, f32[8,16,128]{2,1,0:T(8,128)S(1)}, u32[]{:S(2)}, u32[]{:S(2)}) collective-permute-start(f32[8,16,128]{2,1,0:T(8,128)} %get-tuple-element.14), channel_id=1, source_target_pairs={{1,0},{2,1},{3,2},{4,3},{5,4},{6,5},{7,6},{9,8},{10,9},{11,10},{12... | collective-permute-start | bytes 196616 | tf_op jit(solution)/shard_map/ppermute | solution.py:136
  38.0 5.3 %copy-start = (f32[8,16,128]{2,1,0:T(8,128)}, f32[8,16,128]{2,1,0:T(8,128)S(1)}, u32[]{:S(2)}) copy-start(f32[8,16,128]{2,1,0:T(8,128)S(1)} %collective-permute-done.low_x_ref) | copy-start | bytes 196612
  38.0 5.3 %copy-start.1 = (f32[8,16,128]{2,1,0:T(8,128)}, f32[8,16,128]{2,1,0:T(8,128)S(1)}, u32[]{:S(2)}) copy-start(f32[8,16,128]{2,1,0:T(8,128)S(1)} %collective-permute-done.1.high_x_ref) | copy-start | bytes 196612
  38.0 5.3 %copy-start.2 = (f32[8,16,128]{2,1,0:T(8,128)}, f32[8,16,128]{2,1,0:T(8,128)S(1)}, u32[]{:S(2)}) copy-start(f32[8,16,128]{2,1,0:T(8,128)S(1)} %collective-permute-done.2.low_y_ref) | copy-start | bytes 196612
  43.3 0.6 %copy-start.3 = (f32[8,16,128]{2,1,0:T(8,128)}, f32[8,16,128]{2,1,0:T(8,128)S(1)}, u32[]{:S(2)}) copy-start(f32[8,16,128]{2,1,0:T(8,128)S(1)} %collective-permute-done.3.high_y_ref) | copy-start | bytes 196612

commit v11 on v10

--- a/solution.py
+++ b/solution.py
@@ -301,6 +301,54 @@
     )(targets, grid_cells, stacked)
 
 
+def halo_kernel(low_x_ref, high_x_ref, low_y_ref, high_y_ref, out_ref, landed, send_sem, recv_sem):
+    column = lax.axis_index("gx")
+    row = lax.axis_index("yz")
+    gx_count = lax.axis_size("gx")
+    yz_count = lax.axis_size("yz")
+    up_x = {"gx": lax.rem(column + 1, gx_count)}
+    down_x = {"gx": lax.rem(column + gx_count - 1, gx_count)}
+    up_y = {"yz": lax.rem(row + 1, yz_count)}
+    down_y = {"yz": lax.rem(row + yz_count - 1, yz_count)}
+    barrier = pltpu.get_barrier_semaphore()
+    for partner in (up_x, down_x, up_y, down_y):
+        pl.semaphore_signal(barrier, inc=1, device_id=partner, device_id_type=MESH)
+    pl.semaphore_wait(barrier, 4)
+    sends = ((high_x_ref, up_x), (low_x_ref, down_x), (high_y_ref, up_y), (low_y_ref, down_y))
+    copies = []
+    for slot, (source, partner) in enumerate(sends):
+        copy = pltpu.make_async_remote_copy(
+            src_ref=source,
+            dst_ref=landed.at[slot],
+            send_sem=send_sem.at[slot],
+            recv_sem=recv_sem.at[slot],
+            device_id=partner,
+            device_id_type=MESH,
+        )
+        copy.start()
+        copies.append(copy)
+    for copy in copies:
+        copy.wait()
+    out_ref[...] = landed[...]
+
+
+def exchange_faces(low_x, high_x, low_y, high_y):
+    face = (4,) + low_x.shape
+    vmem = pl.BlockSpec(memory_space=pltpu.VMEM)
+    return pl.pallas_call(
+        halo_kernel,
+        out_shape=jax.ShapeDtypeStruct(face, low_x.dtype),
+        in_specs=[vmem] * 4,
+        out_specs=vmem,
+        scratch_shapes=[
+            pltpu.VMEM(face, low_x.dtype),
+            pltpu.SemaphoreType.DMA((4,)),
+            pltpu.SemaphoreType.DMA((4,)),
+        ],
+        compiler_params=pltpu.CompilerParams(collective_id=1, has_side_effects=True),
+    )(low_x, high_x, low_y, high_y)
+
+
 def local(field_state, shell_owner, block_sources, block_targets, interp_weights):
     grid_cells = field_state[0]
     ncomp, len_x, len_y, len_z = grid_cells.shape
@@ -358,8 +406,8 @@
     stacked = jnp.dot(stacked, spread, precision=lax.Precision.HIGHEST)
     stacked = stacked.reshape(slots_here, ncomp, BLK, BLK, len_z)
     grid_cells, head_x, tail_x, head_y, tail_y = fill_blocks(block_targets[0, 0], grid_cells, stacked)
-    ghost_low_x, ghost_high_x = ghost_pair(head_x, tail_x, "gx", True)
-    ghost_low_y, ghost_high_y = ghost_pair(head_y, tail_y, "yz", False)
+    ghosts = exchange_faces(head_x, tail_x, head_y, tail_y)
+    ghost_low_x, ghost_high_x, ghost_low_y, ghost_high_y = (ghosts[n] for n in range(4))
     updated = stencil(grid_cells, ghost_low_x, ghost_high_x, ghost_low_y, ghost_high_y)
     return updated[None]
 

time: 49.3 us -> 48.4 us (0.982)
  the two profiles are of different devices: /device:TPU:7 before, /device:TPU:1 now
where the time goes in v11:
time: 48.4 us; the launch traced here: 47.9 us
  Pallas kernels  30.3 us (63%)
  local copies, waits for them, and re-layouts  9.07 us (19%)
  matrix products  6.54 us (14%)
  other arithmetic  1.95 us (4%)
    pallas_call x1, Pallas kernels, exchange_faces(): pl.pallas_call(halo_kernel, out_shape=jax.ShapeDtypeStruct(face, low_x.dt...  13.4 us
    pallas_call x1, Pallas kernels, route_blocks(): pl.pallas_call(route_kernel, out_shape=jax.ShapeDtypeStruct(send_cells.sh...  9.02 us
    pallas_call x1, Pallas kernels, stencil(): pl.pallas_call(stencil_kernel, out_shape=jax.ShapeDtypeStruct(grid_cells....  5.01 us
    dot_general x1, matrix products, local(): jnp.einsum('jkcs,jkst->jct', picked, interp_weights[0, 0], preferred_elem...  4.56 us
    pallas_call x1, Pallas kernels, fill_blocks(): pl.pallas_call(fill_kernel, out_shape=(jax.ShapeDtypeStruct(grid_cells.sh...  2.83 us
    convert_element_type x3, local copies, waits for them, and re-layouts, local(): shell_cells.transpose(1, 3, 5, 0, 2, 4, 6).reshape(-1, ncomp * volume)  2.12 us
    squeeze x1, local copies, waits for them, and re-layouts, local(): ghosts[n]  1.65 us
    dot_general x1, matrix products, local(): stacked = jnp.dot(stacked, spread, precision=lax.Precision.HIGHEST)  1.58 us

profile of v11, /device:TPU:1, one launch (start us, length us, event | category | flops | bytes accessed | tf_op | source)
XLA Modules:
  0.0 47.9 jit_solution(2214931696341125422)
XLA Ops:
  0.0 0.8 %convert_reduce_fusion.1 = s32[8]{0:T(128)S(1)} fusion(s32[1,8,8]{2,1,0:T(8,128)} %param.6, s32[]{:T(128)S(6)} %axis_index.12), kind=kLoop, calls=%fused_computation.20 | loop fusion | flops 184 | bytes 292 | tf_op jit(solution)/shard_map/reduce_sum | solution.py:385
  0.8 0.8 %eq.53 = s32[16]{0:T(128)S(1)} reshape(s32[1,1,4,4]{3,2,1,0:T(4,128)} %param.7) | data formatting | bytes 128 | tf_op jit(solution)/shard_map/eq | solution.py:392
  1.6 0.2 reduce-window.8
  1.8 0.7 %dynamic-slice_bitcast_fusion = s32[8]{0:T(128)S(1)} fusion(s32[1,8,8]{2,1,0:T(8,128)} %param.6, s32[]{:T(128)S(6)} %select_n.24), kind=kLoop, calls=%fused_computation.34 | loop fusion | bytes 68 | tf_op jit(solution)/shard_map/jit(dynamic_index_in_dim)/squeeze | solution.py:370
  2.5 0.2 convert_reduce_fusion
  2.6 0.7 %multiply_add_fusion = s32[8]{0:T(128)S(1)} fusion(s32[8]{0:T(128)S(1)} %convert_reduce_fusion, s32[1,8,8]{2,1,0:T(8,128)} %param.6, s32[]{:T(128)S(6)} %select_n.24), kind=kLoop, calls=%fused_computation.33 | loop fusion | flops 16 | bytes 100 | tf_op jit(solution)/shard_map/add | solution.py:376
  3.3 0.1 add_select_fusion
  3.4 0.1 select_n.23
  3.5 1.4 %slice.27 = bf16[8,16,16,16]{3,2,1,0:T(8,128)(2,1)S(1)} slice(f32[8,16,16,128]{3,2,1,0:T(8,128)} %bitcast.46), slice={[0:8], [0:16], [0:16], [112:128]} | slice | bytes 131072 | tf_op jit(solution)/shard_map/slice | solution.py:363
  4.9 0.4 convert_element_type.28
  5.3 0.2 copy.12
  5.6 1.5 %convert_element_type.30 = bf16[8,4096]{1,0:T(8,128)(2,1)S(1)} reshape(bf16[2,2,2,8,8,8,8]{6,5,4,3,2,1,0:T(8,128)(2,1)S(1)} %bitcast.45) | data formatting | bytes 131072 | tf_op jit(solution)/shard_map/convert_element_type | solution.py:366
  7.1 0.2 convolution_convert_fusion.1
  7.2 0.7 %reshape.101.send_ref = bf16[8,16,512]{2,1,0:T(8,128)(2,1)} reshape(bf16[16,4096]{1,0:T(8,128)(2,1)S(1)} %convolution_convert_fusion.1) | data formatting | bytes 262144 | tf_op jit(solution)/shard_map/reshape | solution.py:382
  8.0 9.0 %shard_map.55 = bf16[8,16,512]{2,1,0:T(8,128)(2,1)} custom-call(bf16[8,16,512]{2,1,0:T(8,128)(2,1)} %reshape.101.send_ref), custom_call_target="tpu_custom_call" | custom-call | tf_op jit(solution)/shard_map/pallas_call | solution.py:115
  17.0 1.0 %reshape.102 = bf16[16,4096]{1,0:T(8,128)(2,1)S(1)} reshape(bf16[8,16,512]{2,1,0:T(8,128)(2,1)} %shard_map.55) | data formatting | bytes 262144 | tf_op jit(solution)/shard_map/reshape | solution.py:383
  18.0 0.2 convolution_convert_fusion
  18.2 4.6 %fusion.2 = f32[4,8,512]{2,1,0:T(8,128)S(1)} fusion(bf16[4,4,8,512]{3,2,1,0:T(8,128)(2,1)S(1)} %bitcast.48, bf16[1,1,4,4,512,512]{5,4,3,2,1,0:T(8,128)(2,1)} %param.9), kind=kOutput, calls=%fused_computation.4 | convolution fusion | flops 67108864 | bytes 8585216 | tf_op jit(solution)/shard_map/jkcs,jkst->jct/dot_general | solution.py:398
  22.8 0.6 %dot_general.17 = f32[4,8,8,8,8]{4,3,2,1,0:T(8,128)S(1)} reshape(f32[4,8,512]{2,1,0:T(8,128)S(1)} %fusion.2) | data formatting | bytes 131072 | tf_op jit(solution)/shard_map/dot_general | solution.py:406
  23.4 1.6 %fusion.13.stacked_ref = f32[4,8,8,8,128]{4,3,2,1,0:T(8,128)} fusion(f32[4,8,8,8,8]{4,3,2,1,0:T(8,128)S(1)} %dot_general.17, s32[128]{0:T(128)S(1)} %get-tuple-element.19, s32[128]{0:T(128)S(1)} %get-tuple-element.20, pred[128]{0:T(512)(128)(4,1)S(1)} %compare_and_fusion), kind=kOutput, calls=%fused_computation.26 | convolution fusion | flops 25167872 | bytes 1115264 | tf_op jit(solution)/shard_map/dot_general | solution.py:406
  25.0 2.8 %shard_map.56 = (f32[8,16,16,128]{3,2,1,0:T(8,128)}, f32[8,16,128]{2,1,0:T(8,128)}, f32[8,16,128]{2,1,0:T(8,128)}, f32[8,16,128]{2,1,0:T(8,128)}, f32[8,16,128]{2,1,0:T(8,128)}) custom-call(s32[4]{0:T(128)} %bitcast.51, f32[8,16,16,128]{3,2,1,0:T(8,128)} %bitcast.47, f32[4,8,8,8,128]{4,3,2,1,0:T(8,128)} %fusion.13.stacked_ref), custom_call_target="tpu_custom_call" | custom-call | tf_op jit(solution)/shard_map/pallas_call | solution.py:296
  27.8 13.4 %shard_map.57 = f32[4,8,16,128]{3,2,1,0:T(8,128)} custom-call(f32[8,16,128]{2,1,0:T(8,128)} %get-tuple-element.11.low_x_ref, f32[8,16,128]{2,1,0:T(8,128)} %get-tuple-element.12.high_x_ref, f32[8,16,128]{2,1,0:T(8,128)} %get-tuple-element.13.low_y_ref, f32[8,16,128]{2,1,0:T(8,128)} %get-tuple-element.14.high_y_ref), custom_call_target="tpu_custom_call" | custom-call | tf_op jit(solution)/shard_map/pallas_call | solution.py:338
  41.2 1.7 %slice_bitcast_fusion = (f32[8,16,128]{2,1,0:T(8,128)}, f32[8,16,128]{2,1,0:T(8,128)}, f32[8,16,128]{2,1,0:T(8,128)}, f32[8,16,128]{2,1,0:T(8,128)}) fusion(f32[4,8,16,128]{3,2,1,0:T(8,128)} %shard_map.57), kind=kLoop, calls=%fused_computation.7 | loop fusion | bytes 524288 | tf_op jit(solution)/shard_map/squeeze | solution.py:410
  42.9 5.0 %shard_map.58 = f32[8,16,16,128]{3,2,1,0:T(8,128)} custom-call(f32[8,16,16,128]{3,2,1,0:T(8,128)} %get-tuple-element.10.grid_ref, f32[8,16,128]{2,1,0:T(8,128)} %get-tuple-element.18.low_x_ref, f32[8,16,128]{2,1,0:T(8,128)} %get-tuple-element.17.high_x_ref, f32[8,16,128]{2,1,0:T(8,128)} %get-tuple-element.16.low_y_ref, ...), custom_call_target="tpu_custom_call" | custom-call | tf_op jit(solution)/shard_map/pallas_call | solution.py:257
  (5 shorter events, 0.1 us)

commit v12 on v11

--- a/solution.py
+++ b/solution.py
@@ -366,7 +366,7 @@
         shell_cells.transpose(1, 3, 5, 0, 2, 4, 6).reshape(-1, ncomp * volume).astype(jnp.bfloat16)
     )
     count_here = shell_cells.shape[0]
-    owner_table = shell_owner[0]
+    shell_cells, owner_table = lax.optimization_barrier((shell_cells, shell_owner[0]))
     own_owner = lax.dynamic_index_in_dim(owner_table, yz_index, 0, keepdims=False)
     index_here = jnp.arange(count_here, dtype=jnp.int32)
     local_same = own_owner[None, :] == own_owner[:, None]
@@ -381,6 +381,9 @@
     )
     send_cells = send_cells.astype(jnp.bfloat16).reshape(yz_count, CAP * ncomp, volume)
     got_cells = route_blocks(send_cells).reshape(slot_count, ncomp * volume)
+    got_cells, owner_table, block_sources = lax.optimization_barrier(
+        (got_cells, shell_owner[0], block_sources)
+    )
     mine = (owner_table == yz_index).astype(jnp.int32)
     per_sender = jnp.sum(mine, axis=1)
     before = jnp.cumsum(per_sender) - per_sender

time: 48.4 us -> 48.4 us (level)
    eq x0 -> x1, local copies, waits for them, and re-layouts: none -> 0.7 us  [local(): local_same = own_owner[None, :] == own_owner[:, None]]
    add x1 -> x0, other arithmetic: 0.7 us -> none  [local(): slot_of = own_owner * CAP + rank_local]
    eq x0 -> x1, other arithmetic: none -> 0.7 us  [local(): jnp.arange(slot_count, dtype=jnp.int32)[:, None] == slot_of[None, :]]
    squeeze x1 -> x0, local copies, waits for them, and re-layouts: 0.69 us -> none  [local(): lax.dynamic_index_in_dim(owner_table, yz_index, 0, keepdims=False)]
where the time goes in v12:
time: 48.4 us; the launch traced here: 47.9 us
  Pallas kernels  30.3 us (63%)
  local copies, waits for them, and re-layouts  9.07 us (19%)
  matrix products  6.54 us (14%)
  other arithmetic  1.96 us (4%)
    pallas_call x1, Pallas kernels, exchange_faces(): pl.pallas_call(halo_kernel, out_shape=jax.ShapeDtypeStruct(face, low_x.dt...  13.4 us
    pallas_call x1, Pallas kernels, route_blocks(): pl.pallas_call(route_kernel, out_shape=jax.ShapeDtypeStruct(send_cells.sh...  9.02 us
    pallas_call x1, Pallas kernels, stencil(): pl.pallas_call(stencil_kernel, out_shape=jax.ShapeDtypeStruct(grid_cells....  5.01 us
    dot_general x1, matrix products, local(): jnp.einsum('jkcs,jkst->jct', picked, interp_weights[0, 0], preferred_elem...  4.56 us
    pallas_call x1, Pallas kernels, fill_blocks(): pl.pallas_call(fill_kernel, out_shape=(jax.ShapeDtypeStruct(grid_cells.sh...  2.83 us
    convert_element_type x3, local copies, waits for them, and re-layouts, local(): shell_cells.transpose(1, 3, 5, 0, 2, 4, 6).reshape(-1, ncomp * volume)  2.12 us
    squeeze x1, local copies, waits for them, and re-layouts, local(): ghosts[n]  1.65 us
    dot_general x1, matrix products, local(): stacked = jnp.dot(stacked, spread, precision=lax.Precision.HIGHEST)  1.58 us

profile of v12, /device:TPU:1, one launch (start us, length us, event | category | flops | bytes accessed | tf_op | source)
XLA Modules:
  0.0 47.9 jit_solution(11984096144502938048)
XLA Ops:
  0.0 1.4 %slice.27 = bf16[8,16,16,16]{3,2,1,0:T(8,128)(2,1)S(1)} slice(f32[8,16,16,128]{3,2,1,0:T(8,128)} %bitcast.51), slice={[0:8], [0:16], [0:16], [112:128]} | slice | bytes 131072 | tf_op jit(solution)/shard_map/slice | solution.py:363
  1.4 0.4 convert_element_type.25
  1.9 0.2 copy.12
  2.1 1.5 %convert_element_type.27 = bf16[8,4096]{1,0:T(8,128)(2,1)S(1)} reshape(bf16[2,2,2,8,8,8,8]{6,5,4,3,2,1,0:T(8,128)(2,1)S(1)} %bitcast.50) | data formatting | bytes 131072 | tf_op jit(solution)/shard_map/convert_element_type | solution.py:366
  3.6 0.7 %fusion.19 = s32[8]{0:T(128)S(1)} fusion(s32[8,8]{1,0:T(8,128)} %bitcast.55, s32[]{:T(128)S(6)} %select_n.22), kind=kLoop, calls=%fused_computation.38 | loop fusion | bytes 68 | tf_op jit(solution)/shard_map/eq | solution.py:372
  4.3 0.2 convert_reduce_fusion.1
  4.5 0.7 %fusion.18 = s32[8]{0:T(128)S(1)} fusion(s32[8]{0:T(128)S(1)} %convert_reduce_fusion.1, s32[8,8]{1,0:T(8,128)} %bitcast.56, s32[]{:T(128)S(6)} %select_n.22), kind=kLoop, calls=%fused_computation.33 | loop fusion | flops 16 | bytes 100 | tf_op jit(solution)/shard_map/eq | solution.py:378
  5.2 0.2 convolution_convert_fusion.1
  5.3 0.7 %reshape.86.send_ref = bf16[8,16,512]{2,1,0:T(8,128)(2,1)} reshape(bf16[16,4096]{1,0:T(8,128)(2,1)S(1)} %convolution_convert_fusion.1) | data formatting | bytes 262144 | tf_op jit(solution)/shard_map/reshape | solution.py:382
  6.0 9.0 %shard_map.55 = bf16[8,16,512]{2,1,0:T(8,128)(2,1)} custom-call(bf16[8,16,512]{2,1,0:T(8,128)(2,1)} %reshape.86.send_ref), custom_call_target="tpu_custom_call" | custom-call | tf_op jit(solution)/shard_map/pallas_call | solution.py:115
  15.1 1.0 %reshape.87 = bf16[16,4096]{1,0:T(8,128)(2,1)S(1)} reshape(bf16[8,16,512]{2,1,0:T(8,128)(2,1)} %shard_map.55) | data formatting | bytes 262144 | tf_op jit(solution)/shard_map/reshape | solution.py:383
  16.0 0.8 %convert_reduce_fusion = s32[8]{0:T(128)S(1)} fusion(s32[8,8]{1,0:T(8,128)} %bitcast.57, s32[]{:T(128)S(6)} %axis_index.12), kind=kLoop, calls=%fused_computation.17 | loop fusion | flops 184 | bytes 292 | tf_op jit(solution)/shard_map/reduce_sum | solution.py:388
  16.8 0.8 %eq.64 = s32[16]{0:T(128)S(1)} reshape(s32[1,1,4,4]{3,2,1,0:T(4,128)} %param.7) | data formatting | bytes 128 | tf_op jit(solution)/shard_map/eq | solution.py:395
  17.6 0.2 reduce-window.8
  17.8 0.1 add_select_fusion
  17.9 0.1 select_n.24
  18.0 0.2 convolution_convert_fusion
  18.3 4.6 %fusion.2 = f32[4,8,512]{2,1,0:T(8,128)S(1)} fusion(bf16[4,4,8,512]{3,2,1,0:T(8,128)(2,1)S(1)} %bitcast.53, bf16[1,1,4,4,512,512]{5,4,3,2,1,0:T(8,128)(2,1)} %param.9), kind=kOutput, calls=%fused_computation.4 | convolution fusion | flops 67108864 | bytes 8585216 | tf_op jit(solution)/shard_map/jkcs,jkst->jct/dot_general | solution.py:401
  22.8 0.6 %dot_general.17 = f32[4,8,8,8,8]{4,3,2,1,0:T(8,128)S(1)} reshape(f32[4,8,512]{2,1,0:T(8,128)S(1)} %fusion.2) | data formatting | bytes 131072 | tf_op jit(solution)/shard_map/dot_general | solution.py:409
  23.4 1.6 %fusion.13.stacked_ref = f32[4,8,8,8,128]{4,3,2,1,0:T(8,128)} fusion(f32[4,8,8,8,8]{4,3,2,1,0:T(8,128)S(1)} %dot_general.17, s32[128]{0:T(128)S(1)} %get-tuple-element.29, s32[128]{0:T(128)S(1)} %get-tuple-element.30, pred[128]{0:T(512)(128)(4,1)S(1)} %compare_and_fusion), kind=kOutput, calls=%fused_computation.26 | convolution fusion | flops 25167872 | bytes 1115264 | tf_op jit(solution)/shard_map/dot_general | solution.py:409
  25.0 2.8 %shard_map.56 = (f32[8,16,16,128]{3,2,1,0:T(8,128)}, f32[8,16,128]{2,1,0:T(8,128)}, f32[8,16,128]{2,1,0:T(8,128)}, f32[8,16,128]{2,1,0:T(8,128)}, f32[8,16,128]{2,1,0:T(8,128)}) custom-call(s32[4]{0:T(128)} %bitcast.59, f32[8,16,16,128]{3,2,1,0:T(8,128)} %bitcast.52, f32[4,8,8,8,128]{4,3,2,1,0:T(8,128)} %fusion.13.stacked_ref), custom_call_target="tpu_custom_call" | custom-call | tf_op jit(solution)/shard_map/pallas_call | solution.py:296
  27.8 13.4 %shard_map.57 = f32[4,8,16,128]{3,2,1,0:T(8,128)} custom-call(f32[8,16,128]{2,1,0:T(8,128)} %get-tuple-element.21.low_x_ref, f32[8,16,128]{2,1,0:T(8,128)} %get-tuple-element.22.high_x_ref, f32[8,16,128]{2,1,0:T(8,128)} %get-tuple-element.23.low_y_ref, f32[8,16,128]{2,1,0:T(8,128)} %get-tuple-element.24.high_y_ref), custom_call_target="tpu_custom_call" | custom-call | tf_op jit(solution)/shard_map/pallas_call | solution.py:338
  41.2 1.7 %slice_bitcast_fusion = (f32[8,16,128]{2,1,0:T(8,128)}, f32[8,16,128]{2,1,0:T(8,128)}, f32[8,16,128]{2,1,0:T(8,128)}, f32[8,16,128]{2,1,0:T(8,128)}) fusion(f32[4,8,16,128]{3,2,1,0:T(8,128)} %shard_map.57), kind=kLoop, calls=%fused_computation.7 | loop fusion | bytes 524288 | tf_op jit(solution)/shard_map/squeeze | solution.py:413
  42.9 5.0 %shard_map.58 = f32[8,16,16,128]{3,2,1,0:T(8,128)} custom-call(f32[8,16,16,128]{3,2,1,0:T(8,128)} %get-tuple-element.20.grid_ref, f32[8,16,128]{2,1,0:T(8,128)} %get-tuple-element.28.low_x_ref, f32[8,16,128]{2,1,0:T(8,128)} %get-tuple-element.27.high_x_ref, f32[8,16,128]{2,1,0:T(8,128)} %get-tuple-element.26.low_y_ref, ...), custom_call_target="tpu_custom_call" | custom-call | tf_op jit(solution)/shard_map/pallas_call | solution.py:257
  (5 shorter events, 0.1 us)

commit v13 on v10

--- a/solution.py
+++ b/solution.py
@@ -318,7 +318,7 @@
         shell_cells.transpose(1, 3, 5, 0, 2, 4, 6).reshape(-1, ncomp * volume).astype(jnp.bfloat16)
     )
     count_here = shell_cells.shape[0]
-    owner_table = shell_owner[0]
+    shell_cells, owner_table = lax.optimization_barrier((shell_cells, shell_owner[0]))
     own_owner = lax.dynamic_index_in_dim(owner_table, yz_index, 0, keepdims=False)
     index_here = jnp.arange(count_here, dtype=jnp.int32)
     local_same = own_owner[None, :] == own_owner[:, None]
@@ -333,6 +333,9 @@
     )
     send_cells = send_cells.astype(jnp.bfloat16).reshape(yz_count, CAP * ncomp, volume)
     got_cells = route_blocks(send_cells).reshape(slot_count, ncomp * volume)
+    got_cells, owner_table, block_sources = lax.optimization_barrier(
+        (got_cells, shell_owner[0], block_sources)
+    )
     mine = (owner_table == yz_index).astype(jnp.int32)
     per_sender = jnp.sum(mine, axis=1)
     before = jnp.cumsum(per_sender) - per_sender

time: 49.3 us -> 49.3 us (level)
    eq x0 -> x1, local copies, waits for them, and re-layouts: none -> 0.7 us  [local(): local_same = own_owner[None, :] == own_owner[:, None]]
    eq x0 -> x1, other arithmetic: none -> 0.7 us  [local(): jnp.arange(slot_count, dtype=jnp.int32)[:, None] == slot_of[None, :]]
    add x1 -> x0, other arithmetic: 0.7 us -> none  [local(): slot_of = own_owner * CAP + rank_local]
    squeeze x1 -> x0, local copies, waits for them, and re-layouts: 0.69 us -> none  [local(): lax.dynamic_index_in_dim(owner_table, yz_index, 0, keepdims=False)]
where the time goes in v13:
time: 49.3 us; the launch traced here: 48.9 us
  Pallas kernels  15.4 us (31%)
  starting transfers between devices  11.6 us (24%)
  local copies, waits for them, and re-layouts  8.05 us (16%)
  matrix products  6.54 us (13%)
  waiting for transfers between devices  5.17 us (10%)
  other arithmetic  1.96 us (4%)
    ppermute x4, starting transfers between devices, ghost_pair(): return (lax.ppermute(tail, axis, up), lax.ppermute(head, axis, down))  11.6 us
    pallas_call x1, Pallas kernels, route_blocks(): pl.pallas_call(route_kernel, out_shape=jax.ShapeDtypeStruct(send_cells.sh...  7.65 us
    ppermute x4, waiting for transfers between devices, ghost_pair(): return (lax.ppermute(tail, axis, up), lax.ppermute(head, axis, down))  5.17 us
    pallas_call x1, Pallas kernels, stencil(): pl.pallas_call(stencil_kernel, out_shape=jax.ShapeDtypeStruct(grid_cells....  5.01 us
    dot_general x1, matrix products, local(): jnp.einsum('jkcs,jkst->jct', picked, interp_weights[0, 0], preferred_elem...  4.56 us
    pallas_call x1, Pallas kernels, fill_blocks(): pl.pallas_call(fill_kernel, out_shape=(jax.ShapeDtypeStruct(grid_cells.sh...  2.78 us
    convert_element_type x3, local copies, waits for them, and re-layouts, local(): shell_cells.transpose(1, 3, 5, 0, 2, 4, 6).reshape(-1, ncomp * volume)  2.12 us
    dot_general x1, matrix products, local(): stacked = jnp.dot(stacked, spread, precision=lax.Precision.HIGHEST)  1.58 us
  transfers between devices with their start and end apart: 4, of which 1 were waited for; matrix products, arithmetic and copies ran while one was open for 0% of the time, Pallas kernels for 0%

profile of v13, /device:TPU:7, one launch (start us, length us, event | category | flops | bytes accessed | tf_op | source)
XLA Modules:
  0.0 48.9 jit_solution(14457592789441083114)
XLA Ops:
  0.0 1.4 %slice.7 = bf16[8,16,16,16]{3,2,1,0:T(8,128)(2,1)S(1)} slice(f32[8,16,16,128]{3,2,1,0:T(8,128)} %bitcast.43), slice={[0:8], [0:16], [0:16], [112:128]} | slice | bytes 131072 | tf_op jit(solution)/shard_map/slice | solution.py:315
  1.4 0.4 convert_element_type.25
  1.9 0.2 copy.12
  2.1 1.5 %convert_element_type.27 = bf16[8,4096]{1,0:T(8,128)(2,1)S(1)} reshape(bf16[2,2,2,8,8,8,8]{6,5,4,3,2,1,0:T(8,128)(2,1)S(1)} %bitcast.42) | data formatting | bytes 131072 | tf_op jit(solution)/shard_map/convert_element_type | solution.py:318
  3.6 0.7 %fusion.19 = s32[8]{0:T(128)S(1)} fusion(s32[8,8]{1,0:T(8,128)} %bitcast.47, s32[]{:T(128)S(6)} %select_n.22), kind=kLoop, calls=%fused_computation.34 | loop fusion | bytes 68 | tf_op jit(solution)/shard_map/eq | solution.py:324
  4.3 0.2 convert_reduce_fusion.1
  4.5 0.7 %fusion.18 = s32[8]{0:T(128)S(1)} fusion(s32[8]{0:T(128)S(1)} %convert_reduce_fusion.1, s32[8,8]{1,0:T(8,128)} %bitcast.48, s32[]{:T(128)S(6)} %select_n.22), kind=kLoop, calls=%fused_computation.29 | loop fusion | flops 16 | bytes 100 | tf_op jit(solution)/shard_map/eq | solution.py:330
  5.2 0.2 convolution_convert_fusion.1
  5.3 0.7 %reshape.86.send_ref = bf16[8,16,512]{2,1,0:T(8,128)(2,1)} reshape(bf16[16,4096]{1,0:T(8,128)(2,1)S(1)} %convolution_convert_fusion.1) | data formatting | bytes 262144 | tf_op jit(solution)/shard_map/reshape | solution.py:334
  6.0 7.7 %shard_map.55 = bf16[8,16,512]{2,1,0:T(8,128)(2,1)} custom-call(bf16[8,16,512]{2,1,0:T(8,128)(2,1)} %reshape.86.send_ref), custom_call_target="tpu_custom_call" | custom-call | tf_op jit(solution)/shard_map/pallas_call | solution.py:115
  13.7 1.0 %reshape.87 = bf16[16,4096]{1,0:T(8,128)(2,1)S(1)} reshape(bf16[8,16,512]{2,1,0:T(8,128)(2,1)} %shard_map.55) | data formatting | bytes 262144 | tf_op jit(solution)/shard_map/reshape | solution.py:335
  14.7 0.8 %convert_reduce_fusion = s32[8]{0:T(128)S(1)} fusion(s32[8,8]{1,0:T(8,128)} %bitcast.49, s32[]{:T(128)S(6)} %axis_index.12), kind=kLoop, calls=%fused_computation.13 | loop fusion | flops 184 | bytes 292 | tf_op jit(solution)/shard_map/reduce_sum | solution.py:340
  15.5 0.8 %eq.64 = s32[16]{0:T(128)S(1)} reshape(s32[1,1,4,4]{3,2,1,0:T(4,128)} %param.7) | data formatting | bytes 128 | tf_op jit(solution)/shard_map/eq | solution.py:347
  16.3 0.2 reduce-window.8
  16.4 0.1 add_select_fusion
  16.5 0.1 select_n.24
  16.6 0.2 convolution_convert_fusion
  16.9 4.6 %fusion.2 = f32[4,8,512]{2,1,0:T(8,128)S(1)} fusion(bf16[4,4,8,512]{3,2,1,0:T(8,128)(2,1)S(1)} %bitcast.45, bf16[1,1,4,4,512,512]{5,4,3,2,1,0:T(8,128)(2,1)} %param.9), kind=kOutput, calls=%fused_computation.4 | convolution fusion | flops 67108864 | bytes 8585216 | tf_op jit(solution)/shard_map/jkcs,jkst->jct/dot_general | solution.py:353
  21.5 0.6 %dot_general.17 = f32[4,8,8,8,8]{4,3,2,1,0:T(8,128)S(1)} reshape(f32[4,8,512]{2,1,0:T(8,128)S(1)} %fusion.2) | data formatting | bytes 131072 | tf_op jit(solution)/shard_map/dot_general | solution.py:361
  22.1 1.6 %fusion.13.stacked_ref = f32[4,8,8,8,128]{4,3,2,1,0:T(8,128)} fusion(f32[4,8,8,8,8]{4,3,2,1,0:T(8,128)S(1)} %dot_general.17, s32[128]{0:T(128)S(1)} %get-tuple-element.25, s32[128]{0:T(128)S(1)} %get-tuple-element.26, pred[128]{0:T(512)(128)(4,1)S(1)} %compare_and_fusion), kind=kOutput, calls=%fused_computation.22 | convolution fusion | flops 25167872 | bytes 1115264 | tf_op jit(solution)/shard_map/dot_general | solution.py:361
  23.6 2.8 %shard_map.56 = (f32[8,16,16,128]{3,2,1,0:T(8,128)}, f32[8,16,128]{2,1,0:T(8,128)}, f32[8,16,128]{2,1,0:T(8,128)}, f32[8,16,128]{2,1,0:T(8,128)}, f32[8,16,128]{2,1,0:T(8,128)}) custom-call(s32[4]{0:T(128)} %bitcast.51, f32[8,16,16,128]{3,2,1,0:T(8,128)} %bitcast.44, f32[4,8,8,8,128]{4,3,2,1,0:T(8,128)} %fusion.13.stacked_ref), custom_call_target="tpu_custom_call" | custom-call | tf_op jit(solution)/shard_map/pallas_call | solution.py:296
  26.4 2.9 %collective-permute-start = (f32[8,16,128]{2,1,0:T(8,128)}, f32[8,16,128]{2,1,0:T(8,128)S(1)}, u32[]{:S(2)}, u32[]{:S(2)}) collective-permute-start(f32[8,16,128]{2,1,0:T(8,128)} %get-tuple-element.21), channel_id=1, source_target_pairs={{0,8},{8,16},{16,24},{24,32},{32,40},{40,48},{48,56},{56,0},{1,9},... | collective-permute-start | bytes 196616 | tf_op jit(solution)/shard_map/ppermute | solution.py:136
  29.3 3.5 %collective-permute-start.1 = (f32[8,16,128]{2,1,0:T(8,128)}, f32[8,16,128]{2,1,0:T(8,128)S(1)}, u32[]{:S(2)}, u32[]{:S(2)}) collective-permute-start(f32[8,16,128]{2,1,0:T(8,128)} %get-tuple-element.22), channel_id=1, source_target_pairs={{8,0},{16,8},{24,16},{32,24},{40,32},{48,40},{56,48},{0,56},{9,1},... | collective-permute-start | bytes 196616 | tf_op jit(solution)/shard_map/ppermute | solution.py:136
  32.8 3.0 %collective-permute-start.2 = (f32[8,16,128]{2,1,0:T(8,128)}, f32[8,16,128]{2,1,0:T(8,128)S(1)}, u32[]{:S(2)}, u32[]{:S(2)}) collective-permute-start(f32[8,16,128]{2,1,0:T(8,128)} %get-tuple-element.23), channel_id=1, source_target_pairs={{0,1},{1,2},{2,3},{3,4},{4,5},{5,6},{6,7},{8,9},{9,10},{10,11},{11... | collective-permute-start | bytes 196616 | tf_op jit(solution)/shard_map/ppermute | solution.py:136
  35.8 2.2 %collective-permute-start.3 = (f32[8,16,128]{2,1,0:T(8,128)}, f32[8,16,128]{2,1,0:T(8,128)S(1)}, u32[]{:S(2)}, u32[]{:S(2)}) collective-permute-start(f32[8,16,128]{2,1,0:T(8,128)} %get-tuple-element.24), channel_id=1, source_target_pairs={{1,0},{2,1},{3,2},{4,3},{5,4},{6,5},{7,6},{9,8},{10,9},{11,10},{12... | collective-permute-start | bytes 196616 | tf_op jit(solution)/shard_map/ppermute | solution.py:136
  38.1 0.0 collective-permute-done.low_x_ref
  38.1 0.0 copy-start
  38.1 0.0 collective-permute-done.1.high_x_ref
  38.1 0.0 copy-start.1
  38.1 0.0 collective-permute-done.2.low_y_ref
  38.1 0.0 copy-start.2
  38.1 5.2 %collective-permute-done.3.high_y_ref = f32[8,16,128]{2,1,0:T(8,128)S(1)} collective-permute-done((f32[8,16,128]{2,1,0:T(8,128)}, f32[8,16,128]{2,1,0:T(8,128)S(1)}, u32[]{:S(2)}, u32[]{:S(2)}) %collective-permute-start.3) | collective-permute-done | bytes 65568 | tf_op jit(solution)/shard_map/ppermute | solution.py:136
  43.3 0.0 copy-start.3
  43.3 0.0 copy-done
  43.3 0.0 copy-done.1
  43.3 0.0 copy-done.2
  43.3 0.6 %copy-done.3 = f32[8,16,128]{2,1,0:T(8,128)} copy-done((f32[8,16,128]{2,1,0:T(8,128)}, f32[8,16,128]{2,1,0:T(8,128)S(1)}, u32[]{:S(2)}) %copy-start.3) | copy-done | bytes 65560
  43.9 5.0 %shard_map.57 = f32[8,16,16,128]{3,2,1,0:T(8,128)} custom-call(f32[8,16,16,128]{3,2,1,0:T(8,128)} %get-tuple-element.20.grid_ref, f32[8,16,128]{2,1,0:T(8,128)} %copy-done, f32[8,16,128]{2,1,0:T(8,128)} %copy-done.1, f32[8,16,128]{2,1,0:T(8,128)} %copy-done.2, f32[8,16,128]{2,1,0:T(8,128)} %copy-done.3), custom_call_target="tpu_custom_call" | custom-call | tf_op jit(solution)/shard_map/pallas_call | solution.py:257
  (5 shorter events, 0.1 us)
Async XLA Ops:
  26.4 11.6 %collective-permute-start = (f32[8,16,128]{2,1,0:T(8,128)}, f32[8,16,128]{2,1,0:T(8,128)S(1)}, u32[]{:S(2)}, u32[]{:S(2)}) collective-permute-start(f32[8,16,128]{2,1,0:T(8,128)} %get-tuple-element.21), channel_id=1, source_target_pairs={{0,8},{8,16},{16,24},{24,32},{32,40},{40,48},{48,56},{56,0},{1,9},... | collective-permute-start | bytes 196616 | tf_op jit(solution)/shard_map/ppermute | solution.py:136
  29.3 8.8 %collective-permute-start.1 = (f32[8,16,128]{2,1,0:T(8,128)}, f32[8,16,128]{2,1,0:T(8,128)S(1)}, u32[]{:S(2)}, u32[]{:S(2)}) collective-permute-start(f32[8,16,128]{2,1,0:T(8,128)} %get-tuple-element.22), channel_id=1, source_target_pairs={{8,0},{16,8},{24,16},{32,24},{40,32},{48,40},{56,48},{0,56},{9,1},... | collective-permute-start | bytes 196616 | tf_op jit(solution)/shard_map/ppermute | solution.py:136
  32.8 5.3 %collective-permute-start.2 = (f32[8,16,128]{2,1,0:T(8,128)}, f32[8,16,128]{2,1,0:T(8,128)S(1)}, u32[]{:S(2)}, u32[]{:S(2)}) collective-permute-start(f32[8,16,128]{2,1,0:T(8,128)} %get-tuple-element.23), channel_id=1, source_target_pairs={{0,1},{1,2},{2,3},{3,4},{4,5},{5,6},{6,7},{8,9},{9,10},{10,11},{11... | collective-permute-start | bytes 196616 | tf_op jit(solution)/shard_map/ppermute | solution.py:136
  35.8 7.5 %collective-permute-start.3 = (f32[8,16,128]{2,1,0:T(8,128)}, f32[8,16,128]{2,1,0:T(8,128)S(1)}, u32[]{:S(2)}, u32[]{:S(2)}) collective-permute-start(f32[8,16,128]{2,1,0:T(8,128)} %get-tuple-element.24), channel_id=1, source_target_pairs={{1,0},{2,1},{3,2},{4,3},{5,4},{6,5},{7,6},{9,8},{10,9},{11,10},{12... | collective-permute-start | bytes 196616 | tf_op jit(solution)/shard_map/ppermute | solution.py:136
  38.1 5.2 %copy-start = (f32[8,16,128]{2,1,0:T(8,128)}, f32[8,16,128]{2,1,0:T(8,128)S(1)}, u32[]{:S(2)}) copy-start(f32[8,16,128]{2,1,0:T(8,128)S(1)} %collective-permute-done.low_x_ref) | copy-start | bytes 196612
  38.1 5.2 %copy-start.1 = (f32[8,16,128]{2,1,0:T(8,128)}, f32[8,16,128]{2,1,0:T(8,128)S(1)}, u32[]{:S(2)}) copy-start(f32[8,16,128]{2,1,0:T(8,128)S(1)} %collective-permute-done.1.high_x_ref) | copy-start | bytes 196612
  38.1 5.2 %copy-start.2 = (f32[8,16,128]{2,1,0:T(8,128)}, f32[8,16,128]{2,1,0:T(8,128)S(1)}, u32[]{:S(2)}) copy-start(f32[8,16,128]{2,1,0:T(8,128)S(1)} %collective-permute-done.2.low_y_ref) | copy-start | bytes 196612
  43.3 0.6 %copy-start.3 = (f32[8,16,128]{2,1,0:T(8,128)}, f32[8,16,128]{2,1,0:T(8,128)S(1)}, u32[]{:S(2)}) copy-start(f32[8,16,128]{2,1,0:T(8,128)S(1)} %collective-permute-done.3.high_y_ref) | copy-start | bytes 196612

commit v14 on v7

--- a/solution.py
+++ b/solution.py
@@ -143,6 +143,31 @@
     return jnp.concatenate([low, cells, high], axis=dim)
 
 
+def interp_kernel(picked_ref, weights_ref, out_ref):
+    slots, sources = picked_ref.shape[0], picked_ref.shape[1]
+    for slot in range(slots):
+        total = jnp.dot(
+            picked_ref[slot, 0], weights_ref[slot, 0], preferred_element_type=jnp.float32
+        )
+        for source in range(1, sources):
+            total = total + jnp.dot(
+                picked_ref[slot, source], weights_ref[slot, source],
+                preferred_element_type=jnp.float32,
+            )
+        out_ref[slot] = total
+
+
+def interpolate(picked, weights):
+    slots, sources, ncomp, cells = picked.shape
+    vmem = pl.BlockSpec(memory_space=pltpu.VMEM)
+    return pl.pallas_call(
+        interp_kernel,
+        out_shape=jax.ShapeDtypeStruct((slots, ncomp, weights.shape[-1]), jnp.float32),
+        in_specs=[vmem, vmem],
+        out_specs=vmem,
+    )(picked, weights)
+
+
 def local(field_state, shell_owner, block_sources, block_targets, interp_weights):
     grid_cells = field_state[0]
     ncomp, len_x, len_y, len_z = grid_cells.shape
@@ -189,9 +214,7 @@
     )
     slots_here = block_targets.shape[2]
     picked = picked.astype(jnp.bfloat16).reshape(slots_here, -1, ncomp, volume)
-    interp_blocks = jnp.einsum(
-        "jkcs,jkst->jct", picked, interp_weights[0, 0], preferred_element_type=jnp.float32
-    )
+    interp_blocks = interpolate(picked, interp_weights[0, 0])
 
     rows = lax.broadcasted_iota(jnp.int32, (len_x, len_y, len_z), 0) // BLK
     cols = lax.broadcasted_iota(jnp.int32, (len_x, len_y, len_z), 1) // BLK

time: 47.1 us -> 49.3 us (1.047)
  Pallas kernels: 8.43 us -> 13.7 us
  matrix products: 5.58 us -> 1.01 us
  local copies, waits for them, and re-layouts: 9.23 us -> 10.7 us
    pallas_call x0 -> x1, Pallas kernels: none -> 5.28 us  [interpolate(): pl.pallas_call(interp_kernel, out_shape=jax.ShapeDtypeStruct((slots, ncom...]
    dot_general x1 -> x0, matrix products: 4.56 us -> none  [local(): jnp.einsum('jkcs,jkst->jct', picked, interp_weights[0, 0], preferred_elem...]
    reshape x1, local copies, waits for them, and re-layouts: 0.59 us -> 1.42 us  [local(): stacked = interp_blocks.reshape(slots_here * ncomp * BLK * BLK, BLK)]
    unnamed x9, local copies, waits for them, and re-layouts: 1.67 us -> 2.32 us
where the time goes in v14:
time: 49.3 us; the launch traced here: 48.9 us
  Pallas kernels  13.7 us (28%)
  starting transfers between devices  13.2 us (27%)
  local copies, waits for them, and re-layouts  10.7 us (22%)
  other arithmetic  9.76 us (20%)
  matrix products  1.01 us (2%)
  between operations  0.51 us (1%)
    ppermute x2, starting transfers between devices, ghost_pair(): from_high = lax.ppermute(head, axis, down)  8.64 us
    pallas_call x1, Pallas kernels, route_blocks(): pl.pallas_call(route_kernel, out_shape=jax.ShapeDtypeStruct(send_cells.sh...  8.43 us
    pallas_call x1, Pallas kernels, interpolate(): pl.pallas_call(interp_kernel, out_shape=jax.ShapeDtypeStruct((slots, ncom...  5.28 us
    ppermute x2, starting transfers between devices, ghost_pair(): from_low = lax.ppermute(tail, axis, up)  4.56 us
    unnamed x9, local copies, waits for them, and re-layouts  2.32 us
    convert_element_type x3, local copies, waits for them, and re-layouts, local(): shell_cells.transpose(1, 3, 5, 0, 2, 4, 6).reshape(-1, ncomp * volume)  2.12 us
    sub x3, other arithmetic, interface_change(): 0.5 * (low_flux + high_flux)  2.01 us
    broadcast_in_dim x1, other arithmetic, local(): return updated[None]  1.54 us
  transfers between devices with their start and end apart: 4, of which 0 were waited for; matrix products, arithmetic and copies ran while one was open for 12% of the time, Pallas kernels for 0%

profile of v14, /device:TPU:9, one launch (start us, length us, event | category | flops | bytes accessed | tf_op | source)
XLA Modules:
  0.0 48.9 jit_solution(2200448965404313251)
XLA Ops:
  0.1 1.4 %slice.639 = bf16[8,16,16,16]{3,2,1,0:T(8,128)(2,1)S(1)} slice(f32[8,16,16,128]{3,2,1,0:T(8,128)} %bitcast.206), slice={[0:8], [0:16], [0:16], [112:128]} | slice | bytes 131072 | tf_op jit(solution)/shard_map/slice | solution.py:182
  1.5 0.4 convert_element_type.28
  1.9 0.2 copy.10
  2.2 1.5 %convert_element_type.30 = bf16[8,4096]{1,0:T(8,128)(2,1)S(1)} reshape(bf16[2,2,2,8,8,8,8]{6,5,4,3,2,1,0:T(8,128)(2,1)S(1)} %bitcast.205) | data formatting | bytes 131072 | tf_op jit(solution)/shard_map/convert_element_type | solution.py:185
  3.7 0.1 convert_reduce_fusion.1
  3.8 0.2 convert_reduce_fusion
  4.0 0.2 convolution_convert_fusion.1
  4.1 0.7 %reshape.303.send_ref = bf16[8,16,512]{2,1,0:T(8,128)(2,1)} reshape(bf16[16,4096]{1,0:T(8,128)(2,1)S(1)} %convolution_convert_fusion.1) | data formatting | bytes 262144 | tf_op jit(solution)/shard_map/reshape | solution.py:201
  4.9 8.4 %shard_map.55 = bf16[8,16,512]{2,1,0:T(8,128)(2,1)} custom-call(bf16[8,16,512]{2,1,0:T(8,128)(2,1)} %reshape.303.send_ref), custom_call_target="tpu_custom_call" | custom-call | tf_op jit(solution)/shard_map/pallas_call | solution.py:115
  13.3 1.0 %reshape.304 = bf16[16,4096]{1,0:T(8,128)(2,1)S(1)} reshape(bf16[8,16,512]{2,1,0:T(8,128)(2,1)} %shard_map.55) | data formatting | bytes 262144 | tf_op jit(solution)/shard_map/reshape | solution.py:202
  14.3 0.2 reduce-window.8
  14.7 0.2 convolution_convert_fusion
  15.0 0.7 %copy.8 = bf16[2,8,8,512]{3,2,1,0:T(8,128)(2,1)} copy(bf16[2,8,8,512]{3,1,2,0:T(8,128)(2,1)S(1)} %bitcast.212) | data formatting | bytes 262144
  15.7 5.3 %shard_map.56 = f32[4,8,512]{2,1,0:T(8,128)} custom-call(bf16[4,4,8,512]{3,2,1,0:T(8,128)(2,1)} %bitcast.211, bf16[4,4,512,512]{3,2,1,0:T(8,128)(2,1)} %bitcast.200), custom_call_target="tpu_custom_call" | custom-call | tf_op jit(solution)/shard_map/pallas_call | solution.py:163
  20.9 1.4 %reshape.306 = f32[2048,8]{1,0:T(8,128)S(1)} reshape(f32[4,8,512]{2,1,0:T(8,128)} %shard_map.56) | data formatting | bytes 131072 | tf_op jit(solution)/shard_map/reshape | solution.py:225
  22.4 0.6 %fusion.78 = f32[2048,128]{1,0:T(8,128)S(1)} fusion(f32[2048,8]{1,0:T(8,128)S(1)} %reshape.306, s32[128]{0:T(128)S(1)} %get-tuple-element.48, s32[128]{0:T(128)S(1)} %get-tuple-element.49, pred[128]{0:T(512)(128)(4,1)S(1)} %compare_and_fusion), kind=kOutput, calls=%fused_computation.171 | convolution fusion | flops 25167872 | bytes 1115264 | tf_op jit(solution)/shard_map/dot_general | solution.py:226
  23.1 0.6 %copy-done.3 = s32[1,1,4]{2,1,0:T(1,128)S(1)} copy-done((s32[1,1,4]{2,1,0:T(1,128)S(1)}, s32[1,1,4]{2,1,0:T(1,128)}, u32[]{:S(2)}) %copy-start.3) | copy-done | bytes 40
  23.7 0.1 broadcast_select_fusion.3
  23.8 0.2 and_and_fusion
  24.4 1.0 %copy-done = f32[1,8,16,16,128]{4,3,2,1,0:T(8,128)S(1)} copy-done((f32[1,8,16,16,128]{4,3,2,1,0:T(8,128)S(1)}, f32[1,8,16,16,128]{4,3,2,1,0:T(8,128)}, u32[]{:S(2)}) %copy-start) | copy-done | bytes 1048600
  25.4 0.4 select_select_fusion
  25.8 0.7 %fusion.86 = (f32[8,16,1,128]{3,2,1,0:T(1,128)}, f32[8,16,1,128]{3,2,1,0:T(1,128)S(1)}) fusion(f32[8,16,16,128]{3,2,1,0:T(8,128)S(1)} %select_select_fusion), kind=kLoop, calls=%fused_computation.200 | loop fusion | bytes 262144 | tf_op jit(solution)/shard_map/slice | solution.py:133
  26.5 2.5 %collective-permute-start.2 = (f32[8,16,1,128]{3,2,1,0:T(1,128)}, f32[8,16,1,128]{3,2,1,0:T(1,128)S(1)}, u32[]{:S(2)}, u32[]{:S(2)}) collective-permute-start(f32[8,16,1,128]{3,2,1,0:T(1,128)} %get-tuple-element.31), channel_id=1, source_target_pairs={{0,1},{1,2},{2,3},{3,4},{4,5},{5,6},{6,7},{8,9},{9,10},{10,11},{11... | collective-permute-start | bytes 196616 | tf_op jit(solution)/shard_map/ppermute | solution.py:139
  29.0 4.9 %collective-permute-start.3 = (f32[8,16,1,128]{3,2,1,0:T(1,128)S(1)}, f32[8,16,1,128]{3,2,1,0:T(1,128)}, u32[]{:S(2)}, u32[]{:S(2)}) collective-permute-start(f32[8,16,1,128]{3,2,1,0:T(1,128)S(1)} %get-tuple-element.32), channel_id=1, source_target_pairs={{1,0},{2,1},{3,2},{4,3},{5,4},{6,5},{7,6},{9,8},{10,9},{11,10},{12... | collective-permute-start | bytes 196616 | tf_op jit(solution)/shard_map/ppermute | solution.py:140
  33.9 2.1 %collective-permute-start = (f32[8,1,16,128]{3,2,1,0:T(8,128)S(1)}, f32[8,1,16,128]{3,2,1,0:T(8,128)S(1)}, u32[]{:S(2)}, u32[]{:S(2)}) collective-permute-start(f32[8,1,16,128]{3,2,1,0:T(8,128)S(1)} %get-tuple-element.27), channel_id=1, source_target_pairs={{0,8},{8,16},{16,24},{24,32},{32,40},{40,48},{48,56},{56,0},{1,9},... | collective-permute-start | bytes 196616 | tf_op jit(solution)/shard_map/ppermute | solution.py:139
  36.0 3.7 %collective-permute-start.1 = (f32[8,1,16,128]{3,2,1,0:T(8,128)S(1)}, f32[8,1,16,128]{3,2,1,0:T(8,128)S(1)}, u32[]{:S(2)}, u32[]{:S(2)}) collective-permute-start(f32[8,1,16,128]{3,2,1,0:T(8,128)S(1)} %get-tuple-element.28), channel_id=1, source_target_pairs={{8,0},{16,8},{24,16},{32,24},{40,32},{48,40},{56,48},{0,56},{9,1},... | collective-permute-start | bytes 196616 | tf_op jit(solution)/shard_map/ppermute | solution.py:140
  39.8 0.3 fusion.87
  40.1 0.9 %pad_maximum_fusion = f32[8,16,16,130]{3,2,1,0:T(8,128)S(1)} fusion(f32[8,16,16,1]{3,2,1,0:T(8,128)S(1)} %get-tuple-element.34, f32[8,16,16,128]{3,2,1,0:T(8,128)S(1)} %select_select_fusion, f32[8,16,16,1]{3,2,1,0:T(8,128)S(1)} %get-tuple-element.33), kind=kLoop, calls=%fused_computation.5 | loop fusion | flops 532480 | bytes 2129920 | tf_op jit(solution)/shard_map/jit(_pad)/concatenate | solution.py:247
  41.1 0.3 multiply_reduce_fusion
  41.3 0.1 fusion.22
  41.5 0.2 fusion.28
  41.7 0.2 add_dynamic-update-slice_fusion
  41.9 0.1 fusion.18
  42.0 0.1 fusion.16
  42.1 0.1 fusion.14
  42.3 0.2 fusion.30
  42.4 1.2 %fusion.1 = f32[8,16,16,129]{3,2,1,0:T(8,128)S(1)} fusion(f32[8,16,16,130]{3,2,1,0:T(8,128)S(1)} %fusion.30, f32[8,16,16,1]{3,2,1,0:T(8,128)S(1)} %get-tuple-element.34, f32[8,16,16,128]{3,2,1,0:T(8,128)S(1)} %select_select_fusion, f32[8,16,16,1]{3,2,1,0:T(8,128)S(1)} %get-tuple-element.33, f32[16,16,129]{2,1,0:T(8,128)S(1)} %fusion.14), kind=kLoop, calls=%fused_computation.4 | loop fusion | flops 1849344 | bytes 4367360 | tf_op jit(solution)/shard_map/sub | solution.py:58
  43.7 1.0 %broadcast_select_fusion.1 = (f32[8,16,1,128]{3,2,1,0:T(1,128)S(1)}, f32[8,16,1,128]{3,2,1,0:T(1,128)S(1)}) fusion(f32[8,16,1,128]{3,2,1,0:T(1,128)S(1)} %collective-permute-done.2, pred[]{:T(512)S(6)} %eq.140, f32[8,16,16,128]{3,2,1,0:T(8,128)S(1)} %select_select_fusion, f32[8,16,1,128]{3,2,1,0:T(1,128)} %collective-permute-done.3, pred[]{:T(512)S(6)} %eq.141), kind=kLoop, calls=%fused_computation.152 | loop fusion | flops 32768 | bytes 393218 | tf_op jit(solution)/shard_map/jit(_where)/select_n | solution.py:141
  44.7 0.3 pad_maximum_fusion.1
  45.0 0.2 multiply_reduce_fusion.3
  45.2 0.1 fusion.46
  45.4 0.1 add_dynamic-update-slice_fusion.1
  45.9 0.1 multiply_reduce_fusion.6
  46.0 0.1 fusion.63
  46.4 0.1 fusion.48
  46.5 0.6 %fusion.4 = f32[8,16,17,128]{3,2,1,0:T(8,128)S(1)} fusion(f32[8,16,18,128]{3,2,1,0:T(8,128)S(1)} %fusion.48, f32[8,16,1,128]{3,2,1,0:T(1,128)S(1)} %get-tuple-element.30, f32[8,16,16,128]{3,2,1,0:T(8,128)S(1)} %select_select_fusion, f32[8,16,1,128]{3,2,1,0:T(1,128)S(1)} %get-tuple-element.29, f32[16,17,128]{2,1,0:T(8,128)S(1)} %fusion.32), kind=kLoop, calls=%fused_computation.10 | loop fusion | flops 1949696 | bytes 4661248 | tf_op jit(solution)/shard_map/sub | solution.py:58
  47.2 0.2 fusion.7
  47.4 1.5 %fusion.12 = f32[1,8,16,16,128]{4,3,2,1,0:T(8,128)} fusion(f32[8,16,16,128]{3,2,1,0:T(8,128)S(1)} %select_select_fusion, f32[8,16,16,129]{3,2,1,0:T(8,128)S(1)} %fusion.1, f32[8,16,17,128]{3,2,1,0:T(8,128)S(1)} %fusion.4, f32[8,17,16,128]{3,2,1,0:T(8,128)S(1)} %fusion.7, f32[]{:T(128)S(6)} %select_n.166), kind=kLoop, calls=%fused_computation.24 | loop fusion | flops 1835008 | bytes 8388612 | tf_op jit(solution)/shard_map/broadcast_in_dim | solution.py:250
  (52 shorter events, 1.7 us)
Async XLA Ops:
  1.9 1.8 %copy-start.1 = (s32[1,8,8]{2,1,0:T(8,128)S(1)}, s32[1,8,8]{2,1,0:T(8,128)}, u32[]{:S(2)}) copy-start(s32[1,8,8]{2,1,0:T(8,128)} %param.6) | copy-start | bytes 772
  2.2 12.5 %copy-start.2 = (s32[1,1,4,4]{3,2,1,0:T(4,128)S(1)}, s32[1,1,4,4]{3,2,1,0:T(4,128)}, u32[]{:S(2)}) copy-start(s32[1,1,4,4]{3,2,1,0:T(4,128)} %param.7) | copy-start | bytes 196
  23.0 0.7 %copy-start.3 = (s32[1,1,4]{2,1,0:T(1,128)S(1)}, s32[1,1,4]{2,1,0:T(1,128)}, u32[]{:S(2)}) copy-start(s32[1,1,4]{2,1,0:T(1,128)} %param.8) | copy-start | bytes 52
  24.2 1.2 %copy-start = (f32[1,8,16,16,128]{4,3,2,1,0:T(8,128)S(1)}, f32[1,8,16,16,128]{4,3,2,1,0:T(8,128)}, u32[]{:S(2)}) copy-start(f32[1,8,16,16,128]{4,3,2,1,0:T(8,128)} %param.5) | copy-start | bytes 3145732
  26.5 17.2 %collective-permute-start.2 = (f32[8,16,1,128]{3,2,1,0:T(1,128)}, f32[8,16,1,128]{3,2,1,0:T(1,128)S(1)}, u32[]{:S(2)}, u32[]{:S(2)}) collective-permute-start(f32[8,16,1,128]{3,2,1,0:T(1,128)} %get-tuple-element.31), channel_id=1, source_target_pairs={{0,1},{1,2},{2,3},{3,4},{4,5},{5,6},{6,7},{8,9},{9,10},{10,11},{11... | collective-permute-start | bytes 196616 | tf_op jit(solution)/shard_map/ppermute | solution.py:139
  29.0 14.7 %collective-permute-start.3 = (f32[8,16,1,128]{3,2,1,0:T(1,128)S(1)}, f32[8,16,1,128]{3,2,1,0:T(1,128)}, u32[]{:S(2)}, u32[]{:S(2)}) collective-permute-start(f32[8,16,1,128]{3,2,1,0:T(1,128)S(1)} %get-tuple-element.32), channel_id=1, source_target_pairs={{1,0},{2,1},{3,2},{4,3},{5,4},{6,5},{7,6},{9,8},{10,9},{11,10},{12... | collective-permute-start | bytes 196616 | tf_op jit(solution)/shard_map/ppermute | solution.py:140
  33.9 11.8 %collective-permute-start = (f32[8,1,16,128]{3,2,1,0:T(8,128)S(1)}, f32[8,1,16,128]{3,2,1,0:T(8,128)S(1)}, u32[]{:S(2)}, u32[]{:S(2)}) collective-permute-start(f32[8,1,16,128]{3,2,1,0:T(8,128)S(1)} %get-tuple-element.27), channel_id=1, source_target_pairs={{0,8},{8,16},{16,24},{24,32},{32,40},{40,48},{48,56},{56,0},{1,9},... | collective-permute-start | bytes 196616 | tf_op jit(solution)/shard_map/ppermute | solution.py:139
  36.0 9.7 %collective-permute-start.1 = (f32[8,1,16,128]{3,2,1,0:T(8,128)S(1)}, f32[8,1,16,128]{3,2,1,0:T(8,128)S(1)}, u32[]{:S(2)}, u32[]{:S(2)}) collective-permute-start(f32[8,1,16,128]{3,2,1,0:T(8,128)S(1)} %get-tuple-element.28), channel_id=1, source_target_pairs={{8,0},{16,8},{24,16},{32,24},{40,32},{48,40},{56,48},{0,56},{9,1},... | collective-permute-start | bytes 196616 | tf_op jit(solution)/shard_map/ppermute | solution.py:140

commit v15 on v7

--- a/solution.py
+++ b/solution.py
@@ -174,7 +174,7 @@
         select.astype(jnp.bfloat16), shell_cells, preferred_element_type=jnp.float32
     )
     send_cells = send_cells.astype(jnp.bfloat16).reshape(yz_count, CAP * ncomp, volume)
-    got_cells = route_blocks(send_cells).reshape(slot_count, ncomp * volume)
+    got_cells = route_blocks(send_cells).reshape(slot_count, ncomp, volume)
     mine = (owner_table == yz_index).astype(jnp.int32)
     per_sender = jnp.sum(mine, axis=1)
     before = jnp.cumsum(per_sender) - per_sender
@@ -184,8 +184,9 @@
     ).reshape(slot_count)
     wanted = block_sources[0, 0].reshape(-1)
     match_table = (wanted[:, None] == got_tags[None, :]) & (wanted[:, None] >= 0)
-    picked = jnp.dot(
-        match_table.astype(jnp.bfloat16), got_cells, preferred_element_type=jnp.float32
+    picked = jnp.einsum(
+        "ws,scv->wcv", match_table.astype(jnp.bfloat16), got_cells,
+        preferred_element_type=jnp.float32,
     )
     slots_here = block_targets.shape[2]
     picked = picked.astype(jnp.bfloat16).reshape(slots_here, -1, ncomp, volume)

time: 47.1 us -> 47.1 us (level)
  local copies, waits for them, and re-layouts: 9.23 us -> 8.31 us
  matrix products: 5.58 us -> 6.48 us
    dot_general x1, matrix products: 0.23 us -> 1.13 us  [local(): jnp.einsum('ws,scv->wcv', match_table.astype(jnp.bfloat16), got_cells, pr...]
    reshape x1, local copies, waits for them, and re-layouts: 0.97 us -> 0.08 us  [local(): picked = picked.astype(jnp.bfloat16).reshape(slots_here, -1, ncomp, volume)]
    unnamed x9 -> x8, local copies, waits for them, and re-layouts: 1.67 us -> 1.63 us
where the time goes in v15:
time: 47.1 us; the launch traced here: 46.7 us
  starting transfers between devices  13.2 us (28%)
  other arithmetic  9.79 us (21%)
  Pallas kernels  8.43 us (18%)
  local copies, waits for them, and re-layouts  8.31 us (18%)
  matrix products  6.48 us (14%)
  between operations  0.5 us (1%)
    ppermute x2, starting transfers between devices, ghost_pair(): from_high = lax.ppermute(head, axis, down)  8.64 us
    pallas_call x1, Pallas kernels, route_blocks(): pl.pallas_call(route_kernel, out_shape=jax.ShapeDtypeStruct(send_cells.sh...  8.43 us
    dot_general x1, matrix products, local(): jnp.einsum('jkcs,jkst->jct', picked, interp_weights[0, 0], preferred_elem...  4.56 us
    ppermute x2, starting transfers between devices, ghost_pair(): from_low = lax.ppermute(tail, axis, up)  4.56 us
    convert_element_type x3, local copies, waits for them, and re-layouts, local(): shell_cells.transpose(1, 3, 5, 0, 2, 4, 6).reshape(-1, ncomp * volume)  2.13 us
    sub x3, other arithmetic, interface_change(): 0.5 * (low_flux + high_flux)  2.02 us
    unnamed x8, local copies, waits for them, and re-layouts  1.63 us
    broadcast_in_dim x1, other arithmetic, local(): return updated[None]  1.54 us
  transfers between devices with their start and end apart: 4, of which 0 were waited for; matrix products, arithmetic and copies ran while one was open for 12% of the time, Pallas kernels for 0%

profile of v15, /device:TPU:9, one launch (start us, length us, event | category | flops | bytes accessed | tf_op | source)
XLA Modules:
  0.0 46.7 jit_solution(4096331785329450636)
XLA Ops:
  0.1 1.4 %slice.639 = bf16[8,16,16,16]{3,2,1,0:T(8,128)(2,1)S(1)} slice(f32[8,16,16,128]{3,2,1,0:T(8,128)} %bitcast.214), slice={[0:8], [0:16], [0:16], [112:128]} | slice | bytes 131072 | tf_op jit(solution)/shard_map/slice | solution.py:157
  1.5 0.4 convert_element_type.28
  1.9 0.2 copy.19
  2.2 1.5 %convert_element_type.30 = bf16[8,4096]{1,0:T(8,128)(2,1)S(1)} reshape(bf16[2,2,2,8,8,8,8]{6,5,4,3,2,1,0:T(8,128)(2,1)S(1)} %bitcast.213) | data formatting | bytes 131072 | tf_op jit(solution)/shard_map/convert_element_type | solution.py:160
  3.7 0.1 convert_reduce_fusion.1
  3.8 0.2 convert_reduce_fusion
  4.0 0.2 convolution_convert_fusion
  4.2 0.7 %reshape.303.send_ref = bf16[8,16,512]{2,1,0:T(8,128)(2,1)} reshape(bf16[16,4096]{1,0:T(8,128)(2,1)S(1)} %convolution_convert_fusion) | data formatting | bytes 262144 | tf_op jit(solution)/shard_map/reshape | solution.py:176
  4.9 8.4 %shard_map.55 = bf16[8,16,512]{2,1,0:T(8,128)(2,1)} custom-call(bf16[8,16,512]{2,1,0:T(8,128)(2,1)} %reshape.303.send_ref), custom_call_target="tpu_custom_call" | custom-call | tf_op jit(solution)/shard_map/pallas_call | solution.py:115
  13.3 0.2 reduce-window.8
  13.7 0.1 eq.124
  13.8 1.1 %convolution_convert_fusion.1 = bf16[16,8,512]{2,0,1:T(8,128)(2,1)S(1)} fusion(bf16[16,8,512]{2,1,0:T(8,128)(2,1)} %bitcast.220, s32[16]{0:T(128)S(1)} %select_n.159, s32[16]{0:T(128)S(1)} %eq.124, pred[16]{0:T(512)(128)(4,1)S(1)} %broadcast_compare_fusion), kind=kOutput, calls=%fused_computation.16 | convolution fusion | flops 2163200 | bytes 262288 | tf_op jit(solution)/shard_map/ws,scv->wcv/dot_general | solution.py:187
  15.0 4.6 %fusion.8 = f32[4,8,512]{2,1,0:T(8,128)S(1)} fusion(bf16[4,4,8,512]{3,2,1,0:T(8,128)(2,1)S(1)} %bitcast.219, bf16[1,1,4,4,512,512]{5,4,3,2,1,0:T(8,128)(2,1)} %param.9), kind=kOutput, calls=%fused_computation.17 | convolution fusion | flops 67108864 | bytes 8585216 | tf_op jit(solution)/shard_map/jkcs,jkst->jct/dot_general | solution.py:193
  19.5 0.6 %reshape.306 = f32[2048,8]{1,0:T(8,128)S(1)} reshape(f32[4,8,512]{2,1,0:T(8,128)S(1)} %fusion.8) | data formatting | bytes 131072 | tf_op jit(solution)/shard_map/reshape | solution.py:203
  20.1 0.6 %fusion.85 = f32[2048,128]{1,0:T(8,128)S(1)} fusion(f32[2048,8]{1,0:T(8,128)S(1)} %reshape.306, s32[128]{0:T(128)S(1)} %get-tuple-element.48, s32[128]{0:T(128)S(1)} %get-tuple-element.49, pred[128]{0:T(512)(128)(4,1)S(1)} %compare_and_fusion), kind=kOutput, calls=%fused_computation.176 | convolution fusion | flops 25167872 | bytes 1115264 | tf_op jit(solution)/shard_map/dot_general | solution.py:204
  20.9 0.6 %copy-done.3 = s32[1,1,4]{2,1,0:T(1,128)S(1)} copy-done((s32[1,1,4]{2,1,0:T(1,128)S(1)}, s32[1,1,4]{2,1,0:T(1,128)}, u32[]{:S(2)}) %copy-start.3) | copy-done | bytes 40
  21.5 0.1 broadcast_select_fusion.3
  21.6 0.2 and_and_fusion
  22.2 1.0 %copy-done = f32[1,8,16,16,128]{4,3,2,1,0:T(8,128)S(1)} copy-done((f32[1,8,16,16,128]{4,3,2,1,0:T(8,128)S(1)}, f32[1,8,16,16,128]{4,3,2,1,0:T(8,128)}, u32[]{:S(2)}) %copy-start) | copy-done | bytes 1048600
  23.2 0.4 select_select_fusion
  23.6 0.7 %fusion.93 = (f32[8,16,1,128]{3,2,1,0:T(1,128)}, f32[8,16,1,128]{3,2,1,0:T(1,128)S(1)}) fusion(f32[8,16,16,128]{3,2,1,0:T(8,128)S(1)} %select_select_fusion), kind=kLoop, calls=%fused_computation.205 | loop fusion | bytes 262144 | tf_op jit(solution)/shard_map/slice | solution.py:133
  24.3 2.5 %collective-permute-start.2 = (f32[8,16,1,128]{3,2,1,0:T(1,128)}, f32[8,16,1,128]{3,2,1,0:T(1,128)S(1)}, u32[]{:S(2)}, u32[]{:S(2)}) collective-permute-start(f32[8,16,1,128]{3,2,1,0:T(1,128)} %get-tuple-element.31), channel_id=1, source_target_pairs={{0,1},{1,2},{2,3},{3,4},{4,5},{5,6},{6,7},{8,9},{9,10},{10,11},{11... | collective-permute-start | bytes 196616 | tf_op jit(solution)/shard_map/ppermute | solution.py:139
  26.8 4.9 %collective-permute-start.3 = (f32[8,16,1,128]{3,2,1,0:T(1,128)S(1)}, f32[8,16,1,128]{3,2,1,0:T(1,128)}, u32[]{:S(2)}, u32[]{:S(2)}) collective-permute-start(f32[8,16,1,128]{3,2,1,0:T(1,128)S(1)} %get-tuple-element.32), channel_id=1, source_target_pairs={{1,0},{2,1},{3,2},{4,3},{5,4},{6,5},{7,6},{9,8},{10,9},{11,10},{12... | collective-permute-start | bytes 196616 | tf_op jit(solution)/shard_map/ppermute | solution.py:140
  31.7 2.1 %collective-permute-start = (f32[8,1,16,128]{3,2,1,0:T(8,128)S(1)}, f32[8,1,16,128]{3,2,1,0:T(8,128)S(1)}, u32[]{:S(2)}, u32[]{:S(2)}) collective-permute-start(f32[8,1,16,128]{3,2,1,0:T(8,128)S(1)} %get-tuple-element.27), channel_id=1, source_target_pairs={{0,8},{8,16},{16,24},{24,32},{32,40},{40,48},{48,56},{56,0},{1,9},... | collective-permute-start | bytes 196616 | tf_op jit(solution)/shard_map/ppermute | solution.py:139
  33.8 3.7 %collective-permute-start.1 = (f32[8,1,16,128]{3,2,1,0:T(8,128)S(1)}, f32[8,1,16,128]{3,2,1,0:T(8,128)S(1)}, u32[]{:S(2)}, u32[]{:S(2)}) collective-permute-start(f32[8,1,16,128]{3,2,1,0:T(8,128)S(1)} %get-tuple-element.28), channel_id=1, source_target_pairs={{8,0},{16,8},{24,16},{32,24},{40,32},{48,40},{56,48},{0,56},{9,1},... | collective-permute-start | bytes 196616 | tf_op jit(solution)/shard_map/ppermute | solution.py:140
  37.6 0.3 fusion.94
  37.9 0.9 %pad_maximum_fusion = f32[8,16,16,130]{3,2,1,0:T(8,128)S(1)} fusion(f32[8,16,16,1]{3,2,1,0:T(8,128)S(1)} %get-tuple-element.34, f32[8,16,16,128]{3,2,1,0:T(8,128)S(1)} %select_select_fusion, f32[8,16,16,1]{3,2,1,0:T(8,128)S(1)} %get-tuple-element.33), kind=kLoop, calls=%fused_computation.6 | loop fusion | flops 532480 | bytes 2129920 | tf_op jit(solution)/shard_map/jit(_pad)/concatenate | solution.py:225
  38.9 0.3 multiply_reduce_fusion
  39.1 0.1 fusion.27
  39.2 0.1 fusion.25
  39.3 0.2 fusion.33
  39.5 0.2 add_dynamic-update-slice_fusion
  39.7 0.1 fusion.23
  39.8 0.1 fusion.21
  39.9 0.1 fusion.19
  40.1 0.2 fusion.35
  40.2 1.2 %fusion.3 = f32[8,16,16,129]{3,2,1,0:T(8,128)S(1)} fusion(f32[8,16,16,130]{3,2,1,0:T(8,128)S(1)} %fusion.35, f32[8,16,16,1]{3,2,1,0:T(8,128)S(1)} %get-tuple-element.34, f32[8,16,16,128]{3,2,1,0:T(8,128)S(1)} %select_select_fusion, f32[8,16,16,1]{3,2,1,0:T(8,128)S(1)} %get-tuple-element.33, f32[16,16,129]{2,1,0:T(8,128)S(1)} %fusion.19), kind=kLoop, calls=%fused_computation.5 | loop fusion | flops 1849344 | bytes 4367360 | tf_op jit(solution)/shard_map/sub | solution.py:58
  41.5 1.0 %broadcast_select_fusion.1 = (f32[8,16,1,128]{3,2,1,0:T(1,128)S(1)}, f32[8,16,1,128]{3,2,1,0:T(1,128)S(1)}) fusion(f32[8,16,1,128]{3,2,1,0:T(1,128)S(1)} %collective-permute-done.2, pred[]{:T(512)S(6)} %eq.140, f32[8,16,16,128]{3,2,1,0:T(8,128)S(1)} %select_select_fusion, f32[8,16,1,128]{3,2,1,0:T(1,128)} %collective-permute-done.3, pred[]{:T(512)S(6)} %eq.141), kind=kLoop, calls=%fused_computation.156 | loop fusion | flops 32768 | bytes 393218 | tf_op jit(solution)/shard_map/jit(_where)/select_n | solution.py:141
  42.5 0.3 pad_maximum_fusion.1
  42.8 0.2 multiply_reduce_fusion.3
  43.0 0.1 fusion.51
  43.2 0.1 add_dynamic-update-slice_fusion.1
  43.7 0.1 multiply_reduce_fusion.6
  43.8 0.1 fusion.68
  44.2 0.1 fusion.53
  44.3 0.6 %fusion.6 = f32[8,16,17,128]{3,2,1,0:T(8,128)S(1)} fusion(f32[8,16,18,128]{3,2,1,0:T(8,128)S(1)} %fusion.53, f32[8,16,1,128]{3,2,1,0:T(1,128)S(1)} %get-tuple-element.30, f32[8,16,16,128]{3,2,1,0:T(8,128)S(1)} %select_select_fusion, f32[8,16,1,128]{3,2,1,0:T(1,128)S(1)} %get-tuple-element.29, f32[16,17,128]{2,1,0:T(8,128)S(1)} %fusion.37), kind=kLoop, calls=%fused_computation.11 | loop fusion | flops 1949696 | bytes 4661248 | tf_op jit(solution)/shard_map/sub | solution.py:58
  45.0 0.2 fusion.12
  45.2 1.5 %fusion.17 = f32[1,8,16,16,128]{4,3,2,1,0:T(8,128)} fusion(f32[8,16,16,128]{3,2,1,0:T(8,128)S(1)} %select_select_fusion, f32[8,16,16,129]{3,2,1,0:T(8,128)S(1)} %fusion.3, f32[8,16,17,128]{3,2,1,0:T(8,128)S(1)} %fusion.6, f32[8,17,16,128]{3,2,1,0:T(8,128)S(1)} %fusion.12, f32[]{:T(128)S(6)} %select_n.166), kind=kLoop, calls=%fused_computation.27 | loop fusion | flops 1835008 | bytes 8388612 | tf_op jit(solution)/shard_map/broadcast_in_dim | solution.py:228
  (51 shorter events, 1.6 us)
Async XLA Ops:
  1.9 1.8 %copy-start.1 = (s32[1,8,8]{2,1,0:T(8,128)S(1)}, s32[1,8,8]{2,1,0:T(8,128)}, u32[]{:S(2)}) copy-start(s32[1,8,8]{2,1,0:T(8,128)} %param.6) | copy-start | bytes 772
  1.9 11.7 %copy-start.2 = (s32[1,1,4,4]{3,2,1,0:T(4,128)S(1)}, s32[1,1,4,4]{3,2,1,0:T(4,128)}, u32[]{:S(2)}) copy-start(s32[1,1,4,4]{3,2,1,0:T(4,128)} %param.7) | copy-start | bytes 196
  20.8 0.7 %copy-start.3 = (s32[1,1,4]{2,1,0:T(1,128)S(1)}, s32[1,1,4]{2,1,0:T(1,128)}, u32[]{:S(2)}) copy-start(s32[1,1,4]{2,1,0:T(1,128)} %param.8) | copy-start | bytes 52
  22.0 1.2 %copy-start = (f32[1,8,16,16,128]{4,3,2,1,0:T(8,128)S(1)}, f32[1,8,16,16,128]{4,3,2,1,0:T(8,128)}, u32[]{:S(2)}) copy-start(f32[1,8,16,16,128]{4,3,2,1,0:T(8,128)} %param.5) | copy-start | bytes 3145732
  24.3 17.2 %collective-permute-start.2 = (f32[8,16,1,128]{3,2,1,0:T(1,128)}, f32[8,16,1,128]{3,2,1,0:T(1,128)S(1)}, u32[]{:S(2)}, u32[]{:S(2)}) collective-permute-start(f32[8,16,1,128]{3,2,1,0:T(1,128)} %get-tuple-element.31), channel_id=1, source_target_pairs={{0,1},{1,2},{2,3},{3,4},{4,5},{5,6},{6,7},{8,9},{9,10},{10,11},{11... | collective-permute-start | bytes 196616 | tf_op jit(solution)/shard_map/ppermute | solution.py:139
  26.8 14.7 %collective-permute-start.3 = (f32[8,16,1,128]{3,2,1,0:T(1,128)S(1)}, f32[8,16,1,128]{3,2,1,0:T(1,128)}, u32[]{:S(2)}, u32[]{:S(2)}) collective-permute-start(f32[8,16,1,128]{3,2,1,0:T(1,128)S(1)} %get-tuple-element.32), channel_id=1, source_target_pairs={{1,0},{2,1},{3,2},{4,3},{5,4},{6,5},{7,6},{9,8},{10,9},{11,10},{12... | collective-permute-start | bytes 196616 | tf_op jit(solution)/shard_map/ppermute | solution.py:140
  31.7 11.8 %collective-permute-start = (f32[8,1,16,128]{3,2,1,0:T(8,128)S(1)}, f32[8,1,16,128]{3,2,1,0:T(8,128)S(1)}, u32[]{:S(2)}, u32[]{:S(2)}) collective-permute-start(f32[8,1,16,128]{3,2,1,0:T(8,128)S(1)} %get-tuple-element.27), channel_id=1, source_target_pairs={{0,8},{8,16},{16,24},{24,32},{32,40},{40,48},{48,56},{56,0},{1,9},... | collective-permute-start | bytes 196616 | tf_op jit(solution)/shard_map/ppermute | solution.py:139
  33.8 9.7 %collective-permute-start.1 = (f32[8,1,16,128]{3,2,1,0:T(8,128)S(1)}, f32[8,1,16,128]{3,2,1,0:T(8,128)S(1)}, u32[]{:S(2)}, u32[]{:S(2)}) collective-permute-start(f32[8,1,16,128]{3,2,1,0:T(8,128)S(1)} %get-tuple-element.28), channel_id=1, source_target_pairs={{8,0},{16,8},{24,16},{32,24},{40,32},{48,40},{56,48},{0,56},{9,1},... | collective-permute-start | bytes 196616 | tf_op jit(solution)/shard_map/ppermute | solution.py:140

commit v16 on v7

--- a/solution.py
+++ b/solution.py
@@ -136,8 +136,8 @@
     if wrap:
         up.append((count - 1, 0))
         down.append((0, count - 1))
-    from_low = lax.ppermute(tail, axis, up)
-    from_high = lax.ppermute(head, axis, down)
+    from_low = lax.ppermute(tail.astype(jnp.bfloat16), axis, up).astype(cells.dtype)
+    from_high = lax.ppermute(head.astype(jnp.bfloat16), axis, down).astype(cells.dtype)
     low = jnp.where(fix_low, head, from_low)
     high = jnp.where(fix_high, tail, from_high)
     return jnp.concatenate([low, cells, high], axis=dim)

time: 47.1 us -> 45.6 us (0.968)
  other arithmetic: 9.78 us -> 8.95 us
  local copies, waits for them, and re-layouts: 9.23 us -> 8.6 us
    select_n x2, other arithmetic: 1.01 us -> 0.18 us  [ghost_pair(): low = jnp.where(fix_low, head, from_low)]
    slice x2, local copies, waits for them, and re-layouts: 0.73 us -> 0.11 us  [ghost_pair(): tail = lax.slice_in_dim(cells, size - 1, size, axis=dim)]
  transfers between devices with their start and end apart: 4 -> 4, of which waited for: 0 -> 0; matrix products, arithmetic and copies ran while one was open for 12% -> 11% of each run, Pallas kernels for 0% -> 0%
where the time goes in v16:
time: 45.6 us; the launch traced here: 45.3 us
  starting transfers between devices  13.2 us (29%)
  other arithmetic  8.95 us (20%)
  local copies, waits for them, and re-layouts  8.6 us (19%)
  Pallas kernels  8.43 us (18%)
  matrix products  5.58 us (12%)
  between operations  0.53 us (1%)
    ppermute x2, starting transfers between devices, ghost_pair(): lax.ppermute(head.astype(jnp.bfloat16), axis, down).astype(cells.dtype)  8.64 us
    pallas_call x1, Pallas kernels, route_blocks(): pl.pallas_call(route_kernel, out_shape=jax.ShapeDtypeStruct(send_cells.sh...  8.43 us
    ppermute x2, starting transfers between devices, ghost_pair(): lax.ppermute(tail.astype(jnp.bfloat16), axis, up).astype(cells.dtype)  4.57 us
    dot_general x1, matrix products, local(): jnp.einsum('jkcs,jkst->jct', picked, interp_weights[0, 0], preferred_elem...  4.56 us
    convert_element_type x3, local copies, waits for them, and re-layouts, local(): shell_cells.transpose(1, 3, 5, 0, 2, 4, 6).reshape(-1, ncomp * volume)  2.12 us
    sub x3, other arithmetic, interface_change(): 0.5 * (low_flux + high_flux)  2.01 us
    unnamed x9, local copies, waits for them, and re-layouts  1.67 us
    broadcast_in_dim x1, other arithmetic, local(): return updated[None]  1.54 us
  transfers between devices with their start and end apart: 4, of which 0 were waited for; matrix products, arithmetic and copies ran while one was open for 11% of the time, Pallas kernels for 0%

profile of v16, /device:TPU:9, one launch (start us, length us, event | category | flops | bytes accessed | tf_op | source)
XLA Modules:
  0.0 45.3 jit_solution(13522375883876226363)
XLA Ops:
  0.1 1.4 %slice.643 = bf16[8,16,16,16]{3,2,1,0:T(8,128)(2,1)S(1)} slice(f32[8,16,16,128]{3,2,1,0:T(8,128)} %bitcast.213), slice={[0:8], [0:16], [0:16], [112:128]} | slice | bytes 131072 | tf_op jit(solution)/shard_map/slice | solution.py:157
  1.5 0.4 convert_element_type.52
  1.9 0.2 copy.11
  2.2 1.5 %convert_element_type.54 = bf16[8,4096]{1,0:T(8,128)(2,1)S(1)} reshape(bf16[2,2,2,8,8,8,8]{6,5,4,3,2,1,0:T(8,128)(2,1)S(1)} %bitcast.212) | data formatting | bytes 131072 | tf_op jit(solution)/shard_map/convert_element_type | solution.py:160
  3.7 0.1 convert_reduce_fusion.1
  3.8 0.2 convert_reduce_fusion
  4.0 0.2 convolution_convert_fusion.1
  4.1 0.7 %reshape.303.send_ref = bf16[8,16,512]{2,1,0:T(8,128)(2,1)} reshape(bf16[16,4096]{1,0:T(8,128)(2,1)S(1)} %convolution_convert_fusion.1) | data formatting | bytes 262144 | tf_op jit(solution)/shard_map/reshape | solution.py:176
  4.9 8.4 %shard_map.55 = bf16[8,16,512]{2,1,0:T(8,128)(2,1)} custom-call(bf16[8,16,512]{2,1,0:T(8,128)(2,1)} %reshape.303.send_ref), custom_call_target="tpu_custom_call" | custom-call | tf_op jit(solution)/shard_map/pallas_call | solution.py:115
  13.3 1.0 %reshape.304 = bf16[16,4096]{1,0:T(8,128)(2,1)S(1)} reshape(bf16[8,16,512]{2,1,0:T(8,128)(2,1)} %shard_map.55) | data formatting | bytes 262144 | tf_op jit(solution)/shard_map/reshape | solution.py:177
  14.3 0.2 reduce-window.8
  14.7 0.2 convolution_convert_fusion
  15.0 4.6 %fusion.8 = f32[4,8,512]{2,1,0:T(8,128)S(1)} fusion(bf16[4,4,8,512]{3,2,1,0:T(8,128)(2,1)S(1)} %bitcast.218, bf16[1,1,4,4,512,512]{5,4,3,2,1,0:T(8,128)(2,1)} %param.9), kind=kOutput, calls=%fused_computation.17 | convolution fusion | flops 67108864 | bytes 8585216 | tf_op jit(solution)/shard_map/jkcs,jkst->jct/dot_general | solution.py:192
  19.6 0.6 %reshape.306 = f32[2048,8]{1,0:T(8,128)S(1)} reshape(f32[4,8,512]{2,1,0:T(8,128)S(1)} %fusion.8) | data formatting | bytes 131072 | tf_op jit(solution)/shard_map/reshape | solution.py:202
  20.2 0.6 %fusion.83 = f32[2048,128]{1,0:T(8,128)S(1)} fusion(f32[2048,8]{1,0:T(8,128)S(1)} %reshape.306, s32[128]{0:T(128)S(1)} %get-tuple-element.48, s32[128]{0:T(128)S(1)} %get-tuple-element.49, pred[128]{0:T(512)(128)(4,1)S(1)} %compare_and_fusion), kind=kOutput, calls=%fused_computation.178 | convolution fusion | flops 25167872 | bytes 1115264 | tf_op jit(solution)/shard_map/dot_general | solution.py:203
  20.9 0.6 %copy-done.3 = s32[1,1,4]{2,1,0:T(1,128)S(1)} copy-done((s32[1,1,4]{2,1,0:T(1,128)S(1)}, s32[1,1,4]{2,1,0:T(1,128)}, u32[]{:S(2)}) %copy-start.3) | copy-done | bytes 40
  21.5 0.1 broadcast_select_fusion.3
  21.6 0.2 and_and_fusion
  22.2 1.0 %copy-done = f32[1,8,16,16,128]{4,3,2,1,0:T(8,128)S(1)} copy-done((f32[1,8,16,16,128]{4,3,2,1,0:T(8,128)S(1)}, f32[1,8,16,16,128]{4,3,2,1,0:T(8,128)}, u32[]{:S(2)}) %copy-start) | copy-done | bytes 1048600
  23.3 0.4 select_select_fusion
  23.6 0.1 fusion.91
  23.7 2.5 %collective-permute-start.2 = (bf16[8,16,1,128]{3,2,1,0:T(2,128)(2,1)S(1)}, bf16[8,16,1,128]{3,2,1,0:T(2,128)(2,1)S(1)}, u32[]{:S(2)}, u32[]{:S(2)}) collective-permute-start(bf16[8,16,1,128]{3,2,1,0:T(2,128)(2,1)S(1)} %get-tuple-element.31), channel_id=1, source_target_pairs={{0,1},{1,2},{2,3},{3,4},{4,5},{5,6},{6,7},{8,9},{9,10},{10,11},{11... | collective-permute-start | bytes 98312 | tf_op jit(solution)/shard_map/ppermute | solution.py:139
  26.2 4.9 %collective-permute-start.3 = (bf16[8,16,1,128]{3,2,1,0:T(2,128)(2,1)S(1)}, bf16[8,16,1,128]{3,2,1,0:T(2,128)(2,1)S(1)}, u32[]{:S(2)}, u32[]{:S(2)}) collective-permute-start(bf16[8,16,1,128]{3,2,1,0:T(2,128)(2,1)S(1)} %get-tuple-element.32), channel_id=1, source_target_pairs={{1,0},{2,1},{3,2},{4,3},{5,4},{6,5},{7,6},{9,8},{10,9},{11,10},{12... | collective-permute-start | bytes 98312 | tf_op jit(solution)/shard_map/ppermute | solution.py:140
  31.2 2.1 %collective-permute-start = (bf16[8,1,16,128]{3,2,1,0:T(8,128)(2,1)S(1)}, bf16[8,1,16,128]{3,2,1,0:T(8,128)(2,1)S(1)}, u32[]{:S(2)}, u32[]{:S(2)}) collective-permute-start(bf16[8,1,16,128]{3,2,1,0:T(8,128)(2,1)S(1)} %get-tuple-element.27), channel_id=1, source_target_pairs={{0,8},{8,16},{16,24},{24,32},{32,40},{40,48},{48,56},{56,0},{1,9},... | collective-permute-start | bytes 98312 | tf_op jit(solution)/shard_map/ppermute | solution.py:139
  33.2 3.7 %collective-permute-start.1 = (bf16[8,1,16,128]{3,2,1,0:T(8,128)(2,1)S(1)}, bf16[8,1,16,128]{3,2,1,0:T(8,128)(2,1)S(1)}, u32[]{:S(2)}, u32[]{:S(2)}) collective-permute-start(bf16[8,1,16,128]{3,2,1,0:T(8,128)(2,1)S(1)} %get-tuple-element.28), channel_id=1, source_target_pairs={{8,0},{16,8},{24,16},{32,24},{40,32},{48,40},{56,48},{0,56},{9,1},... | collective-permute-start | bytes 98312 | tf_op jit(solution)/shard_map/ppermute | solution.py:140
  37.0 0.3 fusion.92
  37.3 0.9 %pad_maximum_fusion = f32[8,16,16,130]{3,2,1,0:T(8,128)S(1)} fusion(f32[8,16,16,1]{3,2,1,0:T(8,128)S(1)} %get-tuple-element.34, f32[8,16,16,128]{3,2,1,0:T(8,128)S(1)} %select_select_fusion, f32[8,16,16,1]{3,2,1,0:T(8,128)S(1)} %get-tuple-element.33), kind=kLoop, calls=%fused_computation.7 | loop fusion | flops 532480 | bytes 2129920 | tf_op jit(solution)/shard_map/jit(_pad)/concatenate | solution.py:224
  38.3 0.3 multiply_reduce_fusion
  38.6 0.1 fusion.27
  38.7 0.1 fusion.25
  38.8 0.2 fusion.33
  38.9 0.2 add_dynamic-update-slice_fusion
  39.1 0.1 fusion.23
  39.2 0.1 fusion.21
  39.3 0.1 fusion.19
  39.5 0.2 fusion.35
  39.7 1.2 %fusion.3 = f32[8,16,16,129]{3,2,1,0:T(8,128)S(1)} fusion(f32[8,16,16,130]{3,2,1,0:T(8,128)S(1)} %fusion.35, f32[8,16,16,1]{3,2,1,0:T(8,128)S(1)} %get-tuple-element.34, f32[8,16,16,128]{3,2,1,0:T(8,128)S(1)} %select_select_fusion, f32[8,16,16,1]{3,2,1,0:T(8,128)S(1)} %get-tuple-element.33, f32[16,16,129]{2,1,0:T(8,128)S(1)} %fusion.19), kind=kLoop, calls=%fused_computation.6 | loop fusion | flops 1849344 | bytes 4367360 | tf_op jit(solution)/shard_map/sub | solution.py:58
  40.9 0.2 broadcast_select_fusion.1
  41.1 0.3 pad_maximum_fusion.1
  41.4 0.2 multiply_reduce_fusion.3
  41.6 0.1 fusion.51
  41.8 0.1 add_dynamic-update-slice_fusion.1
  42.3 0.1 multiply_reduce_fusion.6
  42.4 0.1 fusion.68
  42.8 0.1 fusion.53
  42.9 0.6 %fusion.6 = f32[8,16,17,128]{3,2,1,0:T(8,128)S(1)} fusion(f32[8,16,18,128]{3,2,1,0:T(8,128)S(1)} %fusion.53, f32[8,16,1,128]{3,2,1,0:T(1,128)S(1)} %get-tuple-element.30, f32[8,16,16,128]{3,2,1,0:T(8,128)S(1)} %select_select_fusion, f32[8,16,1,128]{3,2,1,0:T(1,128)S(1)} %get-tuple-element.29, f32[16,17,128]{2,1,0:T(8,128)S(1)} %fusion.37), kind=kLoop, calls=%fused_computation.12 | loop fusion | flops 1949696 | bytes 4661248 | tf_op jit(solution)/shard_map/sub | solution.py:58
  43.6 0.2 fusion.12
  43.8 1.5 %fusion.17 = f32[1,8,16,16,128]{4,3,2,1,0:T(8,128)} fusion(f32[8,16,16,128]{3,2,1,0:T(8,128)S(1)} %select_select_fusion, f32[8,16,16,129]{3,2,1,0:T(8,128)S(1)} %fusion.3, f32[8,16,17,128]{3,2,1,0:T(8,128)S(1)} %fusion.6, f32[8,17,16,128]{3,2,1,0:T(8,128)S(1)} %fusion.12, f32[]{:T(128)S(6)} %select_n.166), kind=kLoop, calls=%fused_computation.27 | loop fusion | flops 1835008 | bytes 8388612 | tf_op jit(solution)/shard_map/broadcast_in_dim | solution.py:227
  (52 shorter events, 1.6 us)
Async XLA Ops:
  1.9 1.8 %copy-start.1 = (s32[1,8,8]{2,1,0:T(8,128)S(1)}, s32[1,8,8]{2,1,0:T(8,128)}, u32[]{:S(2)}) copy-start(s32[1,8,8]{2,1,0:T(8,128)} %param.6) | copy-start | bytes 772
  2.2 12.5 %copy-start.2 = (s32[1,1,4,4]{3,2,1,0:T(4,128)S(1)}, s32[1,1,4,4]{3,2,1,0:T(4,128)}, u32[]{:S(2)}) copy-start(s32[1,1,4,4]{3,2,1,0:T(4,128)} %param.7) | copy-start | bytes 196
  20.8 0.7 %copy-start.3 = (s32[1,1,4]{2,1,0:T(1,128)S(1)}, s32[1,1,4]{2,1,0:T(1,128)}, u32[]{:S(2)}) copy-start(s32[1,1,4]{2,1,0:T(1,128)} %param.8) | copy-start | bytes 52
  22.0 1.2 %copy-start = (f32[1,8,16,16,128]{4,3,2,1,0:T(8,128)S(1)}, f32[1,8,16,16,128]{4,3,2,1,0:T(8,128)}, u32[]{:S(2)}) copy-start(f32[1,8,16,16,128]{4,3,2,1,0:T(8,128)} %param.5) | copy-start | bytes 3145732
  23.7 17.2 %collective-permute-start.2 = (bf16[8,16,1,128]{3,2,1,0:T(2,128)(2,1)S(1)}, bf16[8,16,1,128]{3,2,1,0:T(2,128)(2,1)S(1)}, u32[]{:S(2)}, u32[]{:S(2)}) collective-permute-start(bf16[8,16,1,128]{3,2,1,0:T(2,128)(2,1)S(1)} %get-tuple-element.31), channel_id=1, source_target_pairs={{0,1},{1,2},{2,3},{3,4},{4,5},{5,6},{6,7},{8,9},{9,10},{10,11},{11... | collective-permute-start | bytes 98312 | tf_op jit(solution)/shard_map/ppermute | solution.py:139
  26.2 14.7 %collective-permute-start.3 = (bf16[8,16,1,128]{3,2,1,0:T(2,128)(2,1)S(1)}, bf16[8,16,1,128]{3,2,1,0:T(2,128)(2,1)S(1)}, u32[]{:S(2)}, u32[]{:S(2)}) collective-permute-start(bf16[8,16,1,128]{3,2,1,0:T(2,128)(2,1)S(1)} %get-tuple-element.32), channel_id=1, source_target_pairs={{1,0},{2,1},{3,2},{4,3},{5,4},{6,5},{7,6},{9,8},{10,9},{11,10},{12... | collective-permute-start | bytes 98312 | tf_op jit(solution)/shard_map/ppermute | solution.py:140
  31.2 10.9 %collective-permute-start = (bf16[8,1,16,128]{3,2,1,0:T(8,128)(2,1)S(1)}, bf16[8,1,16,128]{3,2,1,0:T(8,128)(2,1)S(1)}, u32[]{:S(2)}, u32[]{:S(2)}) collective-permute-start(bf16[8,1,16,128]{3,2,1,0:T(8,128)(2,1)S(1)} %get-tuple-element.27), channel_id=1, source_target_pairs={{0,8},{8,16},{16,24},{24,32},{32,40},{40,48},{48,56},{56,0},{1,9},... | collective-permute-start | bytes 98312 | tf_op jit(solution)/shard_map/ppermute | solution.py:139
  33.2 8.9 %collective-permute-start.1 = (bf16[8,1,16,128]{3,2,1,0:T(8,128)(2,1)S(1)}, bf16[8,1,16,128]{3,2,1,0:T(8,128)(2,1)S(1)}, u32[]{:S(2)}, u32[]{:S(2)}) collective-permute-start(bf16[8,1,16,128]{3,2,1,0:T(8,128)(2,1)S(1)} %get-tuple-element.28), channel_id=1, source_target_pairs={{8,0},{16,8},{24,16},{32,24},{40,32},{48,40},{56,48},{0,56},{9,1},... | collective-permute-start | bytes 98312 | tf_op jit(solution)/shard_map/ppermute | solution.py:140
